TPU v7x, 32 devices: a whole 2x2x4 slice. The times are simulated.
32 devices in a mesh: groups: 2 (over y), seq: 4 (over z), head: 2 (over x), sub: 2 (over core).
Axes of the slice: x: 2, y: 2, z: 4, core: 2. Of those that a mesh axis runs over, the one named last changes fastest.
Arguments:
- x_raw: bfloat16 [16, 128, 8192], P(('groups', 'seq', 'sub'), 'head'), parts along dimension 0, may hold values from -6 to 6
- bc_raw: bfloat16 [16, 128, 2048], P(('groups', 'seq', 'sub'), 'head'), parts along dimension 0, may hold values from -6 to 6
- dt_raw: bfloat16 [16, 128, 128], P(('groups', 'seq', 'sub'), 'head'), parts along dimension 0, may hold values from -3 to 40
- conv_x_weight: float32 [4, 8192], P(None, 'head'), may hold values from -3 to 3
- conv_x_bias: float32 [8192], P('head'), may hold values from -2.5 to 2.5
- conv_bc_weight: float32 [4, 2048], P(None, 'head'), may hold values from -3 to 3
- conv_bc_bias: float32 [2048], P('head'), may hold values from -2.5 to 2.5
- stride_offset_per_head: float32 [128], P('head'), may hold values from -12 to 0
- a_log: float32 [128], P('head'), may hold values from -8 to 3
- skip_d: float32 [128], P('head'), may hold values from 0.5 to 1.5
- norm_gain: float32 [8192], P('head'), may hold values from 0.1 to 1.9
Outputs:
- mixed: bfloat16 [16, 128, 8192], P(('groups', 'seq', 'sub'), None, 'head'), parts along dimension 0
There are 2 independent parts, one for each index of `groups`. A program takes and returns all parts, laid end to end along the dimension named above; an argument that names none is the same for every part. Nothing has to cross between parts.
All inputs are finite; a program needn't handle non-finite values.
Results may differ from a plain program's by a relative error of at most 0.0061.
Values may be sent and summed in bfloat16 or wider, within the bound.
No kernel may reach another device: no remote copies, remote signals or barrier semaphores. Data moves between devices by JAX's collectives and lax.ppermute only.
A program may use at most 128 MiB of HBM per device.

v0:
```python
import functools

import jax
import jax.numpy as jnp
from jax import lax
from jax.experimental import pallas as pl
from jax.experimental.pallas import tpu as pltpu
from jax.sharding import PartitionSpec as P


STATE = 128
SPAN = 128
LANES = 128
EDGE = 8
EXTRA = 16
NORM_EPSILON = 1e-05
CHUNKS = 2
VMEM_LIMIT = 8 * 1024 * 1024


F32 = jnp.float32
BF16 = jnp.bfloat16


def silu(v):
    return v / (1.0 + jnp.exp(-v))


def widen_pair(table, head, head_dim, lanes):
    count = LANES // head_dim
    strip = jnp.broadcast_to(table[:, head : head + 1], (table.shape[0], LANES))
    for k in range(1, count):
        column = jnp.broadcast_to(table[:, head + k : head + k + 1], (table.shape[0], LANES))
        strip = jnp.where(lanes >= k * head_dim, column, strip)
    return strip


def lane_index(rows):
    return lax.broadcasted_iota(jnp.int32, (rows, LANES), 1)


def tables_kernel(heads, place, own_ref, *refs):
    *recv_refs, offset_ref, a_log_ref, tok_ref, head_ref, raw = refs
    position = place[0]
    rows = own_ref.shape[1]
    shards = len(recv_refs) + 1
    raw[pl.ds(pl.multiple_of(position * rows, rows), rows), :] = own_ref[0].astype(F32)
    for k, ref in enumerate(recv_refs):
        source = lax.rem(position + shards - 1 - k, shards)
        raw[pl.ds(pl.multiple_of(source * rows, rows), rows), :] = ref[...].astype(F32)
    logits = raw[...]
    if shards > 1:
        total = logits.shape[1]
        logits = pltpu.roll(logits, lax.rem(total - position * heads, total), axis=1)
    v = logits[:, :heads] + offset_ref[...]
    dt = jnp.maximum(v, 0.0) + jnp.log1p(jnp.exp(-jnp.abs(v)))
    decay = -jnp.exp(a_log_ref[...]) * dt
    span = decay.shape[0]
    lower = lax.broadcasted_iota(jnp.int32, (span, span), 0) >= lax.broadcasted_iota(
        jnp.int32, (span, span), 1
    )
    cum = jnp.dot(
        lower.astype(F32), decay, precision=lax.Precision.HIGHEST, preferred_element_type=F32
    )
    end = cum[span - 1 :, :]
    tok_ref[0] = cum
    tok_ref[1] = jnp.exp(end - cum) * dt
    tok_ref[2] = jnp.exp(cum)
    head_ref[0] = cum.T
    head_ref[1] = dt.T


def conv_tile(joined, rows, lanes, weight, bias):
    running = bias
    for tap in range(weight.shape[0]):
        start = EDGE - weight.shape[0] + 1 + tap
        running = running + weight[tap : tap + 1, :] * joined[pl.ds(start, rows), lanes]
    return silu(running)


def state_kernel(c, head_dim, groups, place, own_x, own_bc, *refs):
    shards = place.shape[0] - 1
    recv_refs, halos = refs[: shards - 1], refs[shards - 1 : 2 * shards - 1]
    wx_ref, bx_ref, wbc_ref, bbc_ref, tok = refs[2 * shards - 1 : 2 * shards + 4]
    xc_ref, bcc_ref, own_ref, own_d_ref, send_ref = refs[2 * shards + 4 : 2 * shards + 9]
    joined, scaled, full, full_d = refs[2 * shards + 9 :]
    position, sub = place[0], place[1]
    rows = own_x.shape[1]
    width, bc_width = xc_ref.shape[1], bcc_ref.shape[1]
    all_width, all_bc = wx_ref.shape[1], wbc_ref.shape[1]
    first_head = c * width // head_dim
    columns, bc_columns = slice(c * width, (c + 1) * width), slice(c * bc_width, (c + 1) * bc_width)
    wx, bx = wx_ref[:, columns], bx_ref[:, columns]
    wbc, bbc = wbc_ref[:, bc_columns], bbc_ref[:, bc_columns]
    span = SPAN
    edge = halos[0][...].astype(F32)
    for ref in halos[1:]:
        edge = edge + ref[...].astype(F32)
    edge_bc = edge[:, all_width + c * bc_width : all_width + (c + 1) * bc_width]
    edge = edge[:, columns]
    own_columns = pl.ds(pl.multiple_of(position * all_width + c * width, LANES), width)
    own_bc_columns = pl.ds(pl.multiple_of(position * all_bc + c * bc_width, LANES), bc_width)
    joined[:EDGE, :width] = edge
    joined[:EDGE, width:] = edge_bc
    at = pl.multiple_of(EDGE + position * rows, EDGE)
    joined[pl.ds(at, rows), :width] = own_x[0, :, own_columns].astype(F32)
    joined[pl.ds(at, rows), width:] = own_bc[0, :, own_bc_columns].astype(F32)
    for k, ref in enumerate(recv_refs):
        source = lax.rem(position + shards - 1 - k, shards)
        at = pl.multiple_of(EDGE + source * rows, EDGE)
        joined[pl.ds(at, rows), :] = ref[...].astype(F32)
    for j in range(bc_width // LANES):
        lanes = slice(j * LANES, (j + 1) * LANES)
        inner = slice(width + j * LANES, width + (j + 1) * LANES)
        bcc_ref[:, lanes] = conv_tile(joined, span, inner, wbc[:, lanes], bbc[:, lanes]).astype(BF16)
    to_end = tok[1]
    last = tok[2, span - EDGE :, :]
    lane = lane_index(span)
    lane_few = lane_index(EDGE)
    for j in range(width // LANES):
        lanes = slice(j * LANES, (j + 1) * LANES)
        xc = conv_tile(joined, span, lanes, wx[:, lanes], bx[:, lanes]).astype(BF16)
        xc_ref[:, lanes] = xc
        head = first_head + j * (LANES // head_dim)
        factor = widen_pair(to_end, head, head_dim, lane)
        scaled[:, lanes] = (factor * xc.astype(F32)).astype(BF16)
        full_d[:, lanes] = widen_pair(last, head, head_dim, lane_few)
    group_width = width // groups
    for g in range(groups):
        b_in = bcc_ref[:, g * 2 * STATE : g * 2 * STATE + STATE].astype(F32)
        lanes = slice(g * group_width, (g + 1) * group_width)
        full[:, lanes] = jnp.dot(b_in.T.astype(BF16), scaled[:, lanes], preferred_element_type=F32)
    half = width // 2
    mine = pl.ds(pl.multiple_of(sub * half, LANES), half)
    other = pl.ds(pl.multiple_of((1 - sub) * half, LANES), half)
    own_ref[...] = full[:, mine]
    own_d_ref[...] = full_d[EDGE - 1 :, mine]
    send_ref[:STATE, :] = full[:, other].astype(BF16)
    d = full_d[EDGE - 1 :, other]
    high = d.astype(BF16)
    middle = (d - high.astype(F32)).astype(BF16)
    low = (d - high.astype(F32) - middle.astype(F32)).astype(BF16)
    row = lax.broadcasted_iota(jnp.int32, (EXTRA, half), 0)
    parts = jnp.where(row == 0, high.astype(F32), 0.0)
    parts = jnp.where(row == 1, middle.astype(F32), parts)
    parts = jnp.where(row == 2, low.astype(F32), parts)
    send_ref[STATE:, :] = parts.astype(BF16)


def intra_kernel(first_head, head_dim, groups, place, xc_ref, bcc_ref, tok, heads_ref, skip_ref, y_ref):
    span, width = xc_ref.shape
    per_strip = LANES // head_dim
    lane = lane_index(span)
    group_width = width // groups
    causal = lax.broadcasted_iota(jnp.int32, (span, span), 0) >= lax.broadcasted_iota(
        jnp.int32, (span, span), 1
    )
    cum = tok[0]
    for g in range(groups):
        b_in = bcc_ref[:, g * 2 * STATE : g * 2 * STATE + STATE]
        c_out = bcc_ref[:, g * 2 * STATE + STATE : (g + 1) * 2 * STATE]
        inner = lax.dot_general(
            c_out, b_in, (((1,), (1,)), ((), ())), preferred_element_type=F32
        )
        inner = jnp.where(causal, inner, 0.0)
        for j in range(g * group_width // LANES, (g + 1) * group_width // LANES):
            lanes = slice(j * LANES, (j + 1) * LANES)
            xc = xc_ref[:, lanes]
            wide = xc.astype(F32)
            mixes, rights = [], []
            for k in range(per_strip):
                head = first_head + j * per_strip + k
                gap = cum[:, head : head + 1] - heads_ref[0, head : head + 1, :]
                weight = jnp.exp(jnp.minimum(gap, 0.0)) * heads_ref[1, head : head + 1, :]
                mixes.append((inner * weight).astype(BF16))
                own = (lane >= k * head_dim) & (lane < (k + 1) * head_dim)
                rights.append(jnp.where(own, wide, 0.0).astype(BF16))
            y = jnp.dot(
                jnp.concatenate(mixes, axis=1),
                jnp.concatenate(rights, axis=0),
                preferred_element_type=F32,
            )
            head = first_head + j * per_strip
            skip = widen_pair(skip_ref[...], head, head_dim, lane_index(1))
            y_ref[:, lanes] = y + skip * wide


def finish_kernel(c, head_dim, groups, place, y_ref, bcc_ref, tok, mine, other, gain_ref, *refs):
    out_ref, carried, scratch, normed, sems = refs[-5:]
    span, width = y_ref.shape
    first_head = c * width // head_dim
    gain = gain_ref[:, c * width : (c + 1) * width]
    copies = []
    half = width // 2
    sub = place[1]
    carried[:, pl.ds(pl.multiple_of(sub * half, LANES), half)] = mine[...]
    carried[:, pl.ds(pl.multiple_of((1 - sub) * half, LANES), half)] = other[...]
    lane = lane_index(span)
    group_width = width // groups
    decay = tok[2]
    for g in range(groups):
        c_out = bcc_ref[:, g * 2 * STATE + STATE : (g + 1) * 2 * STATE]
        lanes = slice(g * group_width, (g + 1) * group_width)
        scratch[...] = jnp.dot(c_out, carried[:, lanes], preferred_element_type=F32)
        squares = jnp.zeros((span, LANES), F32)
        for j in range(group_width // LANES):
            here = slice(j * LANES, (j + 1) * LANES)
            there = slice(g * group_width + j * LANES, g * group_width + (j + 1) * LANES)
            head = first_head + (g * group_width + j * LANES) // head_dim
            y = y_ref[:, there] + scratch[:, here] * widen_pair(decay, head, head_dim, lane)
            scratch[:, here] = y
            squares = squares + y * y
        mean = jnp.sum(squares, axis=1, keepdims=True) * (1.0 / group_width)
        factor = lax.rsqrt(mean + NORM_EPSILON)
        for j in range(group_width // LANES):
            here = slice(j * LANES, (j + 1) * LANES)
            there = slice(g * group_width + j * LANES, g * group_width + (j + 1) * LANES)
            normed[:, there] = (scratch[:, here] * factor * gain[:, there]).astype(BF16)
        target = slice(c * width + g * group_width, c * width + (g + 1) * group_width)
        copies.append(
            pltpu.make_async_copy(normed.at[:, lanes], out_ref.at[0, :, target], sems.at[g])
        )
        copies[-1].start()
    for copy in copies:
        copy.wait()


def pack_kernel(parts, place, *refs):
    sources, out, sems = refs[: len(parts)], refs[-2], refs[-1]
    copies = []
    column = 0
    for n, (source, (stride, offset, count)) in enumerate(zip(sources, parts)):
        start = pl.multiple_of(place[0] * stride + offset, LANES)
        copies.append(
            pltpu.make_async_copy(
                source.at[0, :, pl.ds(start, count)], out.at[:, pl.ds(column, count)], sems.at[n]
            )
        )
        column += count
    for copy in copies:
        copy.start()
    for copy in copies:
        copy.wait()


def on_device(
    x_raw,
    bc_raw,
    dt_raw,
    conv_x_weight,
    conv_x_bias,
    conv_bc_weight,
    conv_bc_bias,
    stride_offset_per_head,
    a_log,
    skip_d,
    norm_gain,
):
    shards = lax.axis_size("head")
    chips = lax.axis_size("seq")
    position = lax.axis_index("head")
    sub = lax.axis_index("sub")
    rows = x_raw.shape[1]
    width = conv_x_weight.shape[1]
    bc_width = conv_bc_weight.shape[1]
    heads = a_log.shape[0]
    head_dim = width // heads
    groups = bc_width // (2 * STATE)
    chunks = min(CHUNKS, groups)
    cw, cb, cg, ch = width // chunks, bc_width // chunks, groups // chunks, heads // chunks
    half = cw // 2
    place = jnp.stack([position, sub] + [position] * (shards - 1)).astype(jnp.int32)
    row = lambda a: a.reshape(1, a.shape[0])
    even = sub == 0
    anywhere = pl.BlockSpec(memory_space=pl.ANY)
    vmem = pl.BlockSpec(memory_space=pltpu.VMEM)

    def call(kernel, operands, outs, scratch=(), specs=None, out_specs=None, aliases={}):
        return pl.pallas_call(
            kernel,
            grid_spec=pltpu.PrefetchScalarGridSpec(
                num_scalar_prefetch=1,
                grid=(),
                in_specs=specs or [vmem] * (len(operands) - 1),
                out_specs=out_specs or [vmem] * len(outs),
                scratch_shapes=list(scratch),
            ),
            out_shape=list(outs),
            input_output_aliases=aliases,
            compiler_params=pltpu.CompilerParams(vmem_limit_bytes=VMEM_LIMIT),
        )(*operands)

    def shift(k):
        return [(i, (i + k) % shards) for i in range(shards)]

    def send_chunk(c):
        received = []
        for k in range(1, shards):
            target = lax.rem(position + k, shards).astype(jnp.int32).reshape(1)
            (packed,) = call(
                functools.partial(pack_kernel, ((width, c * cw, cw), (bc_width, c * cb, cb))),
                (target, x_raw, bc_raw),
                [pltpu.VMEM((rows, cw + cb), BF16)],
                [pltpu.SemaphoreType.DMA((2,))],
                specs=[pl.BlockSpec(memory_space=pltpu.HBM)] * 2,
            )
            received.append(lax.ppermute(packed, "head", shift(k)))
        return received

    recvs = [send_chunk(c) for c in range(chunks)]
    dt_recv = [lax.ppermute(dt_raw[0], "head", shift(k)) for k in range(1, shards)]

    following = lambda k: [
        ((b * shards + shards - 1) * 2 + s, ((b + s) * shards + k) * 2 + 1 - s)
        for b in range(chips)
        for s in range(2)
        if b + s < chips
    ]
    halos = []
    for k in range(shards):
        tail = jnp.concatenate(
            [
                x_raw[0, rows - EDGE :, k * width : (k + 1) * width],
                bc_raw[0, rows - EDGE :, k * bc_width : (k + 1) * bc_width],
            ],
            axis=1,
        )
        halos.append(lax.ppermute(tail, ("seq", "head", "sub"), following(k)))

    tok, by_head = call(
        functools.partial(tables_kernel, heads),
        (place, dt_raw, *dt_recv, row(stride_offset_per_head), row(a_log)),
        [pltpu.VMEM((3, SPAN, heads), F32), pltpu.VMEM((2, heads, SPAN), F32)],
        [pltpu.VMEM((SPAN, dt_raw.shape[2]), F32)],
    )

    weights = (conv_x_weight, row(conv_x_bias), conv_bc_weight, row(conv_bc_bias))

    def state(c):
        return call(
            functools.partial(state_kernel, c, head_dim, cg),
            (place, x_raw, bc_raw, *recvs[c], *halos, *weights, tok),
            [
                pltpu.VMEM((SPAN, cw), BF16),
                pltpu.VMEM((SPAN, cb), BF16),
                pltpu.VMEM((STATE, half), F32),
                pltpu.VMEM((1, half), F32),
                pltpu.VMEM((STATE + EXTRA, half), BF16),
            ],
            [
                pltpu.VMEM((EDGE + SPAN, cw + cb), F32),
                pltpu.VMEM((SPAN, cw), BF16),
                pltpu.VMEM((STATE, cw), F32),
                pltpu.VMEM((EDGE, cw), F32),
            ],
        )

    def chain(own, own_d, send):
        got = lax.ppermute(send, "sub", [(0, 1), (1, 0)])
        other = got[:STATE].astype(F32)
        other_d = jnp.sum(got[STATE : STATE + 3].astype(F32), axis=0, keepdims=True)
        state_even = jnp.where(even, own, other)
        state_odd = jnp.where(even, other, own)
        decay_even = jnp.where(even, own_d, other_d)
        decay_odd = jnp.where(even, other_d, own_d)
        total = decay_odd * state_even + state_odd
        decay = decay_even * decay_odd
        running = total
        entry = jnp.zeros((STATE, half), F32)
        for step in range(chips - 1):
            arrived = lax.ppermute(running.astype(BF16), "seq", [(step, step + 1)])
            arrived = arrived.astype(F32)
            entry = entry + arrived
            running = decay * arrived + total
        later = decay_even * entry + state_even
        mine = jnp.where(even, entry, later).astype(BF16)
        theirs = jnp.where(even, later, entry).astype(BF16)
        return mine, lax.ppermute(theirs, "sub", [(0, 1), (1, 0)])

    def intra(c, xc, bcc):
        return call(
            functools.partial(intra_kernel, c * ch, head_dim, cg),
            (place, xc, bcc, tok, by_head, row(skip_d)),
            [pltpu.VMEM((SPAN, cw), F32)],
        )[0]

    def finish(c, y, bcc, mine, theirs, out):
        before = [] if out is None else [out]
        return call(
            functools.partial(finish_kernel, c, head_dim, cg),
            (place, y, bcc, tok, mine, theirs, row(norm_gain), *before),
            [jax.ShapeDtypeStruct((1, SPAN, width), BF16)],
            [
                pltpu.VMEM((STATE, cw), BF16),
                pltpu.VMEM((SPAN, cw // cg), F32),
                pltpu.VMEM((SPAN, cw), BF16),
                pltpu.SemaphoreType.DMA((cg,)),
            ],
            specs=[vmem] * 6 + [anywhere] * len(before),
            out_specs=[anywhere],
            aliases={7: 0} if before else {},
        )[0]

    parts = []
    for c in range(chunks):
        xc, bcc, own, own_d, send = state(c)
        mine, theirs = chain(own, own_d, send)
        parts.append((intra(c, xc, bcc), bcc, mine, theirs))
    out = None
    for c in range(chunks):
        out = finish(c, *parts[c], out)
    return out


def solution(mesh):
    placed = (
        P(("groups", "seq", "sub"), "head", None),
        P(("groups", "seq", "sub"), "head", None),
        P(("groups", "seq", "sub"), "head", None),
        P(None, "head"),
        P("head"),
        P(None, "head"),
        P("head"),
        P("head"),
        P("head"),
        P("head"),
        P("head"),
    )
    return jax.shard_map(
        on_device,
        mesh=mesh,
        in_specs=placed,
        out_specs=P(("groups", "seq", "sub"), None, "head"),
        check_vma=False,
    )
```

profile of v0, /device:TPU:25, one launch (start us, length us, event | category | flops | bytes accessed | tf_op | source)
XLA Modules:
  0.0 68.7 jit_solution(2421971100935651718)
XLA Ops:
  0.0 1.2 %copy-done = bf16[1,64,8192]{2,1,0:T(8,128)(2,1)S(1)} copy-done((bf16[1,64,8192]{2,1,0:T(8,128)(2,1)S(1)}, bf16[1,64,8192]{2,1,0:T(8,128)(2,1)}, u32[]{:S(2)}) %copy-start) | copy-done | bytes 1048600
  1.2 0.9 %copy-done.2 = bf16[1,64,2048]{2,1,0:T(8,128)(2,1)S(1)} copy-done((bf16[1,64,2048]{2,1,0:T(8,128)(2,1)S(1)}, bf16[1,64,2048]{2,1,0:T(8,128)(2,1)}, u32[]{:S(2)}) %copy-start.2) | copy-done | bytes 262168
  2.2 0.0 copy-start.3
  2.2 1.3 %collective-permute-start.9 = (bf16[64,2560]{1,0:T(8,128)(2,1)S(1)}, bf16[64,2560]{1,0:T(8,128)(2,1)S(1)}, u32[]{:S(2)}, u32[]{:S(2)}) collective-permute-start(bf16[64,2560]{1,0:T(8,128)(2,1)S(1)} %shard_map.113), channel_id=1, source_target_pairs={{0,2},{2,0},{1,3},{3,1},{4,6},{6,4},{5,7},{7,5},{8,10},{10,8},{9,1... | collective-permute-start | bytes 983048 | tf_op jit(solution)/shard_map/ppermute | solution.py:307
  3.5 0.6 collective-permute-start.3
  4.2 1.3 %collective-permute-start.1 = (bf16[8,5120]{1,0:T(8,128)(2,1)S(1)}, bf16[8,5120]{1,0:T(8,128)(2,1)S(1)}, u32[]{:S(2)}, u32[]{:S(2)}) collective-permute-start(bf16[8,5120]{1,0:T(8,128)(2,1)S(1)} %pad_maximum_fusion), channel_id=1, source_target_pairs={{2,1},{3,4},{6,5},{7,8},{10,9},{11,12},{14,13},{18,17},{19,20},{22... | collective-permute-start | bytes 245768 | tf_op jit(solution)/shard_map/ppermute | solution.py:328
  5.5 0.7 collective-permute-start.2
  6.1 0.8 %shard_map.109 = bf16[64,2560]{1,0:T(8,128)(2,1)} custom-call(s32[1]{0:T(128)} %bitcast.2.place, bf16[1,64,8192]{2,1,0:T(8,128)(2,1)S(1)} %copy-done.1, bf16[1,64,2048]{2,1,0:T(8,128)(2,1)S(1)} %copy-done.3), custom_call_target="tpu_custom_call" | custom-call | tf_op jit(solution)/shard_map/pallas_call | solution.py:279
  6.9 1.0 %collective-permute-start = (bf16[64,2560]{1,0:T(8,128)(2,1)}, bf16[64,2560]{1,0:T(8,128)(2,1)S(1)}, u32[]{:S(2)}, u32[]{:S(2)}) collective-permute-start(bf16[64,2560]{1,0:T(8,128)(2,1)} %shard_map.109), channel_id=1, source_target_pairs={{0,2},{2,0},{1,3},{3,1},{4,6},{6,4},{5,7},{7,5},{8,10},{10,8},{9,1... | collective-permute-start | bytes 983048 | tf_op jit(solution)/shard_map/ppermute | solution.py:307
  7.9 0.1 pad_add_fusion.place
  8.0 4.2 %collective-permute-done.3.refs_0_ = bf16[64,128]{1,0:T(8,128)(2,1)S(1)} collective-permute-done((bf16[64,128]{1,0:T(8,128)(2,1)S(1)}, bf16[64,128]{1,0:T(8,128)(2,1)S(1)}, u32[]{:S(2)}, u32[]{:S(2)}) %collective-permute-start.3) | collective-permute-done | bytes 16416 | tf_op jit(solution)/shard_map/ppermute | solution.py:311
  12.1 0.7 copy-done.14
  12.8 0.0 copy-done.15
  12.8 0.9 %shard_map.110 = (f32[3,128,64]{2,1,0:T(8,128)S(1)}, f32[2,64,128]{2,1,0:T(8,128)S(1)}) custom-call(s32[3]{0:T(128)S(1)} %pad_add_fusion.place, bf16[1,64,128]{2,1,0:T(8,128)(2,1)S(1)} %copy-done.12, bf16[64,128]{1,0:T(8,128)(2,1)S(1)} %collective-permute-done.3.refs_0_, f32[1,64]{1,0:T(1,128)S(1)} %bitcast.35, f32[1,64]{1,0:T(1,128)S(1)} %bitcast.36), custom_call_target="tpu_custom_call" | custom-call | tf_op jit(solution)/shard_map/pallas_call | solution.py:279
  13.7 0.6 copy-done.6
  14.4 1.5 %collective-permute-done.1.refs_1_ = bf16[8,5120]{1,0:T(8,128)(2,1)S(1)} collective-permute-done((bf16[8,5120]{1,0:T(8,128)(2,1)S(1)}, bf16[8,5120]{1,0:T(8,128)(2,1)S(1)}, u32[]{:S(2)}, u32[]{:S(2)}) %collective-permute-start.1) | collective-permute-done | bytes 81952 | tf_op jit(solution)/shard_map/ppermute | solution.py:328
  15.9 0.0 copy-start.4
  15.9 0.8 %copy-done.4 = f32[4,4096]{1,0:T(4,128)S(1)} copy-done((f32[4,4096]{1,0:T(4,128)S(1)}, f32[4,4096]{1,0:T(4,128)}, u32[]{:S(2)}) %copy-start.4) | copy-done | bytes 65560
  16.7 3.3 %shard_map.114 = (bf16[128,2048]{1,0:T(8,128)(2,1)S(1)}, bf16[128,512]{1,0:T(8,128)(2,1)S(1)}, f32[128,1024]{1,0:T(8,128)S(1)}, f32[1,1024]{1,0:T(1,128)S(1)}, bf16[144,1024]{1,0:T(8,128)(2,1)}) custom-call(s32[3]{0:T(128)S(1)} %pad_add_fusion.place, bf16[1,64,8192]{2,1,0:T(8,128)(2,1)S(1)} %copy-done.1, bf16[1,64,2048]{2,1,0:T(8,128)(2,1)S(1)} %copy-done.3, ...), custom_call_target="tpu_custom_call" | custom-call | tf_op jit(solution)/shard_map/pallas_call | solution.py:279
  20.1 1.8 %collective-permute-start.10 = (bf16[144,1024]{1,0:T(8,128)(2,1)}, bf16[144,1024]{1,0:T(8,128)(2,1)}, u32[]{:S(2)}, u32[]{:S(2)}) collective-permute-start(bf16[144,1024]{1,0:T(8,128)(2,1)} %get-tuple-element.26), channel_id=1, source_target_pairs={{0,1},{1,0},{2,3},{3,2},{4,5},{5,4},{6,7},{7,6},{8,9},{9,8},{10,11... | collective-permute-start | bytes 884744 | tf_op jit(solution)/shard_map/ppermute | solution.py:359
  21.9 0.8 %copy-done.5 = f32[4,4096]{1,0:T(4,128)S(1)} copy-done((f32[4,4096]{1,0:T(4,128)S(1)}, f32[4,4096]{1,0:T(4,128)}, u32[]{:S(2)}) %copy-start.5) | copy-done | bytes 65560
  22.7 2.6 %shard_map.111 = (bf16[128,2048]{1,0:T(8,128)(2,1)S(1)}, bf16[128,512]{1,0:T(8,128)(2,1)S(1)}, f32[128,1024]{1,0:T(8,128)S(1)}, f32[1,1024]{1,0:T(1,128)S(1)}, bf16[144,1024]{1,0:T(8,128)(2,1)S(1)}) custom-call(s32[3]{0:T(128)S(1)} %pad_add_fusion.place, bf16[1,64,8192]{2,1,0:T(8,128)(2,1)S(1)} %copy-done.1, bf16[1,64,2048]{2,1,0:T(8,128)(2,1)S(1)} %copy-done.3, ...), custom_call_target="tpu_custom_call" | custom-call | tf_op jit(solution)/shard_map/pallas_call | solution.py:279
  25.4 0.1 collective-permute-start.4
  25.5 0.7 %convert_reduce_fusion = f32[1024]{0:T(1024)S(1)} fusion(bf16[144,1024]{1,0:T(8,128)(2,1)} %collective-permute-done.10), kind=kLoop, calls=%fused_computation.32 | loop fusion | flops 5120 | bytes 10240 | tf_op jit(solution)/shard_map/reduce_sum | solution.py:361
  26.2 1.1 %fusion.12 = bf16[128,1024]{1,0:T(8,128)(2,1)S(1)} fusion(f32[128,1024]{1,0:T(8,128)S(1)} %get-tuple-element.28, bf16[144,1024]{1,0:T(8,128)(2,1)} %collective-permute-done.10, pred[]{:T(512)S(6)} %eq.3, f32[1024]{0:T(1024)S(1)} %bitcast.37), kind=kLoop, calls=%fused_computation.41 | loop fusion | flops 786432 | bytes 1052673 | tf_op jit(solution)/shard_map/convert_element_type | solution.py:371
  27.3 0.7 collective-permute-start.11
  28.0 0.1 fusion.13
  28.1 0.7 collective-permute-start.5
  28.8 1.1 %fusion.8 = bf16[128,1024]{1,0:T(8,128)(2,1)S(1)} fusion(bf16[128,1024]{1,0:T(8,128)(2,1)S(1)} %collective-permute-done.11, f32[1024]{0:T(1024)S(1)} %bitcast.43, f32[128,1024]{1,0:T(8,128)S(1)} %get-tuple-element.28, bf16[144,1024]{1,0:T(8,128)(2,1)} %collective-permute-done.10, pred[]{:T(512)S(6)} %eq.3, f32[1024]{0:T(1024)S(1)} %bitcast.38), kind=kLoop, calls=%fused_computation.18 | loop fusion | flops 1179648 | bytes 1318913 | tf_op jit(solution)/shard_map/convert_element_type | solution.py:371
  29.9 0.7 collective-permute-start.12
  30.6 0.2 fusion.2
  30.8 0.7 collective-permute-start.6
  31.5 1.1 %fusion.11 = bf16[128,1024]{1,0:T(8,128)(2,1)S(1)} fusion(bf16[128,1024]{1,0:T(8,128)(2,1)S(1)} %collective-permute-done.12, f32[1024]{0:T(1024)S(1)} %bitcast.44, f32[128,1024]{1,0:T(8,128)S(1)} %get-tuple-element.28, bf16[144,1024]{1,0:T(8,128)(2,1)} %collective-permute-done.10, pred[]{:T(512)S(6)} %eq.3, f32[1024]{0:T(1024)S(1)} %bitcast.39), kind=kLoop, calls=%fused_computation.21 | loop fusion | flops 1179648 | bytes 1318913 | tf_op jit(solution)/shard_map/convert_element_type | solution.py:371
  32.6 1.3 %collective-permute-start.13 = (bf16[128,1024]{1,0:T(8,128)(2,1)S(1)}, bf16[128,1024]{1,0:T(8,128)(2,1)S(1)}, u32[]{:S(2)}, u32[]{:S(2)}) collective-permute-start(bf16[128,1024]{1,0:T(8,128)(2,1)S(1)} %fusion.11), channel_id=1, source_target_pairs={{8,12},{9,13},{10,14},{11,15},{24,28},{25,29},{26,30},{27,31}} | collective-permute-start | bytes 786440 | tf_op jit(solution)/shard_map/ppermute | solution.py:371
  33.9 0.2 fusion.5
  34.1 1.3 %collective-permute-start.7 = (bf16[128,1024]{1,0:T(8,128)(2,1)S(1)}, bf16[128,1024]{1,0:T(8,128)(2,1)S(1)}, u32[]{:S(2)}, u32[]{:S(2)}) collective-permute-start(bf16[128,1024]{1,0:T(8,128)(2,1)S(1)} %fusion.5), channel_id=1, source_target_pairs={{8,12},{9,13},{10,14},{11,15},{24,28},{25,29},{26,30},{27,31}} | collective-permute-start | bytes 786440 | tf_op jit(solution)/shard_map/ppermute | solution.py:371
  35.4 15.5 %collective-permute-done.13 = bf16[128,1024]{1,0:T(8,128)(2,1)S(1)} collective-permute-done((bf16[128,1024]{1,0:T(8,128)(2,1)S(1)}, bf16[128,1024]{1,0:T(8,128)(2,1)S(1)}, u32[]{:S(2)}, u32[]{:S(2)}) %collective-permute-start.13) | collective-permute-done | bytes 262176 | tf_op jit(solution)/shard_map/ppermute | solution.py:371
  50.9 1.2 %select_convert_fusion = (bf16[128,1024]{1,0:T(8,128)(2,1)S(1)}, bf16[128,1024]{1,0:T(8,128)(2,1)S(1)}) fusion(bf16[128,1024]{1,0:T(8,128)(2,1)S(1)} %collective-permute-done.13, bf16[128,1024]{1,0:T(8,128)(2,1)S(1)} %collective-permute-done.12, bf16[128,1024]{1,0:T(8,128)(2,1)S(1)} %collective-permute-done.11, f32[1024]{0:T(1024)S(1)} %bitcast.48, ...), kind=kLoop, calls=%fused_computation.22 | loop fusion | flops 1703936 | bytes 2101249 | tf_op jit(solution)/shard_map/convert_element_type | solution.py:377
  52.1 4.4 %collective-permute-start.14 = (bf16[128,1024]{1,0:T(8,128)(2,1)S(1)}, bf16[128,1024]{1,0:T(8,128)(2,1)S(1)}, u32[]{:S(2)}, u32[]{:S(2)}) collective-permute-start(bf16[128,1024]{1,0:T(8,128)(2,1)S(1)} %get-tuple-element.35), channel_id=1, source_target_pairs={{0,1},{1,0},{2,3},{3,2},{4,5},{5,4},{6,7},{7,6},{8,9},{9,8},{10,11... | collective-permute-start | bytes 786440 | tf_op jit(solution)/shard_map/ppermute | solution.py:378
  56.5 2.5 %collective-permute-done.7 = bf16[128,1024]{1,0:T(8,128)(2,1)S(1)} collective-permute-done((bf16[128,1024]{1,0:T(8,128)(2,1)S(1)}, bf16[128,1024]{1,0:T(8,128)(2,1)S(1)}, u32[]{:S(2)}, u32[]{:S(2)}) %collective-permute-start.7) | collective-permute-done | bytes 262176 | tf_op jit(solution)/shard_map/ppermute | solution.py:371
  58.9 0.2 select_convert_fusion.2
  59.2 1.4 %collective-permute-start.8 = (bf16[128,1024]{1,0:T(8,128)(2,1)S(1)}, bf16[128,1024]{1,0:T(8,128)(2,1)S(1)}, u32[]{:S(2)}, u32[]{:S(2)}) collective-permute-start(bf16[128,1024]{1,0:T(8,128)(2,1)S(1)} %get-tuple-element.37), channel_id=1, source_target_pairs={{0,1},{1,0},{2,3},{3,2},{4,5},{5,4},{6,7},{7,6},{8,9},{9,8},{10,11... | collective-permute-start | bytes 786440 | tf_op jit(solution)/shard_map/ppermute | solution.py:378
  60.6 0.7 copy-done.13
  61.2 1.5 %shard_map.115.y_ref = f32[128,2048]{1,0:T(8,128)S(1)} custom-call(s32[3]{0:T(128)S(1)} %pad_add_fusion.place, bf16[128,2048]{1,0:T(8,128)(2,1)S(1)} %get-tuple-element.24.xc_ref, bf16[128,512]{1,0:T(8,128)(2,1)S(1)} %get-tuple-element.25.bcc_ref, f32[3,128,64]{2,1,0:T(8,128)S(1)} %get-tuple-element.17.refs_7_.tok, f32[2,64,128]{2,1,0:T(8,128)S(1)} %copy-done.7, ...), custom_call_target="tpu_custom_call" | custom-call | tf_op jit(solution)/shard_map/pallas_call | solution.py:279
  62.7 0.0 copy-start.10
  62.7 1.5 %shard_map.112.y_ref = f32[128,2048]{1,0:T(8,128)S(1)} custom-call(s32[3]{0:T(128)S(1)} %pad_add_fusion.place, bf16[128,2048]{1,0:T(8,128)(2,1)S(1)} %get-tuple-element.18.xc_ref, bf16[128,512]{1,0:T(8,128)(2,1)S(1)} %get-tuple-element.19.bcc_ref, f32[3,128,64]{2,1,0:T(8,128)S(1)} %get-tuple-element.17.refs_7_.tok, f32[2,64,128]{2,1,0:T(8,128)S(1)} %copy-done.7, ...), custom_call_target="tpu_custom_call" | custom-call | tf_op jit(solution)/shard_map/pallas_call | solution.py:279
  64.2 2.2 %shard_map.116.refs_0_ = bf16[1,128,4096]{2,1,0:T(8,128)(2,1)} custom-call(s32[3]{0:T(128)S(1)} %pad_add_fusion.place, f32[128,2048]{1,0:T(8,128)S(1)} %shard_map.115.y_ref, bf16[128,512]{1,0:T(8,128)(2,1)S(1)} %get-tuple-element.25.bcc_ref, f32[3,128,64]{2,1,0:T(8,128)S(1)} %get-tuple-element.17.refs_7_.tok, bf16[128,1024]{1,0:T(8,128)(2,1)S(1)} %get-tuple-element.36.mine, ...), custom_call_target="tpu_custom_call" | custom-call | tf_op jit(solution)/shard_map/pallas_call | solution.py:279
  66.4 2.2 %shard_map.117 = bf16[1,128,4096]{2,1,0:T(8,128)(2,1)} custom-call(s32[3]{0:T(128)S(1)} %pad_add_fusion.place, f32[128,2048]{1,0:T(8,128)S(1)} %shard_map.112.y_ref, bf16[128,512]{1,0:T(8,128)(2,1)S(1)} %get-tuple-element.19.bcc_ref, f32[3,128,64]{2,1,0:T(8,128)S(1)} %get-tuple-element.17.refs_7_.tok, ...), custom_call_target="tpu_custom_call", output_to_operand_aliasing={{}: (7, {})} | custom-call | tf_op jit(solution)/shard_map/pallas_call | solution.py:279
  (40 shorter events, 0.2 us)
Async XLA Ops:
  0.0 1.2 %copy-start = (bf16[1,64,8192]{2,1,0:T(8,128)(2,1)S(1)}, bf16[1,64,8192]{2,1,0:T(8,128)(2,1)}, u32[]{:S(2)}) copy-start(bf16[1,64,8192]{2,1,0:T(8,128)(2,1)} %own_x.3) | copy-start | bytes 3145732
  1.2 0.9 %copy-start.2 = (bf16[1,64,2048]{2,1,0:T(8,128)(2,1)S(1)}, bf16[1,64,2048]{2,1,0:T(8,128)(2,1)}, u32[]{:S(2)}) copy-start(bf16[1,64,2048]{2,1,0:T(8,128)(2,1)} %own_bc.3) | copy-start | bytes 786436
  2.2 1.4 %copy-start.12 = (bf16[1,64,128]{2,1,0:T(8,128)(2,1)S(1)}, bf16[1,64,128]{2,1,0:T(8,128)(2,1)}, u32[]{:S(2)}) copy-start(bf16[1,64,128]{2,1,0:T(8,128)(2,1)} %own_ref.1) | copy-start | bytes 49156
  2.2 1.9 %copy-start.1 = (bf16[1,64,8192]{2,1,0:T(8,128)(2,1)S(1)}, bf16[1,64,8192]{2,1,0:T(8,128)(2,1)}, u32[]{:S(2)}) copy-start(bf16[1,64,8192]{2,1,0:T(8,128)(2,1)} %own_x.3) | copy-start | bytes 3145732
  2.2 1.9 %copy-start.3 = (bf16[1,64,2048]{2,1,0:T(8,128)(2,1)S(1)}, bf16[1,64,2048]{2,1,0:T(8,128)(2,1)}, u32[]{:S(2)}) copy-start(bf16[1,64,2048]{2,1,0:T(8,128)(2,1)} %own_bc.3) | copy-start | bytes 786436
  2.2 13.6 %collective-permute-start.9 = (bf16[64,2560]{1,0:T(8,128)(2,1)S(1)}, bf16[64,2560]{1,0:T(8,128)(2,1)S(1)}, u32[]{:S(2)}, u32[]{:S(2)}) collective-permute-start(bf16[64,2560]{1,0:T(8,128)(2,1)S(1)} %shard_map.113), channel_id=1, source_target_pairs={{0,2},{2,0},{1,3},{3,1},{4,6},{6,4},{5,7},{7,5},{8,10},{10,8},{9,1... | collective-permute-start | bytes 983048 | tf_op jit(solution)/shard_map/ppermute | solution.py:307
  3.5 8.6 %collective-permute-start.3 = (bf16[64,128]{1,0:T(8,128)(2,1)S(1)}, bf16[64,128]{1,0:T(8,128)(2,1)S(1)}, u32[]{:S(2)}, u32[]{:S(2)}) collective-permute-start(bf16[64,128]{1,0:T(8,128)(2,1)S(1)} %bitcast.32), channel_id=1, source_target_pairs={{0,2},{2,0},{1,3},{3,1},{4,6},{6,4},{5,7},{7,5},{8,10},{10,8},{9,1... | collective-permute-start | bytes 49160 | tf_op jit(solution)/shard_map/ppermute | solution.py:311
  4.2 11.7 %collective-permute-start.1 = (bf16[8,5120]{1,0:T(8,128)(2,1)S(1)}, bf16[8,5120]{1,0:T(8,128)(2,1)S(1)}, u32[]{:S(2)}, u32[]{:S(2)}) collective-permute-start(bf16[8,5120]{1,0:T(8,128)(2,1)S(1)} %pad_maximum_fusion), channel_id=1, source_target_pairs={{2,1},{3,4},{6,5},{7,8},{10,9},{11,12},{14,13},{18,17},{19,20},{22... | collective-permute-start | bytes 245768 | tf_op jit(solution)/shard_map/ppermute | solution.py:328
  5.5 10.4 %collective-permute-start.2 = (bf16[8,5120]{1,0:T(8,128)(2,1)S(1)}, bf16[8,5120]{1,0:T(8,128)(2,1)S(1)}, u32[]{:S(2)}, u32[]{:S(2)}) collective-permute-start(bf16[8,5120]{1,0:T(8,128)(2,1)S(1)} %pad_maximum_fusion.1), channel_id=1, source_target_pairs={{2,3},{3,6},{6,7},{7,10},{10,11},{11,14},{14,15},{18,19},{19,22},{... | collective-permute-start | bytes 245768 | tf_op jit(solution)/shard_map/ppermute | solution.py:328
  6.9 15.0 %collective-permute-start = (bf16[64,2560]{1,0:T(8,128)(2,1)}, bf16[64,2560]{1,0:T(8,128)(2,1)S(1)}, u32[]{:S(2)}, u32[]{:S(2)}) collective-permute-start(bf16[64,2560]{1,0:T(8,128)(2,1)} %shard_map.109), channel_id=1, source_target_pairs={{0,2},{2,0},{1,3},{3,1},{4,6},{6,4},{5,7},{7,5},{8,10},{10,8},{9,1... | collective-permute-start | bytes 983048 | tf_op jit(solution)/shard_map/ppermute | solution.py:307
  12.1 0.7 copy-start.14
  12.1 0.7 copy-start.15
  12.8 3.1 %copy-start.8 = (f32[4096]{0:T(1024)S(1)}, f32[4096]{0:T(1024)}, u32[]{:S(2)}) copy-start(f32[4096]{0:T(1024)} %param.15) | copy-start | bytes 49156
  12.8 3.1 %copy-start.9 = (f32[4,1024]{1,0:T(4,128)S(1)}, f32[4,1024]{1,0:T(4,128)}, u32[]{:S(2)}) copy-start(f32[4,1024]{1,0:T(4,128)} %refs_5_.3) | copy-start | bytes 49156
  13.7 0.6 copy-start.6
  14.4 1.5 %copy-start.11 = (f32[1024]{0:T(1024)S(1)}, f32[1024]{0:T(1024)}, u32[]{:S(2)}) copy-start(f32[1024]{0:T(1024)} %param.17) | copy-start | bytes 12292
  15.9 0.8 %copy-start.4 = (f32[4,4096]{1,0:T(4,128)S(1)}, f32[4,4096]{1,0:T(4,128)}, u32[]{:S(2)}) copy-start(f32[4,4096]{1,0:T(4,128)} %refs_3_.3) | copy-start | bytes 196612
  20.1 5.4 %collective-permute-start.10 = (bf16[144,1024]{1,0:T(8,128)(2,1)}, bf16[144,1024]{1,0:T(8,128)(2,1)}, u32[]{:S(2)}, u32[]{:S(2)}) collective-permute-start(bf16[144,1024]{1,0:T(8,128)(2,1)} %get-tuple-element.26), channel_id=1, source_target_pairs={{0,1},{1,0},{2,3},{3,2},{4,5},{5,4},{6,7},{7,6},{8,9},{9,8},{10,11... | collective-permute-start | bytes 884744 | tf_op jit(solution)/shard_map/ppermute | solution.py:359
  21.9 0.8 %copy-start.5 = (f32[4,4096]{1,0:T(4,128)S(1)}, f32[4,4096]{1,0:T(4,128)}, u32[]{:S(2)}) copy-start(f32[4,4096]{1,0:T(4,128)} %refs_3_.3) | copy-start | bytes 196612
  25.4 2.6 %collective-permute-start.4 = (bf16[144,1024]{1,0:T(8,128)(2,1)S(1)}, bf16[144,1024]{1,0:T(8,128)(2,1)S(1)}, u32[]{:S(2)}, u32[]{:S(2)}) collective-permute-start(bf16[144,1024]{1,0:T(8,128)(2,1)S(1)} %get-tuple-element.21), channel_id=1, source_target_pairs={{0,1},{1,0},{2,3},{3,2},{4,5},{5,4},{6,7},{7,6},{8,9},{9,8},{10,11... | collective-permute-start | bytes 884744 | tf_op jit(solution)/shard_map/ppermute | solution.py:359
  27.3 1.5 %collective-permute-start.11 = (bf16[128,1024]{1,0:T(8,128)(2,1)S(1)}, bf16[128,1024]{1,0:T(8,128)(2,1)S(1)}, u32[]{:S(2)}, u32[]{:S(2)}) collective-permute-start(bf16[128,1024]{1,0:T(8,128)(2,1)S(1)} %fusion.12), channel_id=1, source_target_pairs={{0,4},{1,5},{2,6},{3,7},{16,20},{17,21},{18,22},{19,23}} | collective-permute-start | bytes 786440 | tf_op jit(solution)/shard_map/ppermute | solution.py:371
  28.1 2.5 %collective-permute-start.5 = (bf16[128,1024]{1,0:T(8,128)(2,1)S(1)}, bf16[128,1024]{1,0:T(8,128)(2,1)S(1)}, u32[]{:S(2)}, u32[]{:S(2)}) collective-permute-start(bf16[128,1024]{1,0:T(8,128)(2,1)S(1)} %fusion.13), channel_id=1, source_target_pairs={{0,4},{1,5},{2,6},{3,7},{16,20},{17,21},{18,22},{19,23}} | collective-permute-start | bytes 786440 | tf_op jit(solution)/shard_map/ppermute | solution.py:371
  29.9 1.6 %collective-permute-start.12 = (bf16[128,1024]{1,0:T(8,128)(2,1)S(1)}, bf16[128,1024]{1,0:T(8,128)(2,1)S(1)}, u32[]{:S(2)}, u32[]{:S(2)}) collective-permute-start(bf16[128,1024]{1,0:T(8,128)(2,1)S(1)} %fusion.8), channel_id=1, source_target_pairs={{4,8},{5,9},{6,10},{7,11},{20,24},{21,25},{22,26},{23,27}} | collective-permute-start | bytes 786440 | tf_op jit(solution)/shard_map/ppermute | solution.py:371
  30.8 3.1 %collective-permute-start.6 = (bf16[128,1024]{1,0:T(8,128)(2,1)S(1)}, bf16[128,1024]{1,0:T(8,128)(2,1)S(1)}, u32[]{:S(2)}, u32[]{:S(2)}) collective-permute-start(bf16[128,1024]{1,0:T(8,128)(2,1)S(1)} %fusion.2), channel_id=1, source_target_pairs={{4,8},{5,9},{6,10},{7,11},{20,24},{21,25},{22,26},{23,27}} | collective-permute-start | bytes 786440 | tf_op jit(solution)/shard_map/ppermute | solution.py:371
  32.6 18.3 %collective-permute-start.13 = (bf16[128,1024]{1,0:T(8,128)(2,1)S(1)}, bf16[128,1024]{1,0:T(8,128)(2,1)S(1)}, u32[]{:S(2)}, u32[]{:S(2)}) collective-permute-start(bf16[128,1024]{1,0:T(8,128)(2,1)S(1)} %fusion.11), channel_id=1, source_target_pairs={{8,12},{9,13},{10,14},{11,15},{24,28},{25,29},{26,30},{27,31}} | collective-permute-start | bytes 786440 | tf_op jit(solution)/shard_map/ppermute | solution.py:371
  34.1 24.8 %collective-permute-start.7 = (bf16[128,1024]{1,0:T(8,128)(2,1)S(1)}, bf16[128,1024]{1,0:T(8,128)(2,1)S(1)}, u32[]{:S(2)}, u32[]{:S(2)}) collective-permute-start(bf16[128,1024]{1,0:T(8,128)(2,1)S(1)} %fusion.5), channel_id=1, source_target_pairs={{8,12},{9,13},{10,14},{11,15},{24,28},{25,29},{26,30},{27,31}} | collective-permute-start | bytes 786440 | tf_op jit(solution)/shard_map/ppermute | solution.py:371
  52.1 12.1 %collective-permute-start.14 = (bf16[128,1024]{1,0:T(8,128)(2,1)S(1)}, bf16[128,1024]{1,0:T(8,128)(2,1)S(1)}, u32[]{:S(2)}, u32[]{:S(2)}) collective-permute-start(bf16[128,1024]{1,0:T(8,128)(2,1)S(1)} %get-tuple-element.35), channel_id=1, source_target_pairs={{0,1},{1,0},{2,3},{3,2},{4,5},{5,4},{6,7},{7,6},{8,9},{9,8},{10,11... | collective-permute-start | bytes 786440 | tf_op jit(solution)/shard_map/ppermute | solution.py:378
  58.9 1.6 %copy-start.7 = (f32[2,64,128]{2,1,0:T(8,128)S(1)}, f32[2,64,128]{2,1,0:T(8,128)}, u32[]{:S(2)}) copy-start(f32[2,64,128]{2,1,0:T(8,128)} %copy-done.6) | copy-start | bytes 196612
  59.2 7.3 %collective-permute-start.8 = (bf16[128,1024]{1,0:T(8,128)(2,1)S(1)}, bf16[128,1024]{1,0:T(8,128)(2,1)S(1)}, u32[]{:S(2)}, u32[]{:S(2)}) collective-permute-start(bf16[128,1024]{1,0:T(8,128)(2,1)S(1)} %get-tuple-element.37), channel_id=1, source_target_pairs={{0,1},{1,0},{2,3},{3,2},{4,5},{5,4},{6,7},{7,6},{8,9},{9,8},{10,11... | collective-permute-start | bytes 786440 | tf_op jit(solution)/shard_map/ppermute | solution.py:378
  60.5 0.7 copy-start.13
  62.7 1.5 %copy-start.10 = (f32[4096]{0:T(1024)S(1)}, f32[4096]{0:T(1024)}, u32[]{:S(2)}) copy-start(f32[4096]{0:T(1024)} %param.21) | copy-start | bytes 49156
where the time goes:
time: 69.3 us; the launch traced here: 68.7 us
  waiting for transfers between devices  23.6 us (34%)
  starting transfers between devices  17.7 us (26%)
  Pallas kernels  15.1 us (22%)
  other arithmetic  5.98 us (9%)
  local copies, waits for them, and re-layouts  5.84 us (8%)
    ppermute x6, waiting for transfers between devices, chain(): arrived = lax.ppermute(running.astype(BF16), 'seq', [(step, step + 1)])  17.9 us
    pallas_call x9, Pallas kernels, call(): pl.pallas_call(kernel, grid_spec=pltpu.PrefetchScalarGridSpec(num_scalar_...  15.1 us
    unnamed x32, local copies, waits for them, and re-layouts  5.83 us
    ppermute x2, starting transfers between devices, chain(): return (mine, lax.ppermute(theirs, 'sub', [(0, 1), (1, 0)]))  5.79 us
    ppermute x6, starting transfers between devices, chain(): arrived = lax.ppermute(running.astype(BF16), 'seq', [(step, step + 1)])  5.29 us
    ppermute x1, waiting for transfers between devices, on_device(): lax.ppermute(dt_raw[0], 'head', shift(k))  4.17 us
    convert_element_type x6, other arithmetic, chain(): arrived = lax.ppermute(running.astype(BF16), 'seq', [(step, step + 1)])  3.72 us
    ppermute x2, starting transfers between devices, send_chunk(): received.append(lax.ppermute(packed, 'head', shift(k)))  2.23 us
  transfers between devices with their start and end apart: 15, of which 4 were waited for; matrix products, arithmetic and copies ran while one was open for 9% of the time, Pallas kernels for 19%

commit v1 on v0

--- a/solution.py
+++ b/solution.py
@@ -39,9 +39,9 @@
     return lax.broadcasted_iota(jnp.int32, (rows, LANES), 1)
 
 
-def tables_kernel(heads, place, own_ref, *refs):
-    *recv_refs, offset_ref, a_log_ref, tok_ref, head_ref, raw = refs
-    position = place[0]
+def tables_kernel(heads, own_ref, *refs):
+    *recv_refs, by_head, tok_ref, head_ref, raw = refs
+    position = lax.axis_index("head")
     rows = own_ref.shape[1]
     shards = len(recv_refs) + 1
     raw[pl.ds(pl.multiple_of(position * rows, rows), rows), :] = own_ref[0].astype(F32)
@@ -52,9 +52,9 @@
     if shards > 1:
         total = logits.shape[1]
         logits = pltpu.roll(logits, lax.rem(total - position * heads, total), axis=1)
-    v = logits[:, :heads] + offset_ref[...]
+    v = logits[:, :heads] + by_head[0:1, :]
     dt = jnp.maximum(v, 0.0) + jnp.log1p(jnp.exp(-jnp.abs(v)))
-    decay = -jnp.exp(a_log_ref[...]) * dt
+    decay = -jnp.exp(by_head[1:2, :]) * dt
     span = decay.shape[0]
     lower = lax.broadcasted_iota(jnp.int32, (span, span), 0) >= lax.broadcasted_iota(
         jnp.int32, (span, span), 1
@@ -78,33 +78,30 @@
     return silu(running)
 
 
-def state_kernel(c, head_dim, groups, place, own_x, own_bc, *refs):
-    shards = place.shape[0] - 1
+def state_kernel(c, taps, all_width, head_dim, groups, shards, own_columns, *refs):
     recv_refs, halos = refs[: shards - 1], refs[shards - 1 : 2 * shards - 1]
-    wx_ref, bx_ref, wbc_ref, bbc_ref, tok = refs[2 * shards - 1 : 2 * shards + 4]
-    xc_ref, bcc_ref, own_ref, own_d_ref, send_ref = refs[2 * shards + 4 : 2 * shards + 9]
-    joined, scaled, full, full_d = refs[2 * shards + 9 :]
-    position, sub = place[0], place[1]
-    rows = own_x.shape[1]
+    rows_ref, tok = refs[2 * shards - 1 : 2 * shards + 1]
+    xc_ref, bcc_ref, own_ref, own_d_ref, send_ref = refs[2 * shards + 1 : 2 * shards + 6]
+    joined, scaled, full, full_d = refs[2 * shards + 6 :]
+    position, sub = lax.axis_index("head"), lax.axis_index("sub")
+    rows = own_columns.shape[0]
     width, bc_width = xc_ref.shape[1], bcc_ref.shape[1]
-    all_width, all_bc = wx_ref.shape[1], wbc_ref.shape[1]
     first_head = c * width // head_dim
-    columns, bc_columns = slice(c * width, (c + 1) * width), slice(c * bc_width, (c + 1) * bc_width)
-    wx, bx = wx_ref[:, columns], bx_ref[:, columns]
-    wbc, bbc = wbc_ref[:, bc_columns], bbc_ref[:, bc_columns]
+    columns = slice(c * width, (c + 1) * width)
+    bc_columns = slice(all_width + c * bc_width, all_width + (c + 1) * bc_width)
+    wx, bx = rows_ref[:taps, columns], rows_ref[taps : taps + 1, columns]
+    wbc, bbc = rows_ref[:taps, bc_columns], rows_ref[taps : taps + 1, bc_columns]
     span = SPAN
-    edge = halos[0][...].astype(F32)
+    edge = halos[0][:, columns].astype(F32)
+    edge_bc = halos[0][:, bc_columns].astype(F32)
     for ref in halos[1:]:
-        edge = edge + ref[...].astype(F32)
-    edge_bc = edge[:, all_width + c * bc_width : all_width + (c + 1) * bc_width]
-    edge = edge[:, columns]
-    own_columns = pl.ds(pl.multiple_of(position * all_width + c * width, LANES), width)
-    own_bc_columns = pl.ds(pl.multiple_of(position * all_bc + c * bc_width, LANES), bc_width)
+        edge = edge + ref[:, columns].astype(F32)
+        edge_bc = edge_bc + ref[:, bc_columns].astype(F32)
     joined[:EDGE, :width] = edge
     joined[:EDGE, width:] = edge_bc
     at = pl.multiple_of(EDGE + position * rows, EDGE)
-    joined[pl.ds(at, rows), :width] = own_x[0, :, own_columns].astype(F32)
-    joined[pl.ds(at, rows), width:] = own_bc[0, :, own_bc_columns].astype(F32)
+    joined[pl.ds(at, rows), :width] = own_columns[:, columns].astype(F32)
+    joined[pl.ds(at, rows), width:] = own_columns[:, bc_columns].astype(F32)
     for k, ref in enumerate(recv_refs):
         source = lax.rem(position + shards - 1 - k, shards)
         at = pl.multiple_of(EDGE + source * rows, EDGE)
@@ -133,7 +130,7 @@
     half = width // 2
     mine = pl.ds(pl.multiple_of(sub * half, LANES), half)
     other = pl.ds(pl.multiple_of((1 - sub) * half, LANES), half)
-    own_ref[...] = full[:, mine]
+    own_ref[...] = full[:, mine].astype(BF16)
     own_d_ref[...] = full_d[EDGE - 1 :, mine]
     send_ref[:STATE, :] = full[:, other].astype(BF16)
     d = full_d[EDGE - 1 :, other]
@@ -147,7 +144,7 @@
     send_ref[STATE:, :] = parts.astype(BF16)
 
 
-def intra_kernel(first_head, head_dim, groups, place, xc_ref, bcc_ref, tok, heads_ref, skip_ref, y_ref):
+def intra_kernel(first_head, head_dim, groups, xc_ref, bcc_ref, tok, heads_ref, by_head, y_ref):
     span, width = xc_ref.shape
     per_strip = LANES // head_dim
     lane = lane_index(span)
@@ -181,18 +178,18 @@
                 preferred_element_type=F32,
             )
             head = first_head + j * per_strip
-            skip = widen_pair(skip_ref[...], head, head_dim, lane_index(1))
-            y_ref[:, lanes] = y + skip * wide
-
-
-def finish_kernel(c, head_dim, groups, place, y_ref, bcc_ref, tok, mine, other, gain_ref, *refs):
+            skip = widen_pair(by_head[2:3, :], head, head_dim, lane_index(1))
+            y_ref[:, lanes] = (y + skip * wide).astype(y_ref.dtype)
+
+
+def finish_kernel(c, gain_row, head_dim, groups, y_ref, bcc_ref, tok, mine, other, rows_ref, *refs):
     out_ref, carried, scratch, normed, sems = refs[-5:]
     span, width = y_ref.shape
     first_head = c * width // head_dim
-    gain = gain_ref[:, c * width : (c + 1) * width]
+    gain = rows_ref[gain_row : gain_row + 1, c * width : (c + 1) * width]
     copies = []
     half = width // 2
-    sub = place[1]
+    sub = lax.axis_index("sub")
     carried[:, pl.ds(pl.multiple_of(sub * half, LANES), half)] = mine[...]
     carried[:, pl.ds(pl.multiple_of((1 - sub) * half, LANES), half)] = other[...]
     lane = lane_index(span)
@@ -207,7 +204,7 @@
             here = slice(j * LANES, (j + 1) * LANES)
             there = slice(g * group_width + j * LANES, g * group_width + (j + 1) * LANES)
             head = first_head + (g * group_width + j * LANES) // head_dim
-            y = y_ref[:, there] + scratch[:, here] * widen_pair(decay, head, head_dim, lane)
+            y = y_ref[:, there].astype(F32) + scratch[:, here] * widen_pair(decay, head, head_dim, lane)
             scratch[:, here] = y
             squares = squares + y * y
         mean = jnp.sum(squares, axis=1, keepdims=True) * (1.0 / group_width)
@@ -225,20 +222,115 @@
         copy.wait()
 
 
-def pack_kernel(parts, place, *refs):
-    sources, out, sems = refs[: len(parts)], refs[-2], refs[-1]
-    copies = []
-    column = 0
-    for n, (source, (stride, offset, count)) in enumerate(zip(sources, parts)):
-        start = pl.multiple_of(place[0] * stride + offset, LANES)
-        copies.append(
-            pltpu.make_async_copy(
-                source.at[0, :, pl.ds(start, count)], out.at[:, pl.ds(column, count)], sems.at[n]
-            )
-        )
-        column += count
+def copy_all(pairs, sems):
+    copies = [pltpu.make_async_copy(a, b, sems.at[n]) for n, (a, b) in enumerate(pairs)]
     for copy in copies:
         copy.start()
+    for copy in copies:
+        copy.wait()
+
+
+def pack_kernel(k, shards, parts, *refs):
+    sources, out, sems = refs[: len(parts)], refs[-2], refs[-1]
+    target = lax.rem(lax.axis_index("head") + k, shards)
+    pairs = []
+    column = 0
+    for source, (stride, offset, count) in zip(sources, parts):
+        start = pl.multiple_of(target * stride + offset, LANES)
+        pairs.append((source.at[0, :, pl.ds(start, count)], out.at[:, pl.ds(column, count)]))
+        column += count
+    copy_all(pairs, sems)
+
+
+def tails_kernel(width, bc_width, x_ref, bc_ref, *refs):
+    *outs, sems = refs
+    last = pl.ds(x_ref.shape[1] - EDGE, EDGE)
+    pairs = []
+    for k, out in enumerate(outs):
+        pairs.append(
+            (x_ref.at[0, last, pl.ds(k * width, width)], out.at[:, pl.ds(0, width)])
+        )
+        pairs.append(
+            (bc_ref.at[0, last, pl.ds(k * bc_width, bc_width)], out.at[:, pl.ds(width, bc_width)])
+        )
+    copy_all(pairs, sems)
+
+
+def partner_decay(got):
+    rows = got[STATE:, :].astype(F32)
+    return rows[0:1, :] + rows[1:2, :] + rows[2:3, :]
+
+
+def join_kernel(own, own_d, got, total, decay):
+    sub = lax.axis_index("sub")
+    other_d = partner_decay(got)
+    decay[...] = own_d[...] * other_d
+
+    @pl.when(sub == 0)
+    def _():
+        total[...] = (other_d * own[...].astype(F32) + got[:STATE, :].astype(F32)).astype(BF16)
+
+    @pl.when(sub != 0)
+    def _():
+        total[...] = (own_d[...] * got[:STATE, :].astype(F32) + own[...].astype(F32)).astype(BF16)
+
+
+def relay_kernel(arrived, total, decay, out):
+    out[...] = (decay[...] * arrived[...].astype(F32) + total[...].astype(F32)).astype(BF16)
+
+
+def close_kernel(own, own_d, got, *refs):
+    *arrived, mine, theirs, entry = refs
+    chip, sub = lax.axis_index("seq"), lax.axis_index("sub")
+
+    @pl.when(chip == 0)
+    def _():
+        entry[...] = jnp.zeros_like(entry)
+
+    for step, ref in enumerate(arrived):
+
+        @pl.when(chip == step + 1)
+        def _():
+            entry[...] = ref[...]
+
+    @pl.when(sub == 0)
+    def _():
+        mine[...] = entry[...]
+        theirs[...] = (own_d[...] * entry[...].astype(F32) + own[...].astype(F32)).astype(BF16)
+
+    @pl.when(sub != 0)
+    def _():
+        theirs[...] = entry[...]
+        mine[...] = (
+            partner_decay(got) * entry[...].astype(F32) + got[:STATE, :].astype(F32)
+        ).astype(BF16)
+
+
+def prep_kernel(x_ref, bc_ref, wx, bx, wbc, bbc, gain, offset, a_log, skip, *refs):
+    own_ref, rows_ref, heads_ref, sems = refs
+    taps, width = wx.shape
+    bc_width = wbc.shape[1]
+    position = lax.axis_index("head")
+    x_at = pl.multiple_of(position * width, LANES)
+    bc_at = pl.multiple_of(position * bc_width, LANES)
+    copies = [
+        pltpu.make_async_copy(
+            x_ref.at[0, :, pl.ds(x_at, width)], own_ref.at[:, pl.ds(0, width)], sems.at[0]
+        ),
+        pltpu.make_async_copy(
+            bc_ref.at[0, :, pl.ds(bc_at, bc_width)], own_ref.at[:, pl.ds(width, bc_width)], sems.at[1]
+        ),
+    ]
+    for copy in copies:
+        copy.start()
+    rows_ref[:taps, :width] = wx[...]
+    rows_ref[taps : taps + 1, :width] = bx[...]
+    rows_ref[taps + 1 : taps + 2, :width] = gain[...]
+    rows_ref[:taps, width:] = wbc[...]
+    rows_ref[taps : taps + 1, width:] = bbc[...]
+    heads_ref[0:1, :] = offset[...]
+    heads_ref[1:2, :] = a_log[...]
+    heads_ref[2:3, :] = skip[...]
     for copy in copies:
         copy.wait()
 
@@ -258,8 +350,6 @@
 ):
     shards = lax.axis_size("head")
     chips = lax.axis_size("seq")
-    position = lax.axis_index("head")
-    sub = lax.axis_index("sub")
     rows = x_raw.shape[1]
     width = conv_x_weight.shape[1]
     bc_width = conv_bc_weight.shape[1]
@@ -269,22 +359,17 @@
     chunks = min(CHUNKS, groups)
     cw, cb, cg, ch = width // chunks, bc_width // chunks, groups // chunks, heads // chunks
     half = cw // 2
-    place = jnp.stack([position, sub] + [position] * (shards - 1)).astype(jnp.int32)
     row = lambda a: a.reshape(1, a.shape[0])
-    even = sub == 0
+    hbm = pl.BlockSpec(memory_space=pltpu.HBM)
     anywhere = pl.BlockSpec(memory_space=pl.ANY)
     vmem = pl.BlockSpec(memory_space=pltpu.VMEM)
 
     def call(kernel, operands, outs, scratch=(), specs=None, out_specs=None, aliases={}):
         return pl.pallas_call(
             kernel,
-            grid_spec=pltpu.PrefetchScalarGridSpec(
-                num_scalar_prefetch=1,
-                grid=(),
-                in_specs=specs or [vmem] * (len(operands) - 1),
-                out_specs=out_specs or [vmem] * len(outs),
-                scratch_shapes=list(scratch),
-            ),
+            in_specs=specs or [vmem] * len(operands),
+            out_specs=out_specs or [vmem] * len(outs),
+            scratch_shapes=list(scratch),
             out_shape=list(outs),
             input_output_aliases=aliases,
             compiler_params=pltpu.CompilerParams(vmem_limit_bytes=VMEM_LIMIT),
@@ -293,22 +378,49 @@
     def shift(k):
         return [(i, (i + k) % shards) for i in range(shards)]
 
+    x_here = pltpu.with_memory_space_constraint(x_raw, pltpu.HBM)
+    bc_here = pltpu.with_memory_space_constraint(bc_raw, pltpu.HBM)
+
     def send_chunk(c):
         received = []
         for k in range(1, shards):
-            target = lax.rem(position + k, shards).astype(jnp.int32).reshape(1)
             (packed,) = call(
-                functools.partial(pack_kernel, ((width, c * cw, cw), (bc_width, c * cb, cb))),
-                (target, x_raw, bc_raw),
+                functools.partial(
+                    pack_kernel, k, shards, ((width, c * cw, cw), (bc_width, c * cb, cb))
+                ),
+                (x_here, bc_here),
                 [pltpu.VMEM((rows, cw + cb), BF16)],
                 [pltpu.SemaphoreType.DMA((2,))],
-                specs=[pl.BlockSpec(memory_space=pltpu.HBM)] * 2,
+                specs=[hbm] * 2,
             )
             received.append(lax.ppermute(packed, "head", shift(k)))
         return received
 
+    dt_recv = [lax.ppermute(dt_raw[0], "head", shift(k)) for k in range(1, shards)]
     recvs = [send_chunk(c) for c in range(chunks)]
-    dt_recv = [lax.ppermute(dt_raw[0], "head", shift(k)) for k in range(1, shards)]
+    taps = conv_x_weight.shape[0]
+    own_columns, rows_table, heads_table = call(
+        prep_kernel,
+        (
+            x_here,
+            bc_here,
+            conv_x_weight,
+            row(conv_x_bias),
+            conv_bc_weight,
+            row(conv_bc_bias),
+            row(norm_gain),
+            row(stride_offset_per_head),
+            row(a_log),
+            row(skip_d),
+        ),
+        [
+            pltpu.VMEM((rows, width + bc_width), BF16),
+            pltpu.VMEM((8, width + bc_width), F32),
+            pltpu.VMEM((8, heads), F32),
+        ],
+        [pltpu.SemaphoreType.DMA((2,))],
+        specs=[hbm] * 2 + [vmem] * 8,
+    )
 
     following = lambda k: [
         ((b * shards + shards - 1) * 2 + s, ((b + s) * shards + k) * 2 + 1 - s)
@@ -316,34 +428,30 @@
         for s in range(2)
         if b + s < chips
     ]
-    halos = []
-    for k in range(shards):
-        tail = jnp.concatenate(
-            [
-                x_raw[0, rows - EDGE :, k * width : (k + 1) * width],
-                bc_raw[0, rows - EDGE :, k * bc_width : (k + 1) * bc_width],
-            ],
-            axis=1,
-        )
-        halos.append(lax.ppermute(tail, ("seq", "head", "sub"), following(k)))
+    tails = call(
+        functools.partial(tails_kernel, width, bc_width),
+        (x_here, bc_here),
+        [pltpu.VMEM((EDGE, width + bc_width), BF16)] * shards,
+        [pltpu.SemaphoreType.DMA((2 * shards,))],
+        specs=[hbm] * 2,
+    )
+    halos = [lax.ppermute(tails[k], ("seq", "head", "sub"), following(k)) for k in range(shards)]
 
     tok, by_head = call(
         functools.partial(tables_kernel, heads),
-        (place, dt_raw, *dt_recv, row(stride_offset_per_head), row(a_log)),
+        (dt_raw, *dt_recv, heads_table),
         [pltpu.VMEM((3, SPAN, heads), F32), pltpu.VMEM((2, heads, SPAN), F32)],
         [pltpu.VMEM((SPAN, dt_raw.shape[2]), F32)],
     )
 
-    weights = (conv_x_weight, row(conv_x_bias), conv_bc_weight, row(conv_bc_bias))
-
     def state(c):
         return call(
-            functools.partial(state_kernel, c, head_dim, cg),
-            (place, x_raw, bc_raw, *recvs[c], *halos, *weights, tok),
+            functools.partial(state_kernel, c, taps, width, head_dim, cg, shards),
+            (own_columns, *recvs[c], *halos, rows_table, tok),
             [
                 pltpu.VMEM((SPAN, cw), BF16),
                 pltpu.VMEM((SPAN, cb), BF16),
-                pltpu.VMEM((STATE, half), F32),
+                pltpu.VMEM((STATE, half), BF16),
                 pltpu.VMEM((1, half), F32),
                 pltpu.VMEM((STATE + EXTRA, half), BF16),
             ],
@@ -357,38 +465,39 @@
 
     def chain(own, own_d, send):
         got = lax.ppermute(send, "sub", [(0, 1), (1, 0)])
-        other = got[:STATE].astype(F32)
-        other_d = jnp.sum(got[STATE : STATE + 3].astype(F32), axis=0, keepdims=True)
-        state_even = jnp.where(even, own, other)
-        state_odd = jnp.where(even, other, own)
-        decay_even = jnp.where(even, own_d, other_d)
-        decay_odd = jnp.where(even, other_d, own_d)
-        total = decay_odd * state_even + state_odd
-        decay = decay_even * decay_odd
+        state_shape = pltpu.VMEM((STATE, half), BF16)
+        total, decay = call(
+            join_kernel, (own, own_d, got), [state_shape, pltpu.VMEM((1, half), F32)]
+        )
         running = total
-        entry = jnp.zeros((STATE, half), F32)
+        arrived = []
         for step in range(chips - 1):
-            arrived = lax.ppermute(running.astype(BF16), "seq", [(step, step + 1)])
-            arrived = arrived.astype(F32)
-            entry = entry + arrived
-            running = decay * arrived + total
-        later = decay_even * entry + state_even
-        mine = jnp.where(even, entry, later).astype(BF16)
-        theirs = jnp.where(even, later, entry).astype(BF16)
+            pairs = [(step, step + 1)]
+            if step == 0 and chips % 2 == 0:
+                pairs = [(i, i ^ 1) for i in range(chips)]
+            arrived.append(lax.ppermute(running, "seq", pairs))
+            if step < chips - 2:
+                (running,) = call(relay_kernel, (arrived[-1], total, decay), [state_shape])
+        mine, theirs = call(
+            close_kernel,
+            (own, own_d, got, *arrived),
+            [state_shape] * 2,
+            [pltpu.VMEM((STATE, half), BF16)],
+        )
         return mine, lax.ppermute(theirs, "sub", [(0, 1), (1, 0)])
 
     def intra(c, xc, bcc):
         return call(
             functools.partial(intra_kernel, c * ch, head_dim, cg),
-            (place, xc, bcc, tok, by_head, row(skip_d)),
-            [pltpu.VMEM((SPAN, cw), F32)],
+            (xc, bcc, tok, by_head, heads_table),
+            [pltpu.VMEM((SPAN, cw), BF16)],
         )[0]
 
     def finish(c, y, bcc, mine, theirs, out):
         before = [] if out is None else [out]
         return call(
-            functools.partial(finish_kernel, c, head_dim, cg),
-            (place, y, bcc, tok, mine, theirs, row(norm_gain), *before),
+            functools.partial(finish_kernel, c, taps + 1, head_dim, cg),
+            (y, bcc, tok, mine, theirs, rows_table, *before),
             [jax.ShapeDtypeStruct((1, SPAN, width), BF16)],
             [
                 pltpu.VMEM((STATE, cw), BF16),
@@ -398,7 +507,7 @@
             ],
             specs=[vmem] * 6 + [anywhere] * len(before),
             out_specs=[anywhere],
-            aliases={7: 0} if before else {},
+            aliases={6: 0} if before else {},
         )[0]
 
     parts = []

time: 69.3 us -> 61.6 us (0.89)
  other arithmetic: 5.98 us -> 0 us
  waiting for transfers between devices: 23.6 us -> 29 us
  local copies, waits for them, and re-layouts: 5.84 us -> 0.66 us
  starting transfers between devices: 17.7 us -> 16.5 us
    unnamed x32 -> x18, local copies, waits for them, and re-layouts: 5.83 us -> 0.66 us
    convert_element_type x8 -> x0, other arithmetic: 5.12 us -> none  [the longest x6 3.72 us: chain(): arrived = lax.ppermute(running.astype(BF16), 'seq', [(step, step + 1)])]
    ppermute x1, waiting for transfers between devices: 4.17 us -> 8.27 us  [on_device(): lax.ppermute(dt_raw[0], 'head', shift(k))]
    ppermute x2, waiting for transfers between devices: 0.01 us -> 1.22 us  [chain(): got = lax.ppermute(send, 'sub', [(0, 1), (1, 0)])]
    ppermute x8, starting transfers between devices: 7.25 us -> 6.36 us  [the longest x6 4.41 us: chain(): arrived.append(lax.ppermute(running, 'seq', pairs))]
    reduce_sum x2 -> x0, other arithmetic: 0.75 us -> none  [chain(): other_d = jnp.sum(got[STATE:STATE + 3].astype(F32), axis=0, keepdims=True)]
    ppermute x1, starting transfers between devices: 0.58 us -> 1.28 us  [on_device(): lax.ppermute(dt_raw[0], 'head', shift(k))]
    pallas_call x9 -> x19, Pallas kernels: 15.1 us -> 14.9 us  [call(): pl.pallas_call(kernel, in_specs=specs or [vmem] * len(operands), out_spec...]
  transfers between devices with their start and end apart: 15 -> 15, of which waited for: 4 -> 7; matrix products, arithmetic and copies ran while one was open for 9% -> 0% of each run, Pallas kernels for 19% -> 20%
where the time goes in v1:
time: 61.6 us; the launch traced here: 61.3 us
  waiting for transfers between devices  29 us (47%)
  starting transfers between devices  16.5 us (27%)
  Pallas kernels  14.9 us (24%)
  local copies, waits for them, and re-layouts  0.66 us (1%)
    ppermute x6, waiting for transfers between devices, chain(): arrived.append(lax.ppermute(running, 'seq', pairs))  18.3 us
    pallas_call x19, Pallas kernels, call(): pl.pallas_call(kernel, in_specs=specs or [vmem] * len(operands), out_spec...  14.9 us
    ppermute x1, waiting for transfers between devices, on_device(): lax.ppermute(dt_raw[0], 'head', shift(k))  8.27 us
    ppermute x2, starting transfers between devices, chain(): return (mine, lax.ppermute(theirs, 'sub', [(0, 1), (1, 0)]))  5.85 us
    ppermute x6, starting transfers between devices, chain(): arrived.append(lax.ppermute(running, 'seq', pairs))  4.41 us
    ppermute x2, starting transfers between devices, on_device(): lax.ppermute(tails[k], ('seq', 'head', 'sub'), following(k))  1.96 us
    ppermute x2, starting transfers between devices, send_chunk(): received.append(lax.ppermute(packed, 'head', shift(k)))  1.6 us
    ppermute x2, starting transfers between devices, chain(): got = lax.ppermute(send, 'sub', [(0, 1), (1, 0)])  1.42 us
  transfers between devices with their start and end apart: 15, of which 7 were waited for; matrix products, arithmetic and copies ran while one was open for 0% of the time, Pallas kernels for 20%

profile of v1, /device:TPU:25, one launch (start us, length us, event | category | flops | bytes accessed | tf_op | source)
XLA Modules:
  0.0 61.3 jit_solution(11611120082250232928)
XLA Ops:
  0.0 1.0 %shard_map.119 = bf16[64,2560]{1,0:T(8,128)(2,1)S(1)} custom-call(bf16[1,64,8192]{2,1,0:T(8,128)(2,1)} %refs_0_.3, bf16[1,64,2048]{2,1,0:T(8,128)(2,1)} %refs_1_.3), custom_call_target="tpu_custom_call" | custom-call | tf_op jit(solution)/shard_map/pallas_call | solution.py:368
  1.0 1.3 %collective-permute-start.9 = (bf16[64,2560]{1,0:T(8,128)(2,1)S(1)}, bf16[64,2560]{1,0:T(8,128)(2,1)S(1)}, u32[]{:S(2)}, u32[]{:S(2)}) collective-permute-start(bf16[64,2560]{1,0:T(8,128)(2,1)S(1)} %shard_map.119), channel_id=1, source_target_pairs={{0,2},{2,0},{1,3},{3,1},{4,6},{6,4},{5,7},{7,5},{8,10},{10,8},{9,1... | collective-permute-start | bytes 983048 | tf_op jit(solution)/shard_map/ppermute | solution.py:396
  2.3 1.0 %shard_map.110 = bf16[64,2560]{1,0:T(8,128)(2,1)S(1)} custom-call(bf16[1,64,8192]{2,1,0:T(8,128)(2,1)} %refs_0_.3, bf16[1,64,2048]{2,1,0:T(8,128)(2,1)} %refs_1_.3), custom_call_target="tpu_custom_call" | custom-call | tf_op jit(solution)/shard_map/pallas_call | solution.py:368
  3.2 0.0 copy-start.4
  3.2 0.0 copy-start
  3.3 0.3 collective-permute-start
  3.6 1.0 %shard_map.111 = (bf16[8,5120]{1,0:T(8,128)(2,1)S(1)}, bf16[8,5120]{1,0:T(8,128)(2,1)S(1)}) custom-call(bf16[1,64,8192]{2,1,0:T(8,128)(2,1)} %refs_0_.3, bf16[1,64,2048]{2,1,0:T(8,128)(2,1)} %refs_1_.3), custom_call_target="tpu_custom_call" | custom-call | tf_op jit(solution)/shard_map/pallas_call | solution.py:368
  4.6 0.0 copy-start.1
  4.6 1.3 %collective-permute-start.1 = (bf16[8,5120]{1,0:T(8,128)(2,1)S(1)}, bf16[8,5120]{1,0:T(8,128)(2,1)S(1)}, u32[]{:S(2)}, u32[]{:S(2)}) collective-permute-start(bf16[8,5120]{1,0:T(8,128)(2,1)S(1)} %get-tuple-element.31), channel_id=1, source_target_pairs={{2,1},{3,4},{6,5},{7,8},{10,9},{11,12},{14,13},{18,17},{19,20},{22... | collective-permute-start | bytes 245768 | tf_op jit(solution)/shard_map/ppermute | solution.py:438
  5.9 0.7 %collective-permute-start.2 = (bf16[8,5120]{1,0:T(8,128)(2,1)S(1)}, bf16[8,5120]{1,0:T(8,128)(2,1)S(1)}, u32[]{:S(2)}, u32[]{:S(2)}) collective-permute-start(bf16[8,5120]{1,0:T(8,128)(2,1)S(1)} %get-tuple-element.32), channel_id=1, source_target_pairs={{2,3},{3,6},{6,7},{7,10},{10,11},{11,14},{14,15},{18,19},{19,22},{... | collective-permute-start | bytes 245768 | tf_op jit(solution)/shard_map/ppermute | solution.py:438
  6.6 1.3 %collective-permute-start.3 = (bf16[64,128]{1,0:T(8,128)(2,1)S(1)}, bf16[64,128]{1,0:T(8,128)(2,1)S(1)}, u32[]{:S(2)}, u32[]{:S(2)}) collective-permute-start(bf16[64,128]{1,0:T(8,128)(2,1)S(1)} %bitcast.9), channel_id=1, source_target_pairs={{0,2},{2,0},{1,3},{3,1},{4,6},{6,4},{5,7},{7,5},{8,10},{10,8},{9,1... | collective-permute-start | bytes 49160 | tf_op jit(solution)/shard_map/ppermute | solution.py:399
  7.9 0.6 copy-done.6
  8.5 0.0 copy-done.7
  8.5 1.1 %shard_map.109 = (bf16[64,5120]{1,0:T(8,128)(2,1)S(1)}, f32[8,5120]{1,0:T(8,128)S(1)}, f32[8,64]{1,0:T(8,128)S(1)}) custom-call(bf16[1,64,8192]{2,1,0:T(8,128)(2,1)} %refs_0_.3, bf16[1,64,2048]{2,1,0:T(8,128)(2,1)} %refs_1_.3, f32[4,4096]{1,0:T(4,128)S(1)} %copy-done, f32[1,4096]{1,0:T(1,128)S(1)} %bitcast.7, f32[4,1024]{1,0:T(4,128)S(1)} %copy-done.2, ...), custom_call_target="tpu_custom_call" | custom-call | tf_op jit(solution)/shard_map/pallas_call | solution.py:368
  9.6 8.3 %collective-permute-done.3.refs_0_ = bf16[64,128]{1,0:T(8,128)(2,1)S(1)} collective-permute-done((bf16[64,128]{1,0:T(8,128)(2,1)S(1)}, bf16[64,128]{1,0:T(8,128)(2,1)S(1)}, u32[]{:S(2)}, u32[]{:S(2)}) %collective-permute-start.3) | collective-permute-done | bytes 16416 | tf_op jit(solution)/shard_map/ppermute | solution.py:399
  17.9 0.4 shard_map.112
  18.3 1.2 %collective-permute-done.1.refs_1_ = bf16[8,5120]{1,0:T(8,128)(2,1)S(1)} collective-permute-done((bf16[8,5120]{1,0:T(8,128)(2,1)S(1)}, bf16[8,5120]{1,0:T(8,128)(2,1)S(1)}, u32[]{:S(2)}, u32[]{:S(2)}) %collective-permute-start.1) | collective-permute-done | bytes 81952 | tf_op jit(solution)/shard_map/ppermute | solution.py:438
  19.4 0.0 collective-permute-done.2.refs_2_
  19.4 2.2 %shard_map.120 = (bf16[128,2048]{1,0:T(8,128)(2,1)S(1)}, bf16[128,512]{1,0:T(8,128)(2,1)S(1)}, bf16[128,1024]{1,0:T(8,128)(2,1)S(1)}, f32[1,1024]{1,0:T(1,128)S(1)}, bf16[144,1024]{1,0:T(8,128)(2,1)S(1)}) custom-call(bf16[64,5120]{1,0:T(8,128)(2,1)S(1)} %get-tuple-element.30.own_columns, bf16[64,2560]{1,0:T(8,128)(2,1)S(1)} %collective-permute-done.9.refs_0_, ...), custom_call_target="tpu_custom_call" | custom-call | tf_op jit(solution)/shard_map/pallas_call | solution.py:368
  21.7 1.3 %collective-permute-start.10 = (bf16[144,1024]{1,0:T(8,128)(2,1)S(1)}, bf16[144,1024]{1,0:T(8,128)(2,1)S(1)}, u32[]{:S(2)}, u32[]{:S(2)}) collective-permute-start(bf16[144,1024]{1,0:T(8,128)(2,1)S(1)} %get-tuple-element.50), channel_id=1, source_target_pairs={{0,1},{1,0},{2,3},{3,2},{4,5},{5,4},{6,7},{7,6},{8,9},{9,8},{10,11... | collective-permute-start | bytes 884744 | tf_op jit(solution)/shard_map/ppermute | solution.py:467
  23.0 2.2 %shard_map.113 = (bf16[128,2048]{1,0:T(8,128)(2,1)S(1)}, bf16[128,512]{1,0:T(8,128)(2,1)S(1)}, bf16[128,1024]{1,0:T(8,128)(2,1)S(1)}, f32[1,1024]{1,0:T(1,128)S(1)}, bf16[144,1024]{1,0:T(8,128)(2,1)S(1)}) custom-call(bf16[64,5120]{1,0:T(8,128)(2,1)S(1)} %get-tuple-element.30.own_columns, bf16[64,2560]{1,0:T(8,128)(2,1)S(1)} %collective-permute-done.refs_0_, ...), custom_call_target="tpu_custom_call" | custom-call | tf_op jit(solution)/shard_map/pallas_call | solution.py:368
  25.2 0.1 collective-permute-start.4
  25.3 0.0 collective-permute-done.10.got
  25.3 0.1 shard_map.122
  25.4 0.2 collective-permute-start.11
  25.6 1.2 %collective-permute-done.4.got = bf16[144,1024]{1,0:T(8,128)(2,1)S(1)} collective-permute-done((bf16[144,1024]{1,0:T(8,128)(2,1)S(1)}, bf16[144,1024]{1,0:T(8,128)(2,1)S(1)}, u32[]{:S(2)}, u32[]{:S(2)}) %collective-permute-start.4) | collective-permute-done | bytes 294944 | tf_op jit(solution)/shard_map/ppermute | solution.py:467
  26.9 0.1 shard_map.115
  27.0 0.2 collective-permute-start.5
  27.2 5.7 %collective-permute-done.11.arrived.refs_0_ = bf16[128,1024]{1,0:T(8,128)(2,1)S(1)} collective-permute-done((bf16[128,1024]{1,0:T(8,128)(2,1)S(1)}, bf16[128,1024]{1,0:T(8,128)(2,1)S(1)}, u32[]{:S(2)}, u32[]{:S(2)}) %collective-permute-start.11) | collective-permute-done | bytes 262176 | tf_op jit(solution)/shard_map/ppermute | solution.py:478
  32.9 0.1 shard_map.123
  32.9 0.7 %collective-permute-start.12 = (bf16[128,1024]{1,0:T(8,128)(2,1)S(1)}, bf16[128,1024]{1,0:T(8,128)(2,1)S(1)}, u32[]{:S(2)}, u32[]{:S(2)}) collective-permute-start(bf16[128,1024]{1,0:T(8,128)(2,1)S(1)} %shard_map.123), channel_id=1, source_target_pairs={{4,8},{5,9},{6,10},{7,11},{20,24},{21,25},{22,26},{23,27}} | collective-permute-start | bytes 786440 | tf_op jit(solution)/shard_map/ppermute | solution.py:478
  33.6 4.8 %collective-permute-done.5.arrived.refs_0_ = bf16[128,1024]{1,0:T(8,128)(2,1)S(1)} collective-permute-done((bf16[128,1024]{1,0:T(8,128)(2,1)S(1)}, bf16[128,1024]{1,0:T(8,128)(2,1)S(1)}, u32[]{:S(2)}, u32[]{:S(2)}) %collective-permute-start.5) | collective-permute-done | bytes 262176 | tf_op jit(solution)/shard_map/ppermute | solution.py:478
  38.5 0.1 shard_map.116
  38.6 0.7 %collective-permute-start.6 = (bf16[128,1024]{1,0:T(8,128)(2,1)S(1)}, bf16[128,1024]{1,0:T(8,128)(2,1)S(1)}, u32[]{:S(2)}, u32[]{:S(2)}) collective-permute-start(bf16[128,1024]{1,0:T(8,128)(2,1)S(1)} %shard_map.116), channel_id=1, source_target_pairs={{4,8},{5,9},{6,10},{7,11},{20,24},{21,25},{22,26},{23,27}} | collective-permute-start | bytes 786440 | tf_op jit(solution)/shard_map/ppermute | solution.py:478
  39.3 0.1 shard_map.124
  39.3 1.3 %collective-permute-start.13 = (bf16[128,1024]{1,0:T(8,128)(2,1)S(1)}, bf16[128,1024]{1,0:T(8,128)(2,1)S(1)}, u32[]{:S(2)}, u32[]{:S(2)}) collective-permute-start(bf16[128,1024]{1,0:T(8,128)(2,1)S(1)} %shard_map.124), channel_id=1, source_target_pairs={{8,12},{9,13},{10,14},{11,15},{24,28},{25,29},{26,30},{27,31}} | collective-permute-start | bytes 786440 | tf_op jit(solution)/shard_map/ppermute | solution.py:478
  40.7 0.1 shard_map.117
  40.7 1.3 %collective-permute-start.7 = (bf16[128,1024]{1,0:T(8,128)(2,1)S(1)}, bf16[128,1024]{1,0:T(8,128)(2,1)S(1)}, u32[]{:S(2)}, u32[]{:S(2)}) collective-permute-start(bf16[128,1024]{1,0:T(8,128)(2,1)S(1)} %shard_map.117), channel_id=1, source_target_pairs={{8,12},{9,13},{10,14},{11,15},{24,28},{25,29},{26,30},{27,31}} | collective-permute-start | bytes 786440 | tf_op jit(solution)/shard_map/ppermute | solution.py:478
  42.0 5.0 %collective-permute-done.13.refs_2_ = bf16[128,1024]{1,0:T(8,128)(2,1)S(1)} collective-permute-done((bf16[128,1024]{1,0:T(8,128)(2,1)S(1)}, bf16[128,1024]{1,0:T(8,128)(2,1)S(1)}, u32[]{:S(2)}, u32[]{:S(2)}) %collective-permute-start.13) | collective-permute-done | bytes 262176 | tf_op jit(solution)/shard_map/ppermute | solution.py:478
  47.0 0.1 shard_map.125
  47.1 3.0 %collective-permute-start.14 = (bf16[128,1024]{1,0:T(8,128)(2,1)S(1)}, bf16[128,1024]{1,0:T(8,128)(2,1)S(1)}, u32[]{:S(2)}, u32[]{:S(2)}) collective-permute-start(bf16[128,1024]{1,0:T(8,128)(2,1)S(1)} %get-tuple-element.54), channel_id=1, source_target_pairs={{0,1},{1,0},{2,3},{3,2},{4,5},{5,4},{6,7},{7,6},{8,9},{9,8},{10,11... | collective-permute-start | bytes 786440 | tf_op jit(solution)/shard_map/ppermute | solution.py:487
  50.2 2.8 %collective-permute-done.7.refs_2_ = bf16[128,1024]{1,0:T(8,128)(2,1)S(1)} collective-permute-done((bf16[128,1024]{1,0:T(8,128)(2,1)S(1)}, bf16[128,1024]{1,0:T(8,128)(2,1)S(1)}, u32[]{:S(2)}, u32[]{:S(2)}) %collective-permute-start.7) | collective-permute-done | bytes 262176 | tf_op jit(solution)/shard_map/ppermute | solution.py:478
  53.0 0.1 shard_map.118
  53.1 2.8 %collective-permute-start.8 = (bf16[128,1024]{1,0:T(8,128)(2,1)S(1)}, bf16[128,1024]{1,0:T(8,128)(2,1)S(1)}, u32[]{:S(2)}, u32[]{:S(2)}) collective-permute-start(bf16[128,1024]{1,0:T(8,128)(2,1)S(1)} %get-tuple-element.45), channel_id=1, source_target_pairs={{0,1},{1,0},{2,3},{3,2},{4,5},{5,4},{6,7},{7,6},{8,9},{9,8},{10,11... | collective-permute-start | bytes 786440 | tf_op jit(solution)/shard_map/ppermute | solution.py:487
  56.0 0.9 %shard_map.121.y_ref = bf16[128,2048]{1,0:T(8,128)(2,1)S(1)} custom-call(bf16[128,2048]{1,0:T(8,128)(2,1)S(1)} %get-tuple-element.46.xc_ref, bf16[128,512]{1,0:T(8,128)(2,1)S(1)} %get-tuple-element.47.bcc_ref, f32[3,128,64]{2,1,0:T(8,128)S(1)} %get-tuple-element.35.refs_4_.tok, f32[2,64,128]{2,1,0:T(8,128)S(1)} %get-tuple-element.38.heads_ref, ...), custom_call_target="tpu_custom_call" | custom-call | tf_op jit(solution)/shard_map/pallas_call | solution.py:368
  56.9 1.0 %shard_map.114.y_ref = bf16[128,2048]{1,0:T(8,128)(2,1)S(1)} custom-call(bf16[128,2048]{1,0:T(8,128)(2,1)S(1)} %get-tuple-element.36.xc_ref, bf16[128,512]{1,0:T(8,128)(2,1)S(1)} %get-tuple-element.37.bcc_ref, f32[3,128,64]{2,1,0:T(8,128)S(1)} %get-tuple-element.35.refs_4_.tok, f32[2,64,128]{2,1,0:T(8,128)S(1)} %get-tuple-element.38.heads_ref, ...), custom_call_target="tpu_custom_call" | custom-call | tf_op jit(solution)/shard_map/pallas_call | solution.py:368
  57.9 1.7 %shard_map.126.refs_0_ = bf16[1,128,4096]{2,1,0:T(8,128)(2,1)} custom-call(bf16[128,2048]{1,0:T(8,128)(2,1)S(1)} %shard_map.121.y_ref, bf16[128,512]{1,0:T(8,128)(2,1)S(1)} %get-tuple-element.47.bcc_ref, f32[3,128,64]{2,1,0:T(8,128)S(1)} %get-tuple-element.35.refs_4_.tok, bf16[128,1024]{1,0:T(8,128)(2,1)S(1)} %get-tuple-element.53.mine, ...), custom_call_target="tpu_custom_call" | custom-call | tf_op jit(solution)/shard_map/pallas_call | solution.py:368
  59.6 1.7 %shard_map.127 = bf16[1,128,4096]{2,1,0:T(8,128)(2,1)} custom-call(bf16[128,2048]{1,0:T(8,128)(2,1)S(1)} %shard_map.114.y_ref, bf16[128,512]{1,0:T(8,128)(2,1)S(1)} %get-tuple-element.37.bcc_ref, f32[3,128,64]{2,1,0:T(8,128)S(1)} %get-tuple-element.35.refs_4_.tok, bf16[128,1024]{1,0:T(8,128)(2,1)S(1)} %get-tuple-element.44.mine, ...), custom_call_target="tpu_custom_call", output_to_operand_aliasing={{}: (6, {})} | custom-call | tf_op jit(solution)/shard_map/pallas_call | solution.py:368
  (19 shorter events, 0.0 us)
Async XLA Ops:
  1.0 18.5 %collective-permute-start.9 = (bf16[64,2560]{1,0:T(8,128)(2,1)S(1)}, bf16[64,2560]{1,0:T(8,128)(2,1)S(1)}, u32[]{:S(2)}, u32[]{:S(2)}) collective-permute-start(bf16[64,2560]{1,0:T(8,128)(2,1)S(1)} %shard_map.119), channel_id=1, source_target_pairs={{0,2},{2,0},{1,3},{3,1},{4,6},{6,4},{5,7},{7,5},{8,10},{10,8},{9,1... | collective-permute-start | bytes 983048 | tf_op jit(solution)/shard_map/ppermute | solution.py:396
  3.2 3.3 %copy-start.4 = (bf16[1,64,128]{2,1,0:T(8,128)(2,1)S(1)}, bf16[1,64,128]{2,1,0:T(8,128)(2,1)}, u32[]{:S(2)}) copy-start(bf16[1,64,128]{2,1,0:T(8,128)(2,1)} %own_ref.1) | copy-start | bytes 49156
  3.2 4.6 %copy-start = (f32[4,4096]{1,0:T(4,128)S(1)}, f32[4,4096]{1,0:T(4,128)}, u32[]{:S(2)}) copy-start(f32[4,4096]{1,0:T(4,128)} %wx.1) | copy-start | bytes 196612
  3.3 19.7 %collective-permute-start = (bf16[64,2560]{1,0:T(8,128)(2,1)S(1)}, bf16[64,2560]{1,0:T(8,128)(2,1)S(1)}, u32[]{:S(2)}, u32[]{:S(2)}) collective-permute-start(bf16[64,2560]{1,0:T(8,128)(2,1)S(1)} %shard_map.110), channel_id=1, source_target_pairs={{0,2},{2,0},{1,3},{3,1},{4,6},{6,4},{5,7},{7,5},{8,10},{10,8},{9,1... | collective-permute-start | bytes 983048 | tf_op jit(solution)/shard_map/ppermute | solution.py:396
  3.6 4.3 %copy-start.2 = (f32[4,1024]{1,0:T(4,128)S(1)}, f32[4,1024]{1,0:T(4,128)}, u32[]{:S(2)}) copy-start(f32[4,1024]{1,0:T(4,128)} %wbc.1) | copy-start | bytes 49156
  3.6 4.3 %copy-start.3 = (f32[4096]{0:T(1024)S(1)}, f32[4096]{0:T(1024)}, u32[]{:S(2)}) copy-start(f32[4096]{0:T(1024)} %param.21) | copy-start | bytes 49156
  3.6 4.3 %copy-start.5 = (f32[1024]{0:T(1024)S(1)}, f32[1024]{0:T(1024)}, u32[]{:S(2)}) copy-start(f32[1024]{0:T(1024)} %param.17) | copy-start | bytes 12292
  3.6 4.3 %copy-start.8 = (f32[64]{0:T(128)S(1)}, f32[64]{0:T(128)}, u32[]{:S(2)}) copy-start(f32[64]{0:T(128)} %param.20) | copy-start | bytes 772
  4.6 3.3 %copy-start.1 = (f32[4096]{0:T(1024)S(1)}, f32[4096]{0:T(1024)}, u32[]{:S(2)}) copy-start(f32[4096]{0:T(1024)} %param.15) | copy-start | bytes 49156
  4.6 14.9 %collective-permute-start.1 = (bf16[8,5120]{1,0:T(8,128)(2,1)S(1)}, bf16[8,5120]{1,0:T(8,128)(2,1)S(1)}, u32[]{:S(2)}, u32[]{:S(2)}) collective-permute-start(bf16[8,5120]{1,0:T(8,128)(2,1)S(1)} %get-tuple-element.31), channel_id=1, source_target_pairs={{2,1},{3,4},{6,5},{7,8},{10,9},{11,12},{14,13},{18,17},{19,20},{22... | collective-permute-start | bytes 245768 | tf_op jit(solution)/shard_map/ppermute | solution.py:438
  5.9 13.6 %collective-permute-start.2 = (bf16[8,5120]{1,0:T(8,128)(2,1)S(1)}, bf16[8,5120]{1,0:T(8,128)(2,1)S(1)}, u32[]{:S(2)}, u32[]{:S(2)}) collective-permute-start(bf16[8,5120]{1,0:T(8,128)(2,1)S(1)} %get-tuple-element.32), channel_id=1, source_target_pairs={{2,3},{3,6},{6,7},{7,10},{10,11},{11,14},{14,15},{18,19},{19,22},{... | collective-permute-start | bytes 245768 | tf_op jit(solution)/shard_map/ppermute | solution.py:438
  6.6 11.3 %collective-permute-start.3 = (bf16[64,128]{1,0:T(8,128)(2,1)S(1)}, bf16[64,128]{1,0:T(8,128)(2,1)S(1)}, u32[]{:S(2)}, u32[]{:S(2)}) collective-permute-start(bf16[64,128]{1,0:T(8,128)(2,1)S(1)} %bitcast.9), channel_id=1, source_target_pairs={{0,2},{2,0},{1,3},{3,1},{4,6},{6,4},{5,7},{7,5},{8,10},{10,8},{9,1... | collective-permute-start | bytes 49160 | tf_op jit(solution)/shard_map/ppermute | solution.py:399
  7.8 0.7 %copy-start.6 = (f32[64]{0:T(128)S(1)}, f32[64]{0:T(128)}, u32[]{:S(2)}) copy-start(f32[64]{0:T(128)} %param.18) | copy-start | bytes 772
  7.8 0.7 %copy-start.7 = (f32[64]{0:T(128)S(1)}, f32[64]{0:T(128)}, u32[]{:S(2)}) copy-start(f32[64]{0:T(128)} %param.19) | copy-start | bytes 772
  21.7 3.6 %collective-permute-start.10 = (bf16[144,1024]{1,0:T(8,128)(2,1)S(1)}, bf16[144,1024]{1,0:T(8,128)(2,1)S(1)}, u32[]{:S(2)}, u32[]{:S(2)}) collective-permute-start(bf16[144,1024]{1,0:T(8,128)(2,1)S(1)} %get-tuple-element.50), channel_id=1, source_target_pairs={{0,1},{1,0},{2,3},{3,2},{4,5},{5,4},{6,7},{7,6},{8,9},{9,8},{10,11... | collective-permute-start | bytes 884744 | tf_op jit(solution)/shard_map/ppermute | solution.py:467
  25.2 1.6 %collective-permute-start.4 = (bf16[144,1024]{1,0:T(8,128)(2,1)S(1)}, bf16[144,1024]{1,0:T(8,128)(2,1)S(1)}, u32[]{:S(2)}, u32[]{:S(2)}) collective-permute-start(bf16[144,1024]{1,0:T(8,128)(2,1)S(1)} %get-tuple-element.41), channel_id=1, source_target_pairs={{0,1},{1,0},{2,3},{3,2},{4,5},{5,4},{6,7},{7,6},{8,9},{9,8},{10,11... | collective-permute-start | bytes 884744 | tf_op jit(solution)/shard_map/ppermute | solution.py:467
  25.4 7.4 %collective-permute-start.11 = (bf16[128,1024]{1,0:T(8,128)(2,1)S(1)}, bf16[128,1024]{1,0:T(8,128)(2,1)S(1)}, u32[]{:S(2)}, u32[]{:S(2)}) collective-permute-start(bf16[128,1024]{1,0:T(8,128)(2,1)S(1)} %get-tuple-element.51.total), channel_id=1, source_target_pairs={{0,4},{4,0},{8,12},{12,8},{1,5},{5,1},{9,13},{13,9},{2,6},{6,2},{1... | collective-permute-start | bytes 786440 | tf_op jit(solution)/shard_map/ppermute | solution.py:478
  27.0 11.5 %collective-permute-start.5 = (bf16[128,1024]{1,0:T(8,128)(2,1)S(1)}, bf16[128,1024]{1,0:T(8,128)(2,1)S(1)}, u32[]{:S(2)}, u32[]{:S(2)}) collective-permute-start(bf16[128,1024]{1,0:T(8,128)(2,1)S(1)} %get-tuple-element.42.total), channel_id=1, source_target_pairs={{0,4},{4,0},{8,12},{12,8},{1,5},{5,1},{9,13},{13,9},{2,6},{6,2},{1... | collective-permute-start | bytes 786440 | tf_op jit(solution)/shard_map/ppermute | solution.py:478
  32.9 6.3 %collective-permute-start.12 = (bf16[128,1024]{1,0:T(8,128)(2,1)S(1)}, bf16[128,1024]{1,0:T(8,128)(2,1)S(1)}, u32[]{:S(2)}, u32[]{:S(2)}) collective-permute-start(bf16[128,1024]{1,0:T(8,128)(2,1)S(1)} %shard_map.123), channel_id=1, source_target_pairs={{4,8},{5,9},{6,10},{7,11},{20,24},{21,25},{22,26},{23,27}} | collective-permute-start | bytes 786440 | tf_op jit(solution)/shard_map/ppermute | solution.py:478
  38.6 2.1 %collective-permute-start.6 = (bf16[128,1024]{1,0:T(8,128)(2,1)S(1)}, bf16[128,1024]{1,0:T(8,128)(2,1)S(1)}, u32[]{:S(2)}, u32[]{:S(2)}) collective-permute-start(bf16[128,1024]{1,0:T(8,128)(2,1)S(1)} %shard_map.116), channel_id=1, source_target_pairs={{4,8},{5,9},{6,10},{7,11},{20,24},{21,25},{22,26},{23,27}} | collective-permute-start | bytes 786440 | tf_op jit(solution)/shard_map/ppermute | solution.py:478
  39.3 7.7 %collective-permute-start.13 = (bf16[128,1024]{1,0:T(8,128)(2,1)S(1)}, bf16[128,1024]{1,0:T(8,128)(2,1)S(1)}, u32[]{:S(2)}, u32[]{:S(2)}) collective-permute-start(bf16[128,1024]{1,0:T(8,128)(2,1)S(1)} %shard_map.124), channel_id=1, source_target_pairs={{8,12},{9,13},{10,14},{11,15},{24,28},{25,29},{26,30},{27,31}} | collective-permute-start | bytes 786440 | tf_op jit(solution)/shard_map/ppermute | solution.py:478
  40.7 12.2 %collective-permute-start.7 = (bf16[128,1024]{1,0:T(8,128)(2,1)S(1)}, bf16[128,1024]{1,0:T(8,128)(2,1)S(1)}, u32[]{:S(2)}, u32[]{:S(2)}) collective-permute-start(bf16[128,1024]{1,0:T(8,128)(2,1)S(1)} %shard_map.117), channel_id=1, source_target_pairs={{8,12},{9,13},{10,14},{11,15},{24,28},{25,29},{26,30},{27,31}} | collective-permute-start | bytes 786440 | tf_op jit(solution)/shard_map/ppermute | solution.py:478
  47.1 10.7 %collective-permute-start.14 = (bf16[128,1024]{1,0:T(8,128)(2,1)S(1)}, bf16[128,1024]{1,0:T(8,128)(2,1)S(1)}, u32[]{:S(2)}, u32[]{:S(2)}) collective-permute-start(bf16[128,1024]{1,0:T(8,128)(2,1)S(1)} %get-tuple-element.54), channel_id=1, source_target_pairs={{0,1},{1,0},{2,3},{3,2},{4,5},{5,4},{6,7},{7,6},{8,9},{9,8},{10,11... | collective-permute-start | bytes 786440 | tf_op jit(solution)/shard_map/ppermute | solution.py:487
  53.1 6.5 %collective-permute-start.8 = (bf16[128,1024]{1,0:T(8,128)(2,1)S(1)}, bf16[128,1024]{1,0:T(8,128)(2,1)S(1)}, u32[]{:S(2)}, u32[]{:S(2)}) collective-permute-start(bf16[128,1024]{1,0:T(8,128)(2,1)S(1)} %get-tuple-element.45), channel_id=1, source_target_pairs={{0,1},{1,0},{2,3},{3,2},{4,5},{5,4},{6,7},{7,6},{8,9},{9,8},{10,11... | collective-permute-start | bytes 786440 | tf_op jit(solution)/shard_map/ppermute | solution.py:487

commit v2 on v1

--- a/solution.py
+++ b/solution.py
@@ -12,14 +12,18 @@
 SPAN = 128
 LANES = 128
 EDGE = 8
-EXTRA = 16
+EXTRA = 8
 NORM_EPSILON = 1e-05
-CHUNKS = 2
+PIECES = 2
 VMEM_LIMIT = 8 * 1024 * 1024
 
 
 F32 = jnp.float32
 BF16 = jnp.bfloat16
+
+
+def plan_of(groups):
+    return (groups - groups // 2, groups // 2) if groups > 1 else (groups,)
 
 
 def silu(v):
@@ -78,7 +82,20 @@
     return silu(running)
 
 
-def state_kernel(c, taps, all_width, head_dim, groups, shards, own_columns, *refs):
+def state_kernel(which, first, taps, all_width, head_dim, groups, shards, own_columns, *refs):
+    chip = lax.axis_index("seq")
+    body = functools.partial(
+        block_state, first, taps, all_width, head_dim, groups, shards, own_columns
+    )
+    if which == "first":
+        pl.when(chip == 0)(lambda: body(*refs))
+    else:
+        operands = 2 * shards + 1
+        kept = refs[:operands] + refs[operands + 5 :]
+        pl.when(chip != 0)(lambda: body(*kept))
+
+
+def block_state(first, taps, all_width, head_dim, groups, shards, own_columns, *refs):
     recv_refs, halos = refs[: shards - 1], refs[shards - 1 : 2 * shards - 1]
     rows_ref, tok = refs[2 * shards - 1 : 2 * shards + 1]
     xc_ref, bcc_ref, own_ref, own_d_ref, send_ref = refs[2 * shards + 1 : 2 * shards + 6]
@@ -86,19 +103,31 @@
     position, sub = lax.axis_index("head"), lax.axis_index("sub")
     rows = own_columns.shape[0]
     width, bc_width = xc_ref.shape[1], bcc_ref.shape[1]
-    first_head = c * width // head_dim
-    columns = slice(c * width, (c + 1) * width)
-    bc_columns = slice(all_width + c * bc_width, all_width + (c + 1) * bc_width)
+    group_width = width // groups
+    piece = halos[0].shape[1]
+    pieces = all_width // piece
+    start, bc_start = first * group_width, first * 2 * STATE
+    first_head = start // head_dim
+    columns = slice(start, start + width)
+    bc_columns = slice(all_width + bc_start, all_width + bc_start + bc_width)
     wx, bx = rows_ref[:taps, columns], rows_ref[taps : taps + 1, columns]
     wbc, bbc = rows_ref[:taps, bc_columns], rows_ref[taps : taps + 1, bc_columns]
     span = SPAN
-    edge = halos[0][:, columns].astype(F32)
-    edge_bc = halos[0][:, bc_columns].astype(F32)
-    for ref in halos[1:]:
-        edge = edge + ref[:, columns].astype(F32)
-        edge_bc = edge_bc + ref[:, bc_columns].astype(F32)
-    joined[:EDGE, :width] = edge
-    joined[:EDGE, width:] = edge_bc
+    halo = halos[0][...].astype(F32)
+    for j in range(1, shards):
+        halo = jnp.where(lax.rem(position + 1, shards) == j, halos[j][...].astype(F32), halo)
+    halo = jnp.where(lax.axis_index("seq") + sub == 0, 0.0, halo)
+    for r in range(taps - 1):
+        at = slice(EDGE - taps + 1 + r, EDGE - taps + 2 + r)
+        for q in range(pieces):
+            low, high = max(start, q * piece), min(start + width, (q + 1) * piece)
+            if low < high:
+                line = r * (pieces + 1) + q
+                joined[at, low - start : high - start] = halo[
+                    line : line + 1, low - q * piece : high - q * piece
+                ]
+        line = r * (pieces + 1) + pieces
+        joined[at, width:] = halo[line : line + 1, bc_start : bc_start + bc_width]
     at = pl.multiple_of(EDGE + position * rows, EDGE)
     joined[pl.ds(at, rows), :width] = own_columns[:, columns].astype(F32)
     joined[pl.ds(at, rows), width:] = own_columns[:, bc_columns].astype(F32)
@@ -122,7 +151,6 @@
         factor = widen_pair(to_end, head, head_dim, lane)
         scaled[:, lanes] = (factor * xc.astype(F32)).astype(BF16)
         full_d[:, lanes] = widen_pair(last, head, head_dim, lane_few)
-    group_width = width // groups
     for g in range(groups):
         b_in = bcc_ref[:, g * 2 * STATE : g * 2 * STATE + STATE].astype(F32)
         lanes = slice(g * group_width, (g + 1) * group_width)
@@ -130,18 +158,10 @@
     half = width // 2
     mine = pl.ds(pl.multiple_of(sub * half, LANES), half)
     other = pl.ds(pl.multiple_of((1 - sub) * half, LANES), half)
-    own_ref[...] = full[:, mine].astype(BF16)
+    own_ref[...] = full[:, mine]
     own_d_ref[...] = full_d[EDGE - 1 :, mine]
     send_ref[:STATE, :] = full[:, other].astype(BF16)
-    d = full_d[EDGE - 1 :, other]
-    high = d.astype(BF16)
-    middle = (d - high.astype(F32)).astype(BF16)
-    low = (d - high.astype(F32) - middle.astype(F32)).astype(BF16)
-    row = lax.broadcasted_iota(jnp.int32, (EXTRA, half), 0)
-    parts = jnp.where(row == 0, high.astype(F32), 0.0)
-    parts = jnp.where(row == 1, middle.astype(F32), parts)
-    parts = jnp.where(row == 2, low.astype(F32), parts)
-    send_ref[STATE:, :] = parts.astype(BF16)
+    put_decay(send_ref, full_d[EDGE - 1 :, other])
 
 
 def intra_kernel(first_head, head_dim, groups, xc_ref, bcc_ref, tok, heads_ref, by_head, y_ref):
@@ -182,11 +202,12 @@
             y_ref[:, lanes] = (y + skip * wide).astype(y_ref.dtype)
 
 
-def finish_kernel(c, gain_row, head_dim, groups, y_ref, bcc_ref, tok, mine, other, rows_ref, *refs):
+def finish_kernel(first, gain_row, head_dim, groups, y_ref, bcc_ref, tok, mine, other, rows_ref, *refs):
     out_ref, carried, scratch, normed, sems = refs[-5:]
     span, width = y_ref.shape
-    first_head = c * width // head_dim
-    gain = rows_ref[gain_row : gain_row + 1, c * width : (c + 1) * width]
+    start = first * (width // groups)
+    first_head = start // head_dim
+    gain = rows_ref[gain_row : gain_row + 1, start : start + width]
     copies = []
     half = width // 2
     sub = lax.axis_index("sub")
@@ -213,7 +234,7 @@
             here = slice(j * LANES, (j + 1) * LANES)
             there = slice(g * group_width + j * LANES, g * group_width + (j + 1) * LANES)
             normed[:, there] = (scratch[:, here] * factor * gain[:, there]).astype(BF16)
-        target = slice(c * width + g * group_width, c * width + (g + 1) * group_width)
+        target = slice(start + g * group_width, start + (g + 1) * group_width)
         copies.append(
             pltpu.make_async_copy(normed.at[:, lanes], out_ref.at[0, :, target], sems.at[g])
         )
@@ -230,97 +251,141 @@
         copy.wait()
 
 
-def pack_kernel(k, shards, parts, *refs):
-    sources, out, sems = refs[: len(parts)], refs[-2], refs[-1]
-    target = lax.rem(lax.axis_index("head") + k, shards)
+def columns_for(target, sources, out, parts):
     pairs = []
     column = 0
     for source, (stride, offset, count) in zip(sources, parts):
         start = pl.multiple_of(target * stride + offset, LANES)
         pairs.append((source.at[0, :, pl.ds(start, count)], out.at[:, pl.ds(column, count)]))
         column += count
-    copy_all(pairs, sems)
-
-
-def tails_kernel(width, bc_width, x_ref, bc_ref, *refs):
+    return pairs
+
+
+def pack_kernel(shards, parts, x_ref, bc_ref, *refs):
     *outs, sems = refs
-    last = pl.ds(x_ref.shape[1] - EDGE, EDGE)
+    position = lax.axis_index("head")
     pairs = []
     for k, out in enumerate(outs):
-        pairs.append(
-            (x_ref.at[0, last, pl.ds(k * width, width)], out.at[:, pl.ds(0, width)])
-        )
-        pairs.append(
-            (bc_ref.at[0, last, pl.ds(k * bc_width, bc_width)], out.at[:, pl.ds(width, bc_width)])
-        )
+        target = lax.rem(position + k + 1, shards)
+        pairs += columns_for(target, (x_ref, bc_ref), out, parts)
     copy_all(pairs, sems)
 
 
-def partner_decay(got):
-    rows = got[STATE:, :].astype(F32)
+def tails_kernel(count, width, bc_width, x_ref, bc_ref, *refs):
+    *outs, x_tail, bc_tail, sems = refs
+    last = pl.ds(x_ref.shape[1] - EDGE, EDGE)
+    copy_all([(x_ref.at[0, last, :], x_tail), (bc_ref.at[0, last, :], bc_tail)], sems)
+    pieces = width // bc_width
+    for j, out in enumerate(outs):
+        k = (j + len(outs) - 1) % len(outs)
+        lines = []
+        for r in range(EDGE - count, EDGE):
+            for q in range(pieces):
+                at = k * width + q * bc_width
+                lines.append(x_tail[:, at : at + bc_width].astype(F32)[r : r + 1, :])
+            lines.append(bc_tail[:, k * bc_width : (k + 1) * bc_width].astype(F32)[r : r + 1, :])
+        blank = jnp.zeros((out.shape[0] - len(lines), bc_width), F32)
+        out[...] = jnp.concatenate(lines + [blank], axis=0).astype(BF16)
+
+
+def put_decay(ref, decay):
+    high = decay.astype(BF16).astype(F32)
+    middle = (decay - high).astype(BF16).astype(F32)
+    low = decay - high - middle
+    row = lax.broadcasted_iota(jnp.int32, (EXTRA, decay.shape[1]), 0)
+    parts = jnp.where(row == 0, high, 0.0)
+    parts = jnp.where(row == 1, middle, parts)
+    parts = jnp.where(row == 2, low, parts)
+    ref[STATE:, :] = parts.astype(BF16)
+
+
+def get_decay(ref):
+    rows = ref[STATE:, :].astype(F32)
     return rows[0:1, :] + rows[1:2, :] + rows[2:3, :]
 
 
-def join_kernel(own, own_d, got, total, decay):
+def get_state(ref):
+    return ref[:STATE, :].astype(F32)
+
+
+def join_kernel(own, own_d, got, decay, *totals):
+    join_states(own, own_d, got, *totals)
+    decay[...] = own_d[...] * get_decay(got)
+
+
+def join_states(own, own_d, got, *totals):
     sub = lax.axis_index("sub")
-    other_d = partner_decay(got)
-    decay[...] = own_d[...] * other_d
+    other_d = get_decay(got)
+    step = own.shape[1] // len(totals)
 
     @pl.when(sub == 0)
     def _():
-        total[...] = (other_d * own[...].astype(F32) + got[:STATE, :].astype(F32)).astype(BF16)
+        for n, total in enumerate(totals):
+            at = slice(n * step, (n + 1) * step)
+            first, second = own[:, at], got[:STATE, at].astype(F32)
+            total[...] = (other_d[:, at] * first + second).astype(BF16)
 
     @pl.when(sub != 0)
     def _():
-        total[...] = (own_d[...] * got[:STATE, :].astype(F32) + own[...].astype(F32)).astype(BF16)
-
-
-def relay_kernel(arrived, total, decay, out):
-    out[...] = (decay[...] * arrived[...].astype(F32) + total[...].astype(F32)).astype(BF16)
-
-
-def close_kernel(own, own_d, got, *refs):
-    *arrived, mine, theirs, entry = refs
-    chip, sub = lax.axis_index("seq"), lax.axis_index("sub")
+        for n, total in enumerate(totals):
+            at = slice(n * step, (n + 1) * step)
+            first, second = got[:STATE, at].astype(F32), own[:, at]
+            total[...] = (own_d[:, at] * first + second).astype(BF16)
+
+
+def hop_kernel(n, total, decay, arrived, out):
+    step = total.shape[1]
+    here = decay[:, n * step : (n + 1) * step]
+    out[...] = (here * arrived[...].astype(F32) + total[...].astype(F32)).astype(BF16)
+
+
+def enter_blocks(own, own_d, got, final, mine, theirs):
+    sub = lax.axis_index("sub")
+
+    @pl.when(sub == 0)
+    def _():
+        mine[...] = final[...].astype(BF16)
+        theirs[...] = (own_d[...] * final[...] + own[...]).astype(BF16)
+
+    @pl.when(sub != 0)
+    def _():
+        theirs[...] = final[...].astype(BF16)
+        mine[...] = (get_decay(got) * final[...] + get_state(got)).astype(BF16)
+
+
+def pick_kernel(pieces, own, own_d, got, *refs):
+    *arrived, mine, theirs, final = refs
+    chip = lax.axis_index("seq")
+    step = own.shape[1] // pieces
 
     @pl.when(chip == 0)
     def _():
-        entry[...] = jnp.zeros_like(entry)
-
-    for step, ref in enumerate(arrived):
-
-        @pl.when(chip == step + 1)
+        final[...] = jnp.zeros_like(final)
+
+    for hop in range(len(arrived) // pieces):
+
+        @pl.when(chip == hop + 1)
         def _():
-            entry[...] = ref[...]
-
-    @pl.when(sub == 0)
-    def _():
-        mine[...] = entry[...]
-        theirs[...] = (own_d[...] * entry[...].astype(F32) + own[...].astype(F32)).astype(BF16)
-
-    @pl.when(sub != 0)
-    def _():
-        theirs[...] = entry[...]
-        mine[...] = (
-            partner_decay(got) * entry[...].astype(F32) + got[:STATE, :].astype(F32)
-        ).astype(BF16)
-
-
-def prep_kernel(x_ref, bc_ref, wx, bx, wbc, bbc, gain, offset, a_log, skip, *refs):
-    own_ref, rows_ref, heads_ref, sems = refs
+            for n in range(pieces):
+                final[:, n * step : (n + 1) * step] = arrived[hop * pieces + n][...].astype(F32)
+
+    enter_blocks(own, own_d, got, final, mine, theirs)
+
+
+def prep_kernel(
+    shards, parts, x_ref, bc_ref, wx, bx, wbc, bbc, gain, offset, a_log, skip, *refs
+):
+    own_ref, rows_ref, heads_ref, *outs, sems = refs
     taps, width = wx.shape
     bc_width = wbc.shape[1]
     position = lax.axis_index("head")
-    x_at = pl.multiple_of(position * width, LANES)
-    bc_at = pl.multiple_of(position * bc_width, LANES)
-    copies = [
-        pltpu.make_async_copy(
-            x_ref.at[0, :, pl.ds(x_at, width)], own_ref.at[:, pl.ds(0, width)], sems.at[0]
-        ),
-        pltpu.make_async_copy(
-            bc_ref.at[0, :, pl.ds(bc_at, bc_width)], own_ref.at[:, pl.ds(width, bc_width)], sems.at[1]
-        ),
-    ]
+    sources = (x_ref, bc_ref)
+    pairs = []
+    for n, out in enumerate(outs):
+        target = lax.rem(position + 1 + n % (shards - 1), shards)
+        pairs += columns_for(target, sources, out, parts[n // (shards - 1)])
+    pairs += columns_for(position, sources, own_ref, ((width, 0, width), (bc_width, 0, bc_width)))
+    copies = [pltpu.make_async_copy(a, b, sems.at[n]) for n, (a, b) in enumerate(pairs)]
     for copy in copies:
         copy.start()
     rows_ref[:taps, :width] = wx[...]
@@ -356,9 +421,11 @@
     heads = a_log.shape[0]
     head_dim = width // heads
     groups = bc_width // (2 * STATE)
-    chunks = min(CHUNKS, groups)
-    cw, cb, cg, ch = width // chunks, bc_width // chunks, groups // chunks, heads // chunks
-    half = cw // 2
+    group_width = width // groups
+    plan = plan_of(groups)
+    chunks = len(plan)
+    counts = list(plan)
+    firsts = [sum(counts[:c]) for c in range(chunks)]
     row = lambda a: a.reshape(1, a.shape[0])
     hbm = pl.BlockSpec(memory_space=pltpu.HBM)
     anywhere = pl.BlockSpec(memory_space=pl.ANY)
@@ -381,26 +448,25 @@
     x_here = pltpu.with_memory_space_constraint(x_raw, pltpu.HBM)
     bc_here = pltpu.with_memory_space_constraint(bc_raw, pltpu.HBM)
 
-    def send_chunk(c):
-        received = []
-        for k in range(1, shards):
-            (packed,) = call(
-                functools.partial(
-                    pack_kernel, k, shards, ((width, c * cw, cw), (bc_width, c * cb, cb))
-                ),
-                (x_here, bc_here),
-                [pltpu.VMEM((rows, cw + cb), BF16)],
-                [pltpu.SemaphoreType.DMA((2,))],
-                specs=[hbm] * 2,
-            )
-            received.append(lax.ppermute(packed, "head", shift(k)))
-        return received
-
-    dt_recv = [lax.ppermute(dt_raw[0], "head", shift(k)) for k in range(1, shards)]
-    recvs = [send_chunk(c) for c in range(chunks)]
-    taps = conv_x_weight.shape[0]
-    own_columns, rows_table, heads_table = call(
-        prep_kernel,
+    def parts_of(c):
+        return (
+            (width, firsts[c] * group_width, counts[c] * group_width),
+            (bc_width, firsts[c] * 2 * STATE, counts[c] * 2 * STATE),
+        )
+
+    def payload(c):
+        return pltpu.VMEM((rows, counts[c] * (group_width + 2 * STATE)), BF16)
+
+    others = shards - 1
+    packed = call(
+        functools.partial(pack_kernel, shards, parts_of(0)),
+        (x_here, bc_here),
+        [payload(0)] * others,
+        [pltpu.SemaphoreType.DMA((2 * others,))],
+        specs=[hbm] * 2,
+    )
+    own_columns, rows_table, heads_table, *later = call(
+        functools.partial(prep_kernel, shards, [parts_of(c) for c in range(1, chunks)]),
         (
             x_here,
             bc_here,
@@ -417,25 +483,41 @@
             pltpu.VMEM((rows, width + bc_width), BF16),
             pltpu.VMEM((8, width + bc_width), F32),
             pltpu.VMEM((8, heads), F32),
+        ]
+        + [payload(c) for c in range(1, chunks) for _ in range(others)],
+        [pltpu.SemaphoreType.DMA((2 + 2 * others * (chunks - 1),))],
+        specs=[hbm] * 2 + [vmem] * 8,
+    )
+    packed = list(packed) + later
+    dt_recv = [lax.ppermute(dt_raw[0], "head", shift(k)) for k in range(1, shards)]
+    recvs = [
+        [lax.ppermute(packed[c * others + k - 1], "head", shift(k)) for k in range(1, shards)]
+        for c in range(chunks)
+    ]
+
+    def following(j):
+        return [
+            ((b * shards + h) * 2 + t, (n // 2 * shards + (h + j) % shards) * 2 + n % 2)
+            for b in range(chips)
+            for t in range(2)
+            for h in range(shards)
+            for n in [(2 * b + t + 1) % (2 * chips)]
+        ]
+
+    taps = conv_x_weight.shape[0]
+    lines = (taps - 1) * (width // bc_width + 1)
+    tails = call(
+        functools.partial(tails_kernel, taps - 1, width, bc_width),
+        (x_here, bc_here),
+        [pltpu.VMEM((-(-lines // 16) * 16, bc_width), BF16)] * shards,
+        [
+            pltpu.VMEM((EDGE, x_raw.shape[2]), BF16),
+            pltpu.VMEM((EDGE, bc_raw.shape[2]), BF16),
+            pltpu.SemaphoreType.DMA((2,)),
         ],
-        [pltpu.SemaphoreType.DMA((2,))],
-        specs=[hbm] * 2 + [vmem] * 8,
-    )
-
-    following = lambda k: [
-        ((b * shards + shards - 1) * 2 + s, ((b + s) * shards + k) * 2 + 1 - s)
-        for b in range(chips)
-        for s in range(2)
-        if b + s < chips
-    ]
-    tails = call(
-        functools.partial(tails_kernel, width, bc_width),
-        (x_here, bc_here),
-        [pltpu.VMEM((EDGE, width + bc_width), BF16)] * shards,
-        [pltpu.SemaphoreType.DMA((2 * shards,))],
         specs=[hbm] * 2,
     )
-    halos = [lax.ppermute(tails[k], ("seq", "head", "sub"), following(k)) for k in range(shards)]
+    halos = [lax.ppermute(tails[j], ("seq", "head", "sub"), following(j)) for j in range(shards)]
 
     tok, by_head = call(
         functools.partial(tables_kernel, heads),
@@ -444,14 +526,18 @@
         [pltpu.VMEM((SPAN, dt_raw.shape[2]), F32)],
     )
 
-    def state(c):
+    def state(c, which, before=()):
+        cw, cb = counts[c] * group_width, counts[c] * 2 * STATE
+        half = cw // 2
         return call(
-            functools.partial(state_kernel, c, taps, width, head_dim, cg, shards),
-            (own_columns, *recvs[c], *halos, rows_table, tok),
+            functools.partial(
+                state_kernel, which, firsts[c], taps, width, head_dim, counts[c], shards
+            ),
+            (own_columns, *recvs[c], *halos, rows_table, tok, *before),
             [
                 pltpu.VMEM((SPAN, cw), BF16),
                 pltpu.VMEM((SPAN, cb), BF16),
-                pltpu.VMEM((STATE, half), BF16),
+                pltpu.VMEM((STATE, half), F32),
                 pltpu.VMEM((1, half), F32),
                 pltpu.VMEM((STATE + EXTRA, half), BF16),
             ],
@@ -461,49 +547,68 @@
                 pltpu.VMEM((STATE, cw), F32),
                 pltpu.VMEM((EDGE, cw), F32),
             ],
+            aliases={2 * shards + 2 + n: n for n in range(len(before))},
         )
 
-    def chain(own, own_d, send):
+    def lead(c):
+        results = state(c, "first")
+        own, own_d, send = results[2:]
         got = lax.ppermute(send, "sub", [(0, 1), (1, 0)])
-        state_shape = pltpu.VMEM((STATE, half), BF16)
-        total, decay = call(
-            join_kernel, (own, own_d, got), [state_shape, pltpu.VMEM((1, half), F32)]
+        half = counts[c] * group_width // 2
+        pieces = pieces_of(half, chips)
+        totals = call(
+            join_states, (own, own_d, got), [pltpu.VMEM((STATE, half // pieces), BF16)] * pieces
         )
-        running = total
+        return totals, state(c, "rest", results)
+
+    def carry(c, own, own_d, send, first_totals):
+        half = counts[c] * group_width // 2
+        pieces = pieces_of(half, chips)
+        whole = pltpu.VMEM((STATE, half), F32)
+        rounded = pltpu.VMEM((STATE, half), BF16)
+        piece = pltpu.VMEM((STATE, half // pieces), BF16)
+        got = lax.ppermute(send, "sub", [(0, 1), (1, 0)])
+        decay, *totals = call(
+            join_kernel, (own, own_d, got), [pltpu.VMEM((1, half), F32)] + [piece] * pieces
+        )
+        held = list(first_totals)
         arrived = []
-        for step in range(chips - 1):
-            pairs = [(step, step + 1)]
-            if step == 0 and chips % 2 == 0:
-                pairs = [(i, i ^ 1) for i in range(chips)]
-            arrived.append(lax.ppermute(running, "seq", pairs))
-            if step < chips - 2:
-                (running,) = call(relay_kernel, (arrived[-1], total, decay), [state_shape])
+        for hop in range(chips - 1):
+            for n in range(pieces):
+                arrived.append(lax.ppermute(held[n], "seq", [(hop, hop + 1)]))
+                if hop < chips - 2:
+                    (held[n],) = call(
+                        functools.partial(hop_kernel, n), (totals[n], decay, arrived[-1]), [piece]
+                    )
         mine, theirs = call(
-            close_kernel,
+            functools.partial(pick_kernel, pieces),
             (own, own_d, got, *arrived),
-            [state_shape] * 2,
-            [pltpu.VMEM((STATE, half), BF16)],
+            [rounded] * 2,
+            [whole],
         )
         return mine, lax.ppermute(theirs, "sub", [(0, 1), (1, 0)])
 
     def intra(c, xc, bcc):
         return call(
-            functools.partial(intra_kernel, c * ch, head_dim, cg),
+            functools.partial(
+                intra_kernel, firsts[c] * group_width // head_dim, head_dim, counts[c]
+            ),
             (xc, bcc, tok, by_head, heads_table),
-            [pltpu.VMEM((SPAN, cw), BF16)],
+            [pltpu.VMEM((SPAN, counts[c] * group_width), F32)],
         )[0]
 
     def finish(c, y, bcc, mine, theirs, out):
         before = [] if out is None else [out]
+        cw = counts[c] * group_width
         return call(
-            functools.partial(finish_kernel, c, taps + 1, head_dim, cg),
+            functools.partial(finish_kernel, firsts[c], taps + 1, head_dim, counts[c]),
             (y, bcc, tok, mine, theirs, rows_table, *before),
             [jax.ShapeDtypeStruct((1, SPAN, width), BF16)],
             [
                 pltpu.VMEM((STATE, cw), BF16),
-                pltpu.VMEM((SPAN, cw // cg), F32),
+                pltpu.VMEM((SPAN, group_width), F32),
                 pltpu.VMEM((SPAN, cw), BF16),
-                pltpu.SemaphoreType.DMA((cg,)),
+                pltpu.SemaphoreType.DMA((counts[c],)),
             ],
             specs=[vmem] * 6 + [anywhere] * len(before),
             out_specs=[anywhere],
@@ -512,13 +617,18 @@
 
     parts = []
     for c in range(chunks):
-        xc, bcc, own, own_d, send = state(c)
-        mine, theirs = chain(own, own_d, send)
+        first_totals, results = lead(c)
+        xc, bcc, own, own_d, send = results
+        mine, theirs = carry(c, own, own_d, send, first_totals)
         parts.append((intra(c, xc, bcc), bcc, mine, theirs))
     out = None
     for c in range(chunks):
         out = finish(c, *parts[c], out)
     return out
+
+
+def pieces_of(half, chips):
+    return PIECES if half % (PIECES * LANES) == 0 and chips <= 8 else 1
 
 
 def solution(mesh):

time: 61.6 us -> 59.9 us (0.972)
  the two profiles are of different devices: /device:TPU:25 before, /device:TPU:27 now
where the time goes in v2:
time: 59.9 us; the launch traced here: 59.5 us
  waiting for transfers between devices  22.1 us (37%)
  starting transfers between devices  21.5 us (36%)
  Pallas kernels  14.7 us (25%)
  local copies, waits for them, and re-layouts  0.68 us (1%)
    pallas_call x26, Pallas kernels, call(): pl.pallas_call(kernel, in_specs=specs or [vmem] * len(operands), out_spec...  14.7 us
    ppermute x12, waiting for transfers between devices, carry(): arrived.append(lax.ppermute(held[n], 'seq', [(hop, hop + 1)]))  10.9 us
    ppermute x12, starting transfers between devices, carry(): arrived.append(lax.ppermute(held[n], 'seq', [(hop, hop + 1)]))  10.5 us
    ppermute x1, waiting for transfers between devices, on_device(): lax.ppermute(dt_raw[0], 'head', shift(k))  9.47 us
    ppermute x2, starting transfers between devices, carry(): return (mine, lax.ppermute(theirs, 'sub', [(0, 1), (1, 0)]))  4.9 us
    ppermute x2, starting transfers between devices, on_device(): lax.ppermute(packed[c * others + k - 1], 'head', shift(k))  1.6 us
    ppermute x2, starting transfers between devices, lead(): got = lax.ppermute(send, 'sub', [(0, 1), (1, 0)])  1.47 us
    ppermute x1, starting transfers between devices, on_device(): lax.ppermute(dt_raw[0], 'head', shift(k))  1.24 us
  transfers between devices with their start and end apart: 23, of which 6 were waited for; matrix products, arithmetic and copies ran while one was open for 0% of the time, Pallas kernels for 20%

profile of v2, /device:TPU:27, one launch (start us, length us, event | category | flops | bytes accessed | tf_op | source)
XLA Modules:
  0.0 59.5 jit_solution(1148946262908259356)
XLA Ops:
  0.0 1.0 %shard_map.122 = bf16[64,2560]{1,0:T(8,128)(2,1)S(1)} custom-call(bf16[1,64,8192]{2,1,0:T(8,128)(2,1)} %x_ref.5, bf16[1,64,2048]{2,1,0:T(8,128)(2,1)} %bc_ref.5), custom_call_target="tpu_custom_call" | custom-call | tf_op jit(solution)/shard_map/pallas_call | solution.py:435
  1.1 0.3 collective-permute-start.13
  1.4 0.6 %copy-done.5 = f32[1024]{0:T(1024)S(1)} copy-done((f32[1024]{0:T(1024)S(1)}, f32[1024]{0:T(1024)}, u32[]{:S(2)}) %copy-start.5) | copy-done | bytes 4120
  2.1 0.0 copy-done.8
  2.1 1.2 %shard_map.109 = (bf16[64,5120]{1,0:T(8,128)(2,1)S(1)}, f32[8,5120]{1,0:T(8,128)S(1)}, f32[8,64]{1,0:T(8,128)S(1)}, bf16[64,2560]{1,0:T(8,128)(2,1)S(1)}) custom-call(bf16[1,64,8192]{2,1,0:T(8,128)(2,1)} %x_ref.5, bf16[1,64,2048]{2,1,0:T(8,128)(2,1)} %bc_ref.5, f32[4,4096]{1,0:T(4,128)S(1)} %copy-done, f32[1,4096]{1,0:T(1,128)S(1)} %bitcast.7, ...), custom_call_target="tpu_custom_call" | custom-call | tf_op jit(solution)/shard_map/pallas_call | solution.py:435
  3.3 0.0 copy-start.4
  3.3 1.3 %collective-permute-start = (bf16[64,2560]{1,0:T(8,128)(2,1)S(1)}, bf16[64,2560]{1,0:T(8,128)(2,1)S(1)}, u32[]{:S(2)}, u32[]{:S(2)}) collective-permute-start(bf16[64,2560]{1,0:T(8,128)(2,1)S(1)} %get-tuple-element.48), channel_id=1, source_target_pairs={{0,2},{2,0},{1,3},{3,1},{4,6},{6,4},{5,7},{7,5},{8,10},{10,8},{9,1... | collective-permute-start | bytes 983048 | tf_op jit(solution)/shard_map/ppermute | solution.py:494
  4.6 1.0 %shard_map.110 = (bf16[16,1024]{1,0:T(8,128)(2,1)S(1)}, bf16[16,1024]{1,0:T(8,128)(2,1)S(1)}) custom-call(bf16[1,64,8192]{2,1,0:T(8,128)(2,1)} %x_ref.5, bf16[1,64,2048]{2,1,0:T(8,128)(2,1)} %bc_ref.5), custom_call_target="tpu_custom_call" | custom-call | tf_op jit(solution)/shard_map/pallas_call | solution.py:435
  5.6 1.1 %collective-permute-start.1 = (bf16[16,1024]{1,0:T(8,128)(2,1)S(1)}, bf16[16,1024]{1,0:T(8,128)(2,1)S(1)}, u32[]{:S(2)}, u32[]{:S(2)}) collective-permute-start(bf16[16,1024]{1,0:T(8,128)(2,1)S(1)} %get-tuple-element.49), channel_id=1, source_target_pairs={{0,1},{2,3},{1,4},{3,6},{4,5},{6,7},{5,8},{7,10},{8,9},{10,11},{9,... | collective-permute-start | bytes 98312 | tf_op jit(solution)/shard_map/ppermute | solution.py:520
  6.7 0.0 collective-permute-start.2
  6.7 1.2 %collective-permute-start.3 = (bf16[64,128]{1,0:T(8,128)(2,1)S(1)}, bf16[64,128]{1,0:T(8,128)(2,1)S(1)}, u32[]{:S(2)}, u32[]{:S(2)}) collective-permute-start(bf16[64,128]{1,0:T(8,128)(2,1)S(1)} %bitcast.9), channel_id=1, source_target_pairs={{0,2},{2,0},{1,3},{3,1},{4,6},{6,4},{5,7},{7,5},{8,10},{10,8},{9,1... | collective-permute-start | bytes 49160 | tf_op jit(solution)/shard_map/ppermute | solution.py:492
  8.0 9.5 %collective-permute-done.3.refs_0_ = bf16[64,128]{1,0:T(8,128)(2,1)S(1)} collective-permute-done((bf16[64,128]{1,0:T(8,128)(2,1)S(1)}, bf16[64,128]{1,0:T(8,128)(2,1)S(1)}, u32[]{:S(2)}, u32[]{:S(2)}) %collective-permute-start.3) | collective-permute-done | bytes 16416 | tf_op jit(solution)/shard_map/ppermute | solution.py:492
  17.4 0.4 shard_map.111
  17.8 0.6 %collective-permute-done.2.refs_2_ = bf16[16,1024]{1,0:T(8,128)(2,1)S(1)} collective-permute-done((bf16[16,1024]{1,0:T(8,128)(2,1)S(1)}, bf16[16,1024]{1,0:T(8,128)(2,1)S(1)}, u32[]{:S(2)}, u32[]{:S(2)}) %collective-permute-start.2) | collective-permute-done | bytes 32800 | tf_op jit(solution)/shard_map/ppermute | solution.py:520
  18.5 1.4 %collective-permute-start.15 = (bf16[136,1024]{1,0:T(8,128)(2,1)S(1)}, bf16[136,1024]{1,0:T(8,128)(2,1)S(1)}, u32[]{:S(2)}, u32[]{:S(2)}) collective-permute-start(bf16[136,1024]{1,0:T(8,128)(2,1)S(1)} %get-tuple-element.76.refs_9_), channel_id=1, source_target_pairs={{0,1},{1,0},{2,3},{3,2},{4,5},{5,4},{6,7},{7,6},{8,9},{9,8},{10,11... | collective-permute-start | bytes 835592 | tf_op jit(solution)/shard_map/ppermute | solution.py:556
  19.8 0.1 collective-permute-start.5
  19.9 1.1 %collective-permute-done.15.got = bf16[136,1024]{1,0:T(8,128)(2,1)S(1)} collective-permute-done((bf16[136,1024]{1,0:T(8,128)(2,1)S(1)}, bf16[136,1024]{1,0:T(8,128)(2,1)S(1)}, u32[]{:S(2)}, u32[]{:S(2)}) %collective-permute-start.15) | collective-permute-done | bytes 278560 | tf_op jit(solution)/shard_map/ppermute | solution.py:556
  21.0 0.1 shard_map.126
  21.1 2.3 %shard_map.124 = (bf16[128,2048]{1,0:T(8,128)(2,1)S(1)}, bf16[128,512]{1,0:T(8,128)(2,1)S(1)}, f32[128,1024]{1,0:T(8,128)S(1)}, f32[1,1024]{1,0:T(1,128)S(1)}, bf16[136,1024]{1,0:T(8,128)(2,1)S(1)}) custom-call(bf16[64,5120]{1,0:T(8,128)(2,1)S(1)} %get-tuple-element.47.own_columns, ...), custom_call_target="tpu_custom_call", output_to_operand_aliasing={{0}: (6, {}), {1}: (7, {}), {2}: (8, {}), {3}: (9, {}), {4}... | custom-call | tf_op jit(solution)/shard_map/pallas_call | solution.py:435
  23.4 0.4 collective-permute-start.14
  23.8 0.1 shard_map.115
  23.9 2.3 %shard_map.113 = (bf16[128,2048]{1,0:T(8,128)(2,1)S(1)}, bf16[128,512]{1,0:T(8,128)(2,1)S(1)}, f32[128,1024]{1,0:T(8,128)S(1)}, f32[1,1024]{1,0:T(1,128)S(1)}, bf16[136,1024]{1,0:T(8,128)(2,1)S(1)}) custom-call(bf16[64,5120]{1,0:T(8,128)(2,1)S(1)} %get-tuple-element.47.own_columns, ...), custom_call_target="tpu_custom_call", output_to_operand_aliasing={{0}: (6, {}), {1}: (7, {}), {2}: (8, {}), {3}: (9, {}), {4}... | custom-call | tf_op jit(solution)/shard_map/pallas_call | solution.py:435
  26.2 0.2 collective-permute-start.4
  26.4 0.7 %collective-permute-start.17 = (bf16[128,512]{1,0:T(8,128)(2,1)S(1)}, bf16[128,512]{1,0:T(8,128)(2,1)S(1)}, u32[]{:S(2)}, u32[]{:S(2)}) collective-permute-start(bf16[128,512]{1,0:T(8,128)(2,1)S(1)} %get-tuple-element.83), channel_id=1, source_target_pairs={{0,4},{1,5},{2,6},{3,7},{16,20},{17,21},{18,22},{19,23}} | collective-permute-start | bytes 393224 | tf_op jit(solution)/shard_map/ppermute | solution.py:578
  27.0 0.7 %collective-permute-start.16 = (bf16[128,512]{1,0:T(8,128)(2,1)S(1)}, bf16[128,512]{1,0:T(8,128)(2,1)S(1)}, u32[]{:S(2)}, u32[]{:S(2)}) collective-permute-start(bf16[128,512]{1,0:T(8,128)(2,1)S(1)} %get-tuple-element.82), channel_id=1, source_target_pairs={{0,4},{1,5},{2,6},{3,7},{16,20},{17,21},{18,22},{19,23}} | collective-permute-start | bytes 393224 | tf_op jit(solution)/shard_map/ppermute | solution.py:578
  27.7 0.7 %collective-permute-start.7 = (bf16[128,512]{1,0:T(8,128)(2,1)S(1)}, bf16[128,512]{1,0:T(8,128)(2,1)S(1)}, u32[]{:S(2)}, u32[]{:S(2)}) collective-permute-start(bf16[128,512]{1,0:T(8,128)(2,1)S(1)} %get-tuple-element.66), channel_id=1, source_target_pairs={{0,4},{1,5},{2,6},{3,7},{16,20},{17,21},{18,22},{19,23}} | collective-permute-start | bytes 393224 | tf_op jit(solution)/shard_map/ppermute | solution.py:578
  28.4 0.7 %collective-permute-start.6 = (bf16[128,512]{1,0:T(8,128)(2,1)S(1)}, bf16[128,512]{1,0:T(8,128)(2,1)S(1)}, u32[]{:S(2)}, u32[]{:S(2)}) collective-permute-start(bf16[128,512]{1,0:T(8,128)(2,1)S(1)} %get-tuple-element.65), channel_id=1, source_target_pairs={{0,4},{1,5},{2,6},{3,7},{16,20},{17,21},{18,22},{19,23}} | collective-permute-start | bytes 393224 | tf_op jit(solution)/shard_map/ppermute | solution.py:578
  29.1 0.1 shard_map.127
  29.2 0.7 %collective-permute-start.19 = (bf16[128,512]{1,0:T(8,128)(2,1)S(1)}, bf16[128,512]{1,0:T(8,128)(2,1)S(1)}, u32[]{:S(2)}, u32[]{:S(2)}) collective-permute-start(bf16[128,512]{1,0:T(8,128)(2,1)S(1)} %shard_map.129), channel_id=1, source_target_pairs={{4,8},{5,9},{6,10},{7,11},{20,24},{21,25},{22,26},{23,27}} | collective-permute-start | bytes 393224 | tf_op jit(solution)/shard_map/ppermute | solution.py:578
  30.0 0.7 %collective-permute-start.18 = (bf16[128,512]{1,0:T(8,128)(2,1)S(1)}, bf16[128,512]{1,0:T(8,128)(2,1)S(1)}, u32[]{:S(2)}, u32[]{:S(2)}) collective-permute-start(bf16[128,512]{1,0:T(8,128)(2,1)S(1)} %shard_map.128), channel_id=1, source_target_pairs={{4,8},{5,9},{6,10},{7,11},{20,24},{21,25},{22,26},{23,27}} | collective-permute-start | bytes 393224 | tf_op jit(solution)/shard_map/ppermute | solution.py:578
  30.7 0.1 shard_map.116
  30.8 0.7 %collective-permute-start.9 = (bf16[128,512]{1,0:T(8,128)(2,1)S(1)}, bf16[128,512]{1,0:T(8,128)(2,1)S(1)}, u32[]{:S(2)}, u32[]{:S(2)}) collective-permute-start(bf16[128,512]{1,0:T(8,128)(2,1)S(1)} %shard_map.118), channel_id=1, source_target_pairs={{4,8},{5,9},{6,10},{7,11},{20,24},{21,25},{22,26},{23,27}} | collective-permute-start | bytes 393224 | tf_op jit(solution)/shard_map/ppermute | solution.py:578
  31.6 0.7 %collective-permute-start.8 = (bf16[128,512]{1,0:T(8,128)(2,1)S(1)}, bf16[128,512]{1,0:T(8,128)(2,1)S(1)}, u32[]{:S(2)}, u32[]{:S(2)}) collective-permute-start(bf16[128,512]{1,0:T(8,128)(2,1)S(1)} %shard_map.117), channel_id=1, source_target_pairs={{4,8},{5,9},{6,10},{7,11},{20,24},{21,25},{22,26},{23,27}} | collective-permute-start | bytes 393224 | tf_op jit(solution)/shard_map/ppermute | solution.py:578
  32.3 1.3 %collective-permute-start.21 = (bf16[128,512]{1,0:T(8,128)(2,1)S(1)}, bf16[128,512]{1,0:T(8,128)(2,1)S(1)}, u32[]{:S(2)}, u32[]{:S(2)}) collective-permute-start(bf16[128,512]{1,0:T(8,128)(2,1)S(1)} %shard_map.131), channel_id=1, source_target_pairs={{8,12},{9,13},{10,14},{11,15},{24,28},{25,29},{26,30},{27,31}} | collective-permute-start | bytes 393224 | tf_op jit(solution)/shard_map/ppermute | solution.py:578
  33.7 1.3 %collective-permute-start.20 = (bf16[128,512]{1,0:T(8,128)(2,1)S(1)}, bf16[128,512]{1,0:T(8,128)(2,1)S(1)}, u32[]{:S(2)}, u32[]{:S(2)}) collective-permute-start(bf16[128,512]{1,0:T(8,128)(2,1)S(1)} %shard_map.130), channel_id=1, source_target_pairs={{8,12},{9,13},{10,14},{11,15},{24,28},{25,29},{26,30},{27,31}} | collective-permute-start | bytes 393224 | tf_op jit(solution)/shard_map/ppermute | solution.py:578
  35.0 1.3 %collective-permute-start.11 = (bf16[128,512]{1,0:T(8,128)(2,1)S(1)}, bf16[128,512]{1,0:T(8,128)(2,1)S(1)}, u32[]{:S(2)}, u32[]{:S(2)}) collective-permute-start(bf16[128,512]{1,0:T(8,128)(2,1)S(1)} %shard_map.120), channel_id=1, source_target_pairs={{8,12},{9,13},{10,14},{11,15},{24,28},{25,29},{26,30},{27,31}} | collective-permute-start | bytes 393224 | tf_op jit(solution)/shard_map/ppermute | solution.py:578
  36.4 1.3 %collective-permute-start.10 = (bf16[128,512]{1,0:T(8,128)(2,1)S(1)}, bf16[128,512]{1,0:T(8,128)(2,1)S(1)}, u32[]{:S(2)}, u32[]{:S(2)}) collective-permute-start(bf16[128,512]{1,0:T(8,128)(2,1)S(1)} %shard_map.119), channel_id=1, source_target_pairs={{8,12},{9,13},{10,14},{11,15},{24,28},{25,29},{26,30},{27,31}} | collective-permute-start | bytes 393224 | tf_op jit(solution)/shard_map/ppermute | solution.py:578
  37.7 2.9 %collective-permute-done.21.refs_5_ = bf16[128,512]{1,0:T(8,128)(2,1)S(1)} collective-permute-done((bf16[128,512]{1,0:T(8,128)(2,1)S(1)}, bf16[128,512]{1,0:T(8,128)(2,1)S(1)}, u32[]{:S(2)}, u32[]{:S(2)}) %collective-permute-start.21) | collective-permute-done | bytes 131104 | tf_op jit(solution)/shard_map/ppermute | solution.py:578
  40.6 5.0 %collective-permute-done.20.refs_4_ = bf16[128,512]{1,0:T(8,128)(2,1)S(1)} collective-permute-done((bf16[128,512]{1,0:T(8,128)(2,1)S(1)}, bf16[128,512]{1,0:T(8,128)(2,1)S(1)}, u32[]{:S(2)}, u32[]{:S(2)}) %collective-permute-start.20) | collective-permute-done | bytes 131104 | tf_op jit(solution)/shard_map/ppermute | solution.py:578
  45.7 0.3 shard_map.132
  46.0 3.6 %collective-permute-start.22 = (bf16[128,1024]{1,0:T(8,128)(2,1)S(1)}, bf16[128,1024]{1,0:T(8,128)(2,1)S(1)}, u32[]{:S(2)}, u32[]{:S(2)}) collective-permute-start(bf16[128,1024]{1,0:T(8,128)(2,1)S(1)} %get-tuple-element.88), channel_id=1, source_target_pairs={{0,1},{1,0},{2,3},{3,2},{4,5},{5,4},{6,7},{7,6},{8,9},{9,8},{10,11... | collective-permute-start | bytes 786440 | tf_op jit(solution)/shard_map/ppermute | solution.py:589
  49.6 2.9 %collective-permute-done.10.refs_4_ = bf16[128,512]{1,0:T(8,128)(2,1)S(1)} collective-permute-done((bf16[128,512]{1,0:T(8,128)(2,1)S(1)}, bf16[128,512]{1,0:T(8,128)(2,1)S(1)}, u32[]{:S(2)}, u32[]{:S(2)}) %collective-permute-start.10) | collective-permute-done | bytes 131104 | tf_op jit(solution)/shard_map/ppermute | solution.py:578
  52.4 0.1 shard_map.121
  52.6 1.3 %collective-permute-start.12 = (bf16[128,1024]{1,0:T(8,128)(2,1)S(1)}, bf16[128,1024]{1,0:T(8,128)(2,1)S(1)}, u32[]{:S(2)}, u32[]{:S(2)}) collective-permute-start(bf16[128,1024]{1,0:T(8,128)(2,1)S(1)} %get-tuple-element.71), channel_id=1, source_target_pairs={{0,1},{1,0},{2,3},{3,2},{4,5},{5,4},{6,7},{7,6},{8,9},{9,8},{10,11... | collective-permute-start | bytes 786440 | tf_op jit(solution)/shard_map/ppermute | solution.py:589
  53.9 0.9 %shard_map.125.y_ref = f32[128,2048]{1,0:T(8,128)S(1)} custom-call(bf16[128,2048]{1,0:T(8,128)(2,1)S(1)} %get-tuple-element.77.xc_ref, bf16[128,512]{1,0:T(8,128)(2,1)S(1)} %get-tuple-element.78.bcc_ref, f32[3,128,64]{2,1,0:T(8,128)S(1)} %get-tuple-element.53.refs_4_.tok, f32[2,64,128]{2,1,0:T(8,128)S(1)} %get-tuple-element.61.heads_ref, ...), custom_call_target="tpu_custom_call" | custom-call | tf_op jit(solution)/shard_map/pallas_call | solution.py:435
  54.9 0.9 %shard_map.114.y_ref = f32[128,2048]{1,0:T(8,128)S(1)} custom-call(bf16[128,2048]{1,0:T(8,128)(2,1)S(1)} %get-tuple-element.59.xc_ref, bf16[128,512]{1,0:T(8,128)(2,1)S(1)} %get-tuple-element.60.bcc_ref, f32[3,128,64]{2,1,0:T(8,128)S(1)} %get-tuple-element.53.refs_4_.tok, f32[2,64,128]{2,1,0:T(8,128)S(1)} %get-tuple-element.61.heads_ref, ...), custom_call_target="tpu_custom_call" | custom-call | tf_op jit(solution)/shard_map/pallas_call | solution.py:435
  55.8 1.7 %shard_map.133.refs_0_ = bf16[1,128,4096]{2,1,0:T(8,128)(2,1)} custom-call(f32[128,2048]{1,0:T(8,128)S(1)} %shard_map.125.y_ref, bf16[128,512]{1,0:T(8,128)(2,1)S(1)} %get-tuple-element.78.bcc_ref, f32[3,128,64]{2,1,0:T(8,128)S(1)} %get-tuple-element.53.refs_4_.tok, bf16[128,1024]{1,0:T(8,128)(2,1)S(1)} %get-tuple-element.87.mine, ...), custom_call_target="tpu_custom_call" | custom-call | tf_op jit(solution)/shard_map/pallas_call | solution.py:435
  57.6 1.7 %shard_map.134 = bf16[1,128,4096]{2,1,0:T(8,128)(2,1)} custom-call(f32[128,2048]{1,0:T(8,128)S(1)} %shard_map.114.y_ref, bf16[128,512]{1,0:T(8,128)(2,1)S(1)} %get-tuple-element.60.bcc_ref, f32[3,128,64]{2,1,0:T(8,128)S(1)} %get-tuple-element.53.refs_4_.tok, bf16[128,1024]{1,0:T(8,128)(2,1)S(1)} %get-tuple-element.70.mine, ...), custom_call_target="tpu_custom_call", output_to_operand_aliasing={{}: (6, {})} | custom-call | tf_op jit(solution)/shard_map/pallas_call | solution.py:435
  (42 shorter events, 0.4 us)
Async XLA Ops:
  0.0 1.4 %copy-start = (f32[4,4096]{1,0:T(4,128)S(1)}, f32[4,4096]{1,0:T(4,128)}, u32[]{:S(2)}) copy-start(f32[4,4096]{1,0:T(4,128)} %wx.1) | copy-start | bytes 196612
  0.0 1.4 %copy-start.1 = (f32[4096]{0:T(1024)S(1)}, f32[4096]{0:T(1024)}, u32[]{:S(2)}) copy-start(f32[4096]{0:T(1024)} %param.15) | copy-start | bytes 49156
  0.0 1.4 %copy-start.2 = (f32[4,1024]{1,0:T(4,128)S(1)}, f32[4,1024]{1,0:T(4,128)}, u32[]{:S(2)}) copy-start(f32[4,1024]{1,0:T(4,128)} %wbc.1) | copy-start | bytes 49156
  0.0 1.4 %copy-start.3 = (f32[4096]{0:T(1024)S(1)}, f32[4096]{0:T(1024)}, u32[]{:S(2)}) copy-start(f32[4096]{0:T(1024)} %param.21) | copy-start | bytes 49156
  1.1 17.4 %collective-permute-start.13 = (bf16[64,2560]{1,0:T(8,128)(2,1)S(1)}, bf16[64,2560]{1,0:T(8,128)(2,1)S(1)}, u32[]{:S(2)}, u32[]{:S(2)}) collective-permute-start(bf16[64,2560]{1,0:T(8,128)(2,1)S(1)} %shard_map.122), channel_id=1, source_target_pairs={{0,2},{2,0},{1,3},{3,1},{4,6},{6,4},{5,7},{7,5},{8,10},{10,8},{9,1... | collective-permute-start | bytes 983048 | tf_op jit(solution)/shard_map/ppermute | solution.py:494
  1.4 0.7 %copy-start.5 = (f32[1024]{0:T(1024)S(1)}, f32[1024]{0:T(1024)}, u32[]{:S(2)}) copy-start(f32[1024]{0:T(1024)} %param.17) | copy-start | bytes 12292
  1.4 0.7 %copy-start.6 = (f32[64]{0:T(128)S(1)}, f32[64]{0:T(128)}, u32[]{:S(2)}) copy-start(f32[64]{0:T(128)} %param.18) | copy-start | bytes 772
  1.4 0.7 %copy-start.7 = (f32[64]{0:T(128)S(1)}, f32[64]{0:T(128)}, u32[]{:S(2)}) copy-start(f32[64]{0:T(128)} %param.19) | copy-start | bytes 772
  1.4 0.7 %copy-start.8 = (f32[64]{0:T(128)S(1)}, f32[64]{0:T(128)}, u32[]{:S(2)}) copy-start(f32[64]{0:T(128)} %param.20) | copy-start | bytes 772
  3.3 3.4 %copy-start.4 = (bf16[1,64,128]{2,1,0:T(8,128)(2,1)S(1)}, bf16[1,64,128]{2,1,0:T(8,128)(2,1)}, u32[]{:S(2)}) copy-start(bf16[1,64,128]{2,1,0:T(8,128)(2,1)} %own_ref.1) | copy-start | bytes 49156
  3.3 16.5 %collective-permute-start = (bf16[64,2560]{1,0:T(8,128)(2,1)S(1)}, bf16[64,2560]{1,0:T(8,128)(2,1)S(1)}, u32[]{:S(2)}, u32[]{:S(2)}) collective-permute-start(bf16[64,2560]{1,0:T(8,128)(2,1)S(1)} %get-tuple-element.48), channel_id=1, source_target_pairs={{0,2},{2,0},{1,3},{3,1},{4,6},{6,4},{5,7},{7,5},{8,10},{10,8},{9,1... | collective-permute-start | bytes 983048 | tf_op jit(solution)/shard_map/ppermute | solution.py:494
  5.6 12.2 %collective-permute-start.1 = (bf16[16,1024]{1,0:T(8,128)(2,1)S(1)}, bf16[16,1024]{1,0:T(8,128)(2,1)S(1)}, u32[]{:S(2)}, u32[]{:S(2)}) collective-permute-start(bf16[16,1024]{1,0:T(8,128)(2,1)S(1)} %get-tuple-element.49), channel_id=1, source_target_pairs={{0,1},{2,3},{1,4},{3,6},{4,5},{6,7},{5,8},{7,10},{8,9},{10,11},{9,... | collective-permute-start | bytes 98312 | tf_op jit(solution)/shard_map/ppermute | solution.py:520
  6.7 11.7 %collective-permute-start.2 = (bf16[16,1024]{1,0:T(8,128)(2,1)S(1)}, bf16[16,1024]{1,0:T(8,128)(2,1)S(1)}, u32[]{:S(2)}, u32[]{:S(2)}) collective-permute-start(bf16[16,1024]{1,0:T(8,128)(2,1)S(1)} %get-tuple-element.50), channel_id=1, source_target_pairs={{0,3},{2,1},{1,6},{3,4},{4,7},{6,5},{5,10},{7,8},{8,11},{10,9},{9,... | collective-permute-start | bytes 98312 | tf_op jit(solution)/shard_map/ppermute | solution.py:520
  6.7 10.7 %collective-permute-start.3 = (bf16[64,128]{1,0:T(8,128)(2,1)S(1)}, bf16[64,128]{1,0:T(8,128)(2,1)S(1)}, u32[]{:S(2)}, u32[]{:S(2)}) collective-permute-start(bf16[64,128]{1,0:T(8,128)(2,1)S(1)} %bitcast.9), channel_id=1, source_target_pairs={{0,2},{2,0},{1,3},{3,1},{4,6},{6,4},{5,7},{7,5},{8,10},{10,8},{9,1... | collective-permute-start | bytes 49160 | tf_op jit(solution)/shard_map/ppermute | solution.py:492
  18.5 2.5 %collective-permute-start.15 = (bf16[136,1024]{1,0:T(8,128)(2,1)S(1)}, bf16[136,1024]{1,0:T(8,128)(2,1)S(1)}, u32[]{:S(2)}, u32[]{:S(2)}) collective-permute-start(bf16[136,1024]{1,0:T(8,128)(2,1)S(1)} %get-tuple-element.76.refs_9_), channel_id=1, source_target_pairs={{0,1},{1,0},{2,3},{3,2},{4,5},{5,4},{6,7},{7,6},{8,9},{9,8},{10,11... | collective-permute-start | bytes 835592 | tf_op jit(solution)/shard_map/ppermute | solution.py:556
  19.8 4.0 %collective-permute-start.5 = (bf16[136,1024]{1,0:T(8,128)(2,1)S(1)}, bf16[136,1024]{1,0:T(8,128)(2,1)S(1)}, u32[]{:S(2)}, u32[]{:S(2)}) collective-permute-start(bf16[136,1024]{1,0:T(8,128)(2,1)S(1)} %get-tuple-element.58.refs_9_), channel_id=1, source_target_pairs={{0,1},{1,0},{2,3},{3,2},{4,5},{5,4},{6,7},{7,6},{8,9},{9,8},{10,11... | collective-permute-start | bytes 835592 | tf_op jit(solution)/shard_map/ppermute | solution.py:556
  23.4 5.0 %collective-permute-start.14 = (bf16[136,1024]{1,0:T(8,128)(2,1)S(1)}, bf16[136,1024]{1,0:T(8,128)(2,1)S(1)}, u32[]{:S(2)}, u32[]{:S(2)}) collective-permute-start(bf16[136,1024]{1,0:T(8,128)(2,1)S(1)} %get-tuple-element.81), channel_id=1, source_target_pairs={{0,1},{1,0},{2,3},{3,2},{4,5},{5,4},{6,7},{7,6},{8,9},{9,8},{10,11... | collective-permute-start | bytes 835592 | tf_op jit(solution)/shard_map/ppermute | solution.py:570
  26.2 4.5 %collective-permute-start.4 = (bf16[136,1024]{1,0:T(8,128)(2,1)S(1)}, bf16[136,1024]{1,0:T(8,128)(2,1)S(1)}, u32[]{:S(2)}, u32[]{:S(2)}) collective-permute-start(bf16[136,1024]{1,0:T(8,128)(2,1)S(1)} %get-tuple-element.64), channel_id=1, source_target_pairs={{0,1},{1,0},{2,3},{3,2},{4,5},{5,4},{6,7},{7,6},{8,9},{9,8},{10,11... | collective-permute-start | bytes 835592 | tf_op jit(solution)/shard_map/ppermute | solution.py:570
  26.4 2.8 %collective-permute-start.17 = (bf16[128,512]{1,0:T(8,128)(2,1)S(1)}, bf16[128,512]{1,0:T(8,128)(2,1)S(1)}, u32[]{:S(2)}, u32[]{:S(2)}) collective-permute-start(bf16[128,512]{1,0:T(8,128)(2,1)S(1)} %get-tuple-element.83), channel_id=1, source_target_pairs={{0,4},{1,5},{2,6},{3,7},{16,20},{17,21},{18,22},{19,23}} | collective-permute-start | bytes 393224 | tf_op jit(solution)/shard_map/ppermute | solution.py:578
  27.0 2.9 %collective-permute-start.16 = (bf16[128,512]{1,0:T(8,128)(2,1)S(1)}, bf16[128,512]{1,0:T(8,128)(2,1)S(1)}, u32[]{:S(2)}, u32[]{:S(2)}) collective-permute-start(bf16[128,512]{1,0:T(8,128)(2,1)S(1)} %get-tuple-element.82), channel_id=1, source_target_pairs={{0,4},{1,5},{2,6},{3,7},{16,20},{17,21},{18,22},{19,23}} | collective-permute-start | bytes 393224 | tf_op jit(solution)/shard_map/ppermute | solution.py:578
  27.7 3.0 %collective-permute-start.7 = (bf16[128,512]{1,0:T(8,128)(2,1)S(1)}, bf16[128,512]{1,0:T(8,128)(2,1)S(1)}, u32[]{:S(2)}, u32[]{:S(2)}) collective-permute-start(bf16[128,512]{1,0:T(8,128)(2,1)S(1)} %get-tuple-element.66), channel_id=1, source_target_pairs={{0,4},{1,5},{2,6},{3,7},{16,20},{17,21},{18,22},{19,23}} | collective-permute-start | bytes 393224 | tf_op jit(solution)/shard_map/ppermute | solution.py:578
  28.4 3.1 %collective-permute-start.6 = (bf16[128,512]{1,0:T(8,128)(2,1)S(1)}, bf16[128,512]{1,0:T(8,128)(2,1)S(1)}, u32[]{:S(2)}, u32[]{:S(2)}) collective-permute-start(bf16[128,512]{1,0:T(8,128)(2,1)S(1)} %get-tuple-element.65), channel_id=1, source_target_pairs={{0,4},{1,5},{2,6},{3,7},{16,20},{17,21},{18,22},{19,23}} | collective-permute-start | bytes 393224 | tf_op jit(solution)/shard_map/ppermute | solution.py:578
  29.2 3.0 %collective-permute-start.19 = (bf16[128,512]{1,0:T(8,128)(2,1)S(1)}, bf16[128,512]{1,0:T(8,128)(2,1)S(1)}, u32[]{:S(2)}, u32[]{:S(2)}) collective-permute-start(bf16[128,512]{1,0:T(8,128)(2,1)S(1)} %shard_map.129), channel_id=1, source_target_pairs={{4,8},{5,9},{6,10},{7,11},{20,24},{21,25},{22,26},{23,27}} | collective-permute-start | bytes 393224 | tf_op jit(solution)/shard_map/ppermute | solution.py:578
  30.0 3.6 %collective-permute-start.18 = (bf16[128,512]{1,0:T(8,128)(2,1)S(1)}, bf16[128,512]{1,0:T(8,128)(2,1)S(1)}, u32[]{:S(2)}, u32[]{:S(2)}) collective-permute-start(bf16[128,512]{1,0:T(8,128)(2,1)S(1)} %shard_map.128), channel_id=1, source_target_pairs={{4,8},{5,9},{6,10},{7,11},{20,24},{21,25},{22,26},{23,27}} | collective-permute-start | bytes 393224 | tf_op jit(solution)/shard_map/ppermute | solution.py:578
  30.8 4.1 %collective-permute-start.9 = (bf16[128,512]{1,0:T(8,128)(2,1)S(1)}, bf16[128,512]{1,0:T(8,128)(2,1)S(1)}, u32[]{:S(2)}, u32[]{:S(2)}) collective-permute-start(bf16[128,512]{1,0:T(8,128)(2,1)S(1)} %shard_map.118), channel_id=1, source_target_pairs={{4,8},{5,9},{6,10},{7,11},{20,24},{21,25},{22,26},{23,27}} | collective-permute-start | bytes 393224 | tf_op jit(solution)/shard_map/ppermute | solution.py:578
  31.6 4.8 %collective-permute-start.8 = (bf16[128,512]{1,0:T(8,128)(2,1)S(1)}, bf16[128,512]{1,0:T(8,128)(2,1)S(1)}, u32[]{:S(2)}, u32[]{:S(2)}) collective-permute-start(bf16[128,512]{1,0:T(8,128)(2,1)S(1)} %shard_map.117), channel_id=1, source_target_pairs={{4,8},{5,9},{6,10},{7,11},{20,24},{21,25},{22,26},{23,27}} | collective-permute-start | bytes 393224 | tf_op jit(solution)/shard_map/ppermute | solution.py:578
  32.3 8.3 %collective-permute-start.21 = (bf16[128,512]{1,0:T(8,128)(2,1)S(1)}, bf16[128,512]{1,0:T(8,128)(2,1)S(1)}, u32[]{:S(2)}, u32[]{:S(2)}) collective-permute-start(bf16[128,512]{1,0:T(8,128)(2,1)S(1)} %shard_map.131), channel_id=1, source_target_pairs={{8,12},{9,13},{10,14},{11,15},{24,28},{25,29},{26,30},{27,31}} | collective-permute-start | bytes 393224 | tf_op jit(solution)/shard_map/ppermute | solution.py:578
  33.7 12.0 %collective-permute-start.20 = (bf16[128,512]{1,0:T(8,128)(2,1)S(1)}, bf16[128,512]{1,0:T(8,128)(2,1)S(1)}, u32[]{:S(2)}, u32[]{:S(2)}) collective-permute-start(bf16[128,512]{1,0:T(8,128)(2,1)S(1)} %shard_map.130), channel_id=1, source_target_pairs={{8,12},{9,13},{10,14},{11,15},{24,28},{25,29},{26,30},{27,31}} | collective-permute-start | bytes 393224 | tf_op jit(solution)/shard_map/ppermute | solution.py:578
  35.0 14.6 %collective-permute-start.11 = (bf16[128,512]{1,0:T(8,128)(2,1)S(1)}, bf16[128,512]{1,0:T(8,128)(2,1)S(1)}, u32[]{:S(2)}, u32[]{:S(2)}) collective-permute-start(bf16[128,512]{1,0:T(8,128)(2,1)S(1)} %shard_map.120), channel_id=1, source_target_pairs={{8,12},{9,13},{10,14},{11,15},{24,28},{25,29},{26,30},{27,31}} | collective-permute-start | bytes 393224 | tf_op jit(solution)/shard_map/ppermute | solution.py:578
  36.4 16.1 %collective-permute-start.10 = (bf16[128,512]{1,0:T(8,128)(2,1)S(1)}, bf16[128,512]{1,0:T(8,128)(2,1)S(1)}, u32[]{:S(2)}, u32[]{:S(2)}) collective-permute-start(bf16[128,512]{1,0:T(8,128)(2,1)S(1)} %shard_map.119), channel_id=1, source_target_pairs={{8,12},{9,13},{10,14},{11,15},{24,28},{25,29},{26,30},{27,31}} | collective-permute-start | bytes 393224 | tf_op jit(solution)/shard_map/ppermute | solution.py:578
  46.0 9.8 %collective-permute-start.22 = (bf16[128,1024]{1,0:T(8,128)(2,1)S(1)}, bf16[128,1024]{1,0:T(8,128)(2,1)S(1)}, u32[]{:S(2)}, u32[]{:S(2)}) collective-permute-start(bf16[128,1024]{1,0:T(8,128)(2,1)S(1)} %get-tuple-element.88), channel_id=1, source_target_pairs={{0,1},{1,0},{2,3},{3,2},{4,5},{5,4},{6,7},{7,6},{8,9},{9,8},{10,11... | collective-permute-start | bytes 786440 | tf_op jit(solution)/shard_map/ppermute | solution.py:589
  52.6 5.0 %collective-permute-start.12 = (bf16[128,1024]{1,0:T(8,128)(2,1)S(1)}, bf16[128,1024]{1,0:T(8,128)(2,1)S(1)}, u32[]{:S(2)}, u32[]{:S(2)}) collective-permute-start(bf16[128,1024]{1,0:T(8,128)(2,1)S(1)} %get-tuple-element.71), channel_id=1, source_target_pairs={{0,1},{1,0},{2,3},{3,2},{4,5},{5,4},{6,7},{7,6},{8,9},{9,8},{10,11... | collective-permute-start | bytes 786440 | tf_op jit(solution)/shard_map/ppermute | solution.py:589

commit v3 on v2

--- a/solution.py
+++ b/solution.py
@@ -164,7 +164,7 @@
     put_decay(send_ref, full_d[EDGE - 1 :, other])
 
 
-def intra_kernel(first_head, head_dim, groups, xc_ref, bcc_ref, tok, heads_ref, by_head, y_ref):
+def intra_kernel(first_head, head_dim, groups, xc_ref, bcc_ref, tok, heads_ref, by_head, y_ref, wide_ref):
     span, width = xc_ref.shape
     per_strip = LANES // head_dim
     lane = lane_index(span)
@@ -199,44 +199,53 @@
             )
             head = first_head + j * per_strip
             skip = widen_pair(by_head[2:3, :], head, head_dim, lane_index(1))
-            y_ref[:, lanes] = (y + skip * wide).astype(y_ref.dtype)
-
-
-def finish_kernel(first, gain_row, head_dim, groups, y_ref, bcc_ref, tok, mine, other, rows_ref, *refs):
-    out_ref, carried, scratch, normed, sems = refs[-5:]
+            y_ref[:, lanes] = y + skip * wide
+            wide_ref[:, lanes] = widen_pair(tok[2], head, head_dim, lane)
+
+
+def finish_kernel(side, first, gain_row, groups, y_ref, wide_ref, bcc_ref, rows_ref, *refs):
+    states, (scratch, normed, sems) = refs[: 2 if side == "both" else 1], refs[-3:]
+    out_ref = refs[-5] if side == "both" else refs[-4]
     span, width = y_ref.shape
-    start = first * (width // groups)
-    first_head = start // head_dim
-    gain = rows_ref[gain_row : gain_row + 1, start : start + width]
-    copies = []
+    group_width = width // groups
     half = width // 2
     sub = lax.axis_index("sub")
-    carried[:, pl.ds(pl.multiple_of(sub * half, LANES), half)] = mine[...]
-    carried[:, pl.ds(pl.multiple_of((1 - sub) * half, LANES), half)] = other[...]
-    lane = lane_index(span)
-    group_width = width // groups
-    decay = tok[2]
-    for g in range(groups):
-        c_out = bcc_ref[:, g * 2 * STATE + STATE : (g + 1) * 2 * STATE]
+    if side == "both":
+        carried, base, count = refs[-4], 0, groups
+        carried[:, pl.ds(pl.multiple_of(sub * half, LANES), half)] = states[0][...]
+        carried[:, pl.ds(pl.multiple_of((1 - sub) * half, LANES), half)] = states[1][...]
+    else:
+        carried, count = states[0], groups // 2
+        base = (sub if side == "mine" else 1 - sub) * count
+
+    def at(offset, size):
+        return pl.ds(pl.multiple_of(offset, LANES), size)
+
+    copies = []
+    for g in range(count):
+        group = base + g
+        c_out = bcc_ref[:, at(group * 2 * STATE + STATE, STATE)]
         lanes = slice(g * group_width, (g + 1) * group_width)
         scratch[...] = jnp.dot(c_out, carried[:, lanes], preferred_element_type=F32)
         squares = jnp.zeros((span, LANES), F32)
         for j in range(group_width // LANES):
             here = slice(j * LANES, (j + 1) * LANES)
-            there = slice(g * group_width + j * LANES, g * group_width + (j + 1) * LANES)
-            head = first_head + (g * group_width + j * LANES) // head_dim
-            y = y_ref[:, there].astype(F32) + scratch[:, here] * widen_pair(decay, head, head_dim, lane)
+            there = at(group * group_width + j * LANES, LANES)
+            y = y_ref[:, there] + scratch[:, here] * wide_ref[:, there]
             scratch[:, here] = y
             squares = squares + y * y
         mean = jnp.sum(squares, axis=1, keepdims=True) * (1.0 / group_width)
         factor = lax.rsqrt(mean + NORM_EPSILON)
+        target = (first + group) * group_width
         for j in range(group_width // LANES):
             here = slice(j * LANES, (j + 1) * LANES)
-            there = slice(g * group_width + j * LANES, g * group_width + (j + 1) * LANES)
-            normed[:, there] = (scratch[:, here] * factor * gain[:, there]).astype(BF16)
-        target = slice(start + g * group_width, start + (g + 1) * group_width)
+            gain = rows_ref[gain_row : gain_row + 1, at(target + j * LANES, LANES)]
+            inside = slice(g * group_width + j * LANES, g * group_width + (j + 1) * LANES)
+            normed[:, inside] = (scratch[:, here] * factor * gain).astype(BF16)
         copies.append(
-            pltpu.make_async_copy(normed.at[:, lanes], out_ref.at[0, :, target], sems.at[g])
+            pltpu.make_async_copy(
+                normed.at[:, lanes], out_ref.at[0, :, at(target, group_width)], sems.at[g]
+            )
         )
         copies[-1].start()
     for copy in copies:
@@ -594,25 +603,26 @@
                 intra_kernel, firsts[c] * group_width // head_dim, head_dim, counts[c]
             ),
             (xc, bcc, tok, by_head, heads_table),
-            [pltpu.VMEM((SPAN, counts[c] * group_width), F32)],
-        )[0]
-
-    def finish(c, y, bcc, mine, theirs, out):
+            [pltpu.VMEM((SPAN, counts[c] * group_width), F32)] * 2,
+        )
+
+    def finish(c, side, y, wide, bcc, states, out):
         before = [] if out is None else [out]
-        cw = counts[c] * group_width
+        count = counts[c] if side == "both" else counts[c] // 2
+        held = [pltpu.VMEM((STATE, counts[c] * group_width), BF16)] if side == "both" else []
         return call(
-            functools.partial(finish_kernel, firsts[c], taps + 1, head_dim, counts[c]),
-            (y, bcc, tok, mine, theirs, rows_table, *before),
+            functools.partial(finish_kernel, side, firsts[c], taps + 1, counts[c]),
+            (y, wide, bcc, rows_table, *states, *before),
             [jax.ShapeDtypeStruct((1, SPAN, width), BF16)],
-            [
-                pltpu.VMEM((STATE, cw), BF16),
+            held
+            + [
                 pltpu.VMEM((SPAN, group_width), F32),
-                pltpu.VMEM((SPAN, cw), BF16),
-                pltpu.SemaphoreType.DMA((counts[c],)),
+                pltpu.VMEM((SPAN, count * group_width), BF16),
+                pltpu.SemaphoreType.DMA((count,)),
             ],
-            specs=[vmem] * 6 + [anywhere] * len(before),
+            specs=[vmem] * (4 + len(states)) + [anywhere] * len(before),
             out_specs=[anywhere],
-            aliases={6: 0} if before else {},
+            aliases={4 + len(states): 0} if before else {},
         )[0]
 
     parts = []
@@ -620,10 +630,15 @@
         first_totals, results = lead(c)
         xc, bcc, own, own_d, send = results
         mine, theirs = carry(c, own, own_d, send, first_totals)
-        parts.append((intra(c, xc, bcc), bcc, mine, theirs))
+        parts.append(((*intra(c, xc, bcc), bcc), mine, theirs))
     out = None
     for c in range(chunks):
-        out = finish(c, *parts[c], out)
+        local, mine, theirs = parts[c]
+        if counts[c] % 2 == 0:
+            out = finish(c, "mine", *local, (mine,), out)
+            out = finish(c, "other", *local, (theirs,), out)
+        else:
+            out = finish(c, "both", *local, (mine, theirs), out)
     return out
 
 

time: 59.9 us -> 61.7 us (1.030)
  Pallas kernels: 14.7 us -> 16.6 us
    pallas_call x26 -> x28, Pallas kernels: 14.7 us -> 16.6 us  [call(): pl.pallas_call(kernel, in_specs=specs or [vmem] * len(operands), out_spec...]
  transfers between devices with their start and end apart: 23 -> 23, of which waited for: 6 -> 6; matrix products, arithmetic and copies ran while one was open for 0% -> 0% of each run, Pallas kernels for 20% -> 24%
where the time goes in v3:
time: 61.7 us; the launch traced here: 61.3 us
  waiting for transfers between devices  22.1 us (36%)
  starting transfers between devices  21.5 us (35%)
  Pallas kernels  16.6 us (27%)
  local copies, waits for them, and re-layouts  0.68 us (1%)
    pallas_call x28, Pallas kernels, call(): pl.pallas_call(kernel, in_specs=specs or [vmem] * len(operands), out_spec...  16.6 us
    ppermute x12, waiting for transfers between devices, carry(): arrived.append(lax.ppermute(held[n], 'seq', [(hop, hop + 1)]))  10.9 us
    ppermute x12, starting transfers between devices, carry(): arrived.append(lax.ppermute(held[n], 'seq', [(hop, hop + 1)]))  10.5 us
    ppermute x1, waiting for transfers between devices, on_device(): lax.ppermute(dt_raw[0], 'head', shift(k))  9.47 us
    ppermute x2, starting transfers between devices, carry(): return (mine, lax.ppermute(theirs, 'sub', [(0, 1), (1, 0)]))  4.9 us
    ppermute x2, starting transfers between devices, on_device(): lax.ppermute(packed[c * others + k - 1], 'head', shift(k))  1.6 us
    ppermute x2, starting transfers between devices, lead(): got = lax.ppermute(send, 'sub', [(0, 1), (1, 0)])  1.47 us
    ppermute x1, starting transfers between devices, on_device(): lax.ppermute(dt_raw[0], 'head', shift(k))  1.24 us
  transfers between devices with their start and end apart: 23, of which 6 were waited for; matrix products, arithmetic and copies ran while one was open for 0% of the time, Pallas kernels for 24%

profile of v3, /device:TPU:27, one launch (start us, length us, event | category | flops | bytes accessed | tf_op | source)
XLA Modules:
  0.0 61.3 jit_solution(8313975828737416451)
XLA Ops:
  0.0 1.0 %shard_map.122 = bf16[64,2560]{1,0:T(8,128)(2,1)S(1)} custom-call(bf16[1,64,8192]{2,1,0:T(8,128)(2,1)} %x_ref.5, bf16[1,64,2048]{2,1,0:T(8,128)(2,1)} %bc_ref.5), custom_call_target="tpu_custom_call" | custom-call | tf_op jit(solution)/shard_map/pallas_call | solution.py:444
  1.1 0.3 collective-permute-start.13
  1.4 0.6 %copy-done.5 = f32[1024]{0:T(1024)S(1)} copy-done((f32[1024]{0:T(1024)S(1)}, f32[1024]{0:T(1024)}, u32[]{:S(2)}) %copy-start.5) | copy-done | bytes 4120
  2.1 0.0 copy-done.8
  2.1 1.2 %shard_map.109 = (bf16[64,5120]{1,0:T(8,128)(2,1)S(1)}, f32[8,5120]{1,0:T(8,128)S(1)}, f32[8,64]{1,0:T(8,128)S(1)}, bf16[64,2560]{1,0:T(8,128)(2,1)S(1)}) custom-call(bf16[1,64,8192]{2,1,0:T(8,128)(2,1)} %x_ref.5, bf16[1,64,2048]{2,1,0:T(8,128)(2,1)} %bc_ref.5, f32[4,4096]{1,0:T(4,128)S(1)} %copy-done, f32[1,4096]{1,0:T(1,128)S(1)} %bitcast.7, ...), custom_call_target="tpu_custom_call" | custom-call | tf_op jit(solution)/shard_map/pallas_call | solution.py:444
  3.3 1.3 %collective-permute-start = (bf16[64,2560]{1,0:T(8,128)(2,1)S(1)}, bf16[64,2560]{1,0:T(8,128)(2,1)S(1)}, u32[]{:S(2)}, u32[]{:S(2)}) collective-permute-start(bf16[64,2560]{1,0:T(8,128)(2,1)S(1)} %get-tuple-element.52), channel_id=1, source_target_pairs={{0,2},{2,0},{1,3},{3,1},{4,6},{6,4},{5,7},{7,5},{8,10},{10,8},{9,1... | collective-permute-start | bytes 983048 | tf_op jit(solution)/shard_map/ppermute | solution.py:503
  4.6 1.0 %shard_map.110 = (bf16[16,1024]{1,0:T(8,128)(2,1)S(1)}, bf16[16,1024]{1,0:T(8,128)(2,1)S(1)}) custom-call(bf16[1,64,8192]{2,1,0:T(8,128)(2,1)} %x_ref.5, bf16[1,64,2048]{2,1,0:T(8,128)(2,1)} %bc_ref.5), custom_call_target="tpu_custom_call" | custom-call | tf_op jit(solution)/shard_map/pallas_call | solution.py:444
  5.6 1.1 %collective-permute-start.1 = (bf16[16,1024]{1,0:T(8,128)(2,1)S(1)}, bf16[16,1024]{1,0:T(8,128)(2,1)S(1)}, u32[]{:S(2)}, u32[]{:S(2)}) collective-permute-start(bf16[16,1024]{1,0:T(8,128)(2,1)S(1)} %get-tuple-element.53), channel_id=1, source_target_pairs={{0,1},{2,3},{1,4},{3,6},{4,5},{6,7},{5,8},{7,10},{8,9},{10,11},{9,... | collective-permute-start | bytes 98312 | tf_op jit(solution)/shard_map/ppermute | solution.py:529
  6.7 1.2 %collective-permute-start.3 = (bf16[64,128]{1,0:T(8,128)(2,1)S(1)}, bf16[64,128]{1,0:T(8,128)(2,1)S(1)}, u32[]{:S(2)}, u32[]{:S(2)}) collective-permute-start(bf16[64,128]{1,0:T(8,128)(2,1)S(1)} %bitcast.9), channel_id=1, source_target_pairs={{0,2},{2,0},{1,3},{3,1},{4,6},{6,4},{5,7},{7,5},{8,10},{10,8},{9,1... | collective-permute-start | bytes 49160 | tf_op jit(solution)/shard_map/ppermute | solution.py:501
  8.0 9.5 %collective-permute-done.3.refs_0_ = bf16[64,128]{1,0:T(8,128)(2,1)S(1)} collective-permute-done((bf16[64,128]{1,0:T(8,128)(2,1)S(1)}, bf16[64,128]{1,0:T(8,128)(2,1)S(1)}, u32[]{:S(2)}, u32[]{:S(2)}) %collective-permute-start.3) | collective-permute-done | bytes 16416 | tf_op jit(solution)/shard_map/ppermute | solution.py:501
  17.4 0.4 shard_map.111
  17.8 0.6 %collective-permute-done.2.refs_2_ = bf16[16,1024]{1,0:T(8,128)(2,1)S(1)} collective-permute-done((bf16[16,1024]{1,0:T(8,128)(2,1)S(1)}, bf16[16,1024]{1,0:T(8,128)(2,1)S(1)}, u32[]{:S(2)}, u32[]{:S(2)}) %collective-permute-start.2) | collective-permute-done | bytes 32800 | tf_op jit(solution)/shard_map/ppermute | solution.py:529
  18.5 1.4 %collective-permute-start.15 = (bf16[136,1024]{1,0:T(8,128)(2,1)S(1)}, bf16[136,1024]{1,0:T(8,128)(2,1)S(1)}, u32[]{:S(2)}, u32[]{:S(2)}) collective-permute-start(bf16[136,1024]{1,0:T(8,128)(2,1)S(1)} %get-tuple-element.82.refs_9_), channel_id=1, source_target_pairs={{0,1},{1,0},{2,3},{3,2},{4,5},{5,4},{6,7},{7,6},{8,9},{9,8},{10,11... | collective-permute-start | bytes 835592 | tf_op jit(solution)/shard_map/ppermute | solution.py:565
  19.8 0.1 collective-permute-start.5
  19.9 1.1 %collective-permute-done.15.got = bf16[136,1024]{1,0:T(8,128)(2,1)S(1)} collective-permute-done((bf16[136,1024]{1,0:T(8,128)(2,1)S(1)}, bf16[136,1024]{1,0:T(8,128)(2,1)S(1)}, u32[]{:S(2)}, u32[]{:S(2)}) %collective-permute-start.15) | collective-permute-done | bytes 278560 | tf_op jit(solution)/shard_map/ppermute | solution.py:565
  21.0 0.1 shard_map.126
  21.1 2.3 %shard_map.124 = (bf16[128,2048]{1,0:T(8,128)(2,1)S(1)}, bf16[128,512]{1,0:T(8,128)(2,1)S(1)}, f32[128,1024]{1,0:T(8,128)S(1)}, f32[1,1024]{1,0:T(1,128)S(1)}, bf16[136,1024]{1,0:T(8,128)(2,1)S(1)}) custom-call(bf16[64,5120]{1,0:T(8,128)(2,1)S(1)} %get-tuple-element.51.own_columns, ...), custom_call_target="tpu_custom_call", output_to_operand_aliasing={{0}: (6, {}), {1}: (7, {}), {2}: (8, {}), {3}: (9, {}), {4}... | custom-call | tf_op jit(solution)/shard_map/pallas_call | solution.py:444
  23.4 0.4 collective-permute-start.14
  23.8 0.1 shard_map.115
  23.9 2.3 %shard_map.113 = (bf16[128,2048]{1,0:T(8,128)(2,1)S(1)}, bf16[128,512]{1,0:T(8,128)(2,1)S(1)}, f32[128,1024]{1,0:T(8,128)S(1)}, f32[1,1024]{1,0:T(1,128)S(1)}, bf16[136,1024]{1,0:T(8,128)(2,1)S(1)}) custom-call(bf16[64,5120]{1,0:T(8,128)(2,1)S(1)} %get-tuple-element.51.own_columns, ...), custom_call_target="tpu_custom_call", output_to_operand_aliasing={{0}: (6, {}), {1}: (7, {}), {2}: (8, {}), {3}: (9, {}), {4}... | custom-call | tf_op jit(solution)/shard_map/pallas_call | solution.py:444
  26.2 0.2 collective-permute-start.4
  26.4 0.7 %collective-permute-start.17 = (bf16[128,512]{1,0:T(8,128)(2,1)S(1)}, bf16[128,512]{1,0:T(8,128)(2,1)S(1)}, u32[]{:S(2)}, u32[]{:S(2)}) collective-permute-start(bf16[128,512]{1,0:T(8,128)(2,1)S(1)} %get-tuple-element.91), channel_id=1, source_target_pairs={{0,4},{1,5},{2,6},{3,7},{16,20},{17,21},{18,22},{19,23}} | collective-permute-start | bytes 393224 | tf_op jit(solution)/shard_map/ppermute | solution.py:587
  27.0 0.7 %collective-permute-start.16 = (bf16[128,512]{1,0:T(8,128)(2,1)S(1)}, bf16[128,512]{1,0:T(8,128)(2,1)S(1)}, u32[]{:S(2)}, u32[]{:S(2)}) collective-permute-start(bf16[128,512]{1,0:T(8,128)(2,1)S(1)} %get-tuple-element.90), channel_id=1, source_target_pairs={{0,4},{1,5},{2,6},{3,7},{16,20},{17,21},{18,22},{19,23}} | collective-permute-start | bytes 393224 | tf_op jit(solution)/shard_map/ppermute | solution.py:587
  27.7 0.7 %collective-permute-start.7 = (bf16[128,512]{1,0:T(8,128)(2,1)S(1)}, bf16[128,512]{1,0:T(8,128)(2,1)S(1)}, u32[]{:S(2)}, u32[]{:S(2)}) collective-permute-start(bf16[128,512]{1,0:T(8,128)(2,1)S(1)} %get-tuple-element.72), channel_id=1, source_target_pairs={{0,4},{1,5},{2,6},{3,7},{16,20},{17,21},{18,22},{19,23}} | collective-permute-start | bytes 393224 | tf_op jit(solution)/shard_map/ppermute | solution.py:587
  28.4 0.7 %collective-permute-start.6 = (bf16[128,512]{1,0:T(8,128)(2,1)S(1)}, bf16[128,512]{1,0:T(8,128)(2,1)S(1)}, u32[]{:S(2)}, u32[]{:S(2)}) collective-permute-start(bf16[128,512]{1,0:T(8,128)(2,1)S(1)} %get-tuple-element.71), channel_id=1, source_target_pairs={{0,4},{1,5},{2,6},{3,7},{16,20},{17,21},{18,22},{19,23}} | collective-permute-start | bytes 393224 | tf_op jit(solution)/shard_map/ppermute | solution.py:587
  29.1 0.1 shard_map.127
  29.2 0.7 %collective-permute-start.19 = (bf16[128,512]{1,0:T(8,128)(2,1)S(1)}, bf16[128,512]{1,0:T(8,128)(2,1)S(1)}, u32[]{:S(2)}, u32[]{:S(2)}) collective-permute-start(bf16[128,512]{1,0:T(8,128)(2,1)S(1)} %shard_map.129), channel_id=1, source_target_pairs={{4,8},{5,9},{6,10},{7,11},{20,24},{21,25},{22,26},{23,27}} | collective-permute-start | bytes 393224 | tf_op jit(solution)/shard_map/ppermute | solution.py:587
  30.0 0.7 %collective-permute-start.18 = (bf16[128,512]{1,0:T(8,128)(2,1)S(1)}, bf16[128,512]{1,0:T(8,128)(2,1)S(1)}, u32[]{:S(2)}, u32[]{:S(2)}) collective-permute-start(bf16[128,512]{1,0:T(8,128)(2,1)S(1)} %shard_map.128), channel_id=1, source_target_pairs={{4,8},{5,9},{6,10},{7,11},{20,24},{21,25},{22,26},{23,27}} | collective-permute-start | bytes 393224 | tf_op jit(solution)/shard_map/ppermute | solution.py:587
  30.7 0.1 shard_map.116
  30.8 0.7 %collective-permute-start.9 = (bf16[128,512]{1,0:T(8,128)(2,1)S(1)}, bf16[128,512]{1,0:T(8,128)(2,1)S(1)}, u32[]{:S(2)}, u32[]{:S(2)}) collective-permute-start(bf16[128,512]{1,0:T(8,128)(2,1)S(1)} %shard_map.118), channel_id=1, source_target_pairs={{4,8},{5,9},{6,10},{7,11},{20,24},{21,25},{22,26},{23,27}} | collective-permute-start | bytes 393224 | tf_op jit(solution)/shard_map/ppermute | solution.py:587
  31.6 0.7 %collective-permute-start.8 = (bf16[128,512]{1,0:T(8,128)(2,1)S(1)}, bf16[128,512]{1,0:T(8,128)(2,1)S(1)}, u32[]{:S(2)}, u32[]{:S(2)}) collective-permute-start(bf16[128,512]{1,0:T(8,128)(2,1)S(1)} %shard_map.117), channel_id=1, source_target_pairs={{4,8},{5,9},{6,10},{7,11},{20,24},{21,25},{22,26},{23,27}} | collective-permute-start | bytes 393224 | tf_op jit(solution)/shard_map/ppermute | solution.py:587
  32.3 1.3 %collective-permute-start.21 = (bf16[128,512]{1,0:T(8,128)(2,1)S(1)}, bf16[128,512]{1,0:T(8,128)(2,1)S(1)}, u32[]{:S(2)}, u32[]{:S(2)}) collective-permute-start(bf16[128,512]{1,0:T(8,128)(2,1)S(1)} %shard_map.131), channel_id=1, source_target_pairs={{8,12},{9,13},{10,14},{11,15},{24,28},{25,29},{26,30},{27,31}} | collective-permute-start | bytes 393224 | tf_op jit(solution)/shard_map/ppermute | solution.py:587
  33.7 1.3 %collective-permute-start.20 = (bf16[128,512]{1,0:T(8,128)(2,1)S(1)}, bf16[128,512]{1,0:T(8,128)(2,1)S(1)}, u32[]{:S(2)}, u32[]{:S(2)}) collective-permute-start(bf16[128,512]{1,0:T(8,128)(2,1)S(1)} %shard_map.130), channel_id=1, source_target_pairs={{8,12},{9,13},{10,14},{11,15},{24,28},{25,29},{26,30},{27,31}} | collective-permute-start | bytes 393224 | tf_op jit(solution)/shard_map/ppermute | solution.py:587
  35.0 1.3 %collective-permute-start.11 = (bf16[128,512]{1,0:T(8,128)(2,1)S(1)}, bf16[128,512]{1,0:T(8,128)(2,1)S(1)}, u32[]{:S(2)}, u32[]{:S(2)}) collective-permute-start(bf16[128,512]{1,0:T(8,128)(2,1)S(1)} %shard_map.120), channel_id=1, source_target_pairs={{8,12},{9,13},{10,14},{11,15},{24,28},{25,29},{26,30},{27,31}} | collective-permute-start | bytes 393224 | tf_op jit(solution)/shard_map/ppermute | solution.py:587
  36.4 1.3 %collective-permute-start.10 = (bf16[128,512]{1,0:T(8,128)(2,1)S(1)}, bf16[128,512]{1,0:T(8,128)(2,1)S(1)}, u32[]{:S(2)}, u32[]{:S(2)}) collective-permute-start(bf16[128,512]{1,0:T(8,128)(2,1)S(1)} %shard_map.119), channel_id=1, source_target_pairs={{8,12},{9,13},{10,14},{11,15},{24,28},{25,29},{26,30},{27,31}} | collective-permute-start | bytes 393224 | tf_op jit(solution)/shard_map/ppermute | solution.py:587
  37.7 2.9 %collective-permute-done.21.refs_5_ = bf16[128,512]{1,0:T(8,128)(2,1)S(1)} collective-permute-done((bf16[128,512]{1,0:T(8,128)(2,1)S(1)}, bf16[128,512]{1,0:T(8,128)(2,1)S(1)}, u32[]{:S(2)}, u32[]{:S(2)}) %collective-permute-start.21) | collective-permute-done | bytes 131104 | tf_op jit(solution)/shard_map/ppermute | solution.py:587
  40.6 5.0 %collective-permute-done.20.refs_4_ = bf16[128,512]{1,0:T(8,128)(2,1)S(1)} collective-permute-done((bf16[128,512]{1,0:T(8,128)(2,1)S(1)}, bf16[128,512]{1,0:T(8,128)(2,1)S(1)}, u32[]{:S(2)}, u32[]{:S(2)}) %collective-permute-start.20) | collective-permute-done | bytes 131104 | tf_op jit(solution)/shard_map/ppermute | solution.py:587
  45.7 0.3 shard_map.132
  46.0 3.6 %collective-permute-start.22 = (bf16[128,1024]{1,0:T(8,128)(2,1)S(1)}, bf16[128,1024]{1,0:T(8,128)(2,1)S(1)}, u32[]{:S(2)}, u32[]{:S(2)}) collective-permute-start(bf16[128,1024]{1,0:T(8,128)(2,1)S(1)} %get-tuple-element.95), channel_id=1, source_target_pairs={{0,1},{1,0},{2,3},{3,2},{4,5},{5,4},{6,7},{7,6},{8,9},{9,8},{10,11... | collective-permute-start | bytes 786440 | tf_op jit(solution)/shard_map/ppermute | solution.py:598
  49.6 2.9 %collective-permute-done.10.refs_4_ = bf16[128,512]{1,0:T(8,128)(2,1)S(1)} collective-permute-done((bf16[128,512]{1,0:T(8,128)(2,1)S(1)}, bf16[128,512]{1,0:T(8,128)(2,1)S(1)}, u32[]{:S(2)}, u32[]{:S(2)}) %collective-permute-start.10) | collective-permute-done | bytes 131104 | tf_op jit(solution)/shard_map/ppermute | solution.py:587
  52.4 0.1 shard_map.121
  52.6 1.3 %collective-permute-start.12 = (bf16[128,1024]{1,0:T(8,128)(2,1)S(1)}, bf16[128,1024]{1,0:T(8,128)(2,1)S(1)}, u32[]{:S(2)}, u32[]{:S(2)}) collective-permute-start(bf16[128,1024]{1,0:T(8,128)(2,1)S(1)} %get-tuple-element.76), channel_id=1, source_target_pairs={{0,1},{1,0},{2,3},{3,2},{4,5},{5,4},{6,7},{7,6},{8,9},{9,8},{10,11... | collective-permute-start | bytes 786440 | tf_op jit(solution)/shard_map/ppermute | solution.py:598
  53.9 1.4 %shard_map.125 = (f32[128,2048]{1,0:T(8,128)S(1)}, f32[128,2048]{1,0:T(8,128)S(1)}) custom-call(bf16[128,2048]{1,0:T(8,128)(2,1)S(1)} %get-tuple-element.83.xc_ref, bf16[128,512]{1,0:T(8,128)(2,1)S(1)} %get-tuple-element.84.bcc_ref, f32[3,128,64]{2,1,0:T(8,128)S(1)} %get-tuple-element.57.refs_4_.tok, f32[2,64,128]{2,1,0:T(8,128)S(1)} %get-tuple-element.65.heads_ref, ...), custom_call_target="tpu_custom_call" | custom-call | tf_op jit(solution)/shard_map/pallas_call | solution.py:444
  55.4 1.4 %shard_map.114 = (f32[128,2048]{1,0:T(8,128)S(1)}, f32[128,2048]{1,0:T(8,128)S(1)}) custom-call(bf16[128,2048]{1,0:T(8,128)(2,1)S(1)} %get-tuple-element.63.xc_ref, bf16[128,512]{1,0:T(8,128)(2,1)S(1)} %get-tuple-element.64.bcc_ref, f32[3,128,64]{2,1,0:T(8,128)S(1)} %get-tuple-element.57.refs_4_.tok, f32[2,64,128]{2,1,0:T(8,128)S(1)} %get-tuple-element.65.heads_ref, ...), custom_call_target="tpu_custom_call" | custom-call | tf_op jit(solution)/shard_map/pallas_call | solution.py:444
  56.8 1.1 %shard_map.133.refs_1_ = bf16[1,128,4096]{2,1,0:T(8,128)(2,1)} custom-call(f32[128,2048]{1,0:T(8,128)S(1)} %get-tuple-element.85.y_ref, f32[128,2048]{1,0:T(8,128)S(1)} %get-tuple-element.86.wide_ref, bf16[128,512]{1,0:T(8,128)(2,1)S(1)} %get-tuple-element.84.bcc_ref, f32[8,5120]{1,0:T(8,128)S(1)} %get-tuple-element.55.refs_3_.rows_ref, ...), custom_call_target="tpu_custom_call" | custom-call | tf_op jit(solution)/shard_map/pallas_call | solution.py:444
  57.9 1.1 %shard_map.134.refs_1_ = bf16[1,128,4096]{2,1,0:T(8,128)(2,1)} custom-call(f32[128,2048]{1,0:T(8,128)S(1)} %get-tuple-element.85.y_ref, f32[128,2048]{1,0:T(8,128)S(1)} %get-tuple-element.86.wide_ref, bf16[128,512]{1,0:T(8,128)(2,1)S(1)} %get-tuple-element.84.bcc_ref, ...), custom_call_target="tpu_custom_call", output_to_operand_aliasing={{}: (5, {})} | custom-call | tf_op jit(solution)/shard_map/pallas_call | solution.py:444
  59.0 1.1 %shard_map.135.refs_1_ = bf16[1,128,4096]{2,1,0:T(8,128)(2,1)} custom-call(f32[128,2048]{1,0:T(8,128)S(1)} %get-tuple-element.66.y_ref, f32[128,2048]{1,0:T(8,128)S(1)} %get-tuple-element.67.wide_ref, bf16[128,512]{1,0:T(8,128)(2,1)S(1)} %get-tuple-element.64.bcc_ref, ...), custom_call_target="tpu_custom_call", output_to_operand_aliasing={{}: (5, {})} | custom-call | tf_op jit(solution)/shard_map/pallas_call | solution.py:444
  60.1 1.1 %shard_map.136 = bf16[1,128,4096]{2,1,0:T(8,128)(2,1)} custom-call(f32[128,2048]{1,0:T(8,128)S(1)} %get-tuple-element.66.y_ref, f32[128,2048]{1,0:T(8,128)S(1)} %get-tuple-element.67.wide_ref, bf16[128,512]{1,0:T(8,128)(2,1)S(1)} %get-tuple-element.64.bcc_ref, f32[8,5120]{1,0:T(8,128)S(1)} %get-tuple-element.55.refs_3_.rows_ref, ...), custom_call_target="tpu_custom_call", output_to_operand_aliasing={{}: (5, {})} | custom-call | tf_op jit(solution)/shard_map/pallas_call | solution.py:444
  (44 shorter events, 0.4 us)
Async XLA Ops:
  0.0 1.4 %copy-start = (f32[4,4096]{1,0:T(4,128)S(1)}, f32[4,4096]{1,0:T(4,128)}, u32[]{:S(2)}) copy-start(f32[4,4096]{1,0:T(4,128)} %wx.1) | copy-start | bytes 196612
  0.0 1.4 %copy-start.1 = (f32[4096]{0:T(1024)S(1)}, f32[4096]{0:T(1024)}, u32[]{:S(2)}) copy-start(f32[4096]{0:T(1024)} %param.15) | copy-start | bytes 49156
  0.0 1.4 %copy-start.2 = (f32[4,1024]{1,0:T(4,128)S(1)}, f32[4,1024]{1,0:T(4,128)}, u32[]{:S(2)}) copy-start(f32[4,1024]{1,0:T(4,128)} %wbc.1) | copy-start | bytes 49156
  0.0 1.4 %copy-start.3 = (f32[4096]{0:T(1024)S(1)}, f32[4096]{0:T(1024)}, u32[]{:S(2)}) copy-start(f32[4096]{0:T(1024)} %param.21) | copy-start | bytes 49156
  1.1 17.4 %collective-permute-start.13 = (bf16[64,2560]{1,0:T(8,128)(2,1)S(1)}, bf16[64,2560]{1,0:T(8,128)(2,1)S(1)}, u32[]{:S(2)}, u32[]{:S(2)}) collective-permute-start(bf16[64,2560]{1,0:T(8,128)(2,1)S(1)} %shard_map.122), channel_id=1, source_target_pairs={{0,2},{2,0},{1,3},{3,1},{4,6},{6,4},{5,7},{7,5},{8,10},{10,8},{9,1... | collective-permute-start | bytes 983048 | tf_op jit(solution)/shard_map/ppermute | solution.py:503
  1.4 0.7 %copy-start.5 = (f32[1024]{0:T(1024)S(1)}, f32[1024]{0:T(1024)}, u32[]{:S(2)}) copy-start(f32[1024]{0:T(1024)} %param.17) | copy-start | bytes 12292
  1.4 0.7 %copy-start.6 = (f32[64]{0:T(128)S(1)}, f32[64]{0:T(128)}, u32[]{:S(2)}) copy-start(f32[64]{0:T(128)} %param.18) | copy-start | bytes 772
  1.4 0.7 %copy-start.7 = (f32[64]{0:T(128)S(1)}, f32[64]{0:T(128)}, u32[]{:S(2)}) copy-start(f32[64]{0:T(128)} %param.19) | copy-start | bytes 772
  1.4 0.7 %copy-start.8 = (f32[64]{0:T(128)S(1)}, f32[64]{0:T(128)}, u32[]{:S(2)}) copy-start(f32[64]{0:T(128)} %param.20) | copy-start | bytes 772
  3.3 3.4 %copy-start.4 = (bf16[1,64,128]{2,1,0:T(8,128)(2,1)S(1)}, bf16[1,64,128]{2,1,0:T(8,128)(2,1)}, u32[]{:S(2)}) copy-start(bf16[1,64,128]{2,1,0:T(8,128)(2,1)} %own_ref.1) | copy-start | bytes 49156
  3.3 16.5 %collective-permute-start = (bf16[64,2560]{1,0:T(8,128)(2,1)S(1)}, bf16[64,2560]{1,0:T(8,128)(2,1)S(1)}, u32[]{:S(2)}, u32[]{:S(2)}) collective-permute-start(bf16[64,2560]{1,0:T(8,128)(2,1)S(1)} %get-tuple-element.52), channel_id=1, source_target_pairs={{0,2},{2,0},{1,3},{3,1},{4,6},{6,4},{5,7},{7,5},{8,10},{10,8},{9,1... | collective-permute-start | bytes 983048 | tf_op jit(solution)/shard_map/ppermute | solution.py:503
  5.6 12.2 %collective-permute-start.1 = (bf16[16,1024]{1,0:T(8,128)(2,1)S(1)}, bf16[16,1024]{1,0:T(8,128)(2,1)S(1)}, u32[]{:S(2)}, u32[]{:S(2)}) collective-permute-start(bf16[16,1024]{1,0:T(8,128)(2,1)S(1)} %get-tuple-element.53), channel_id=1, source_target_pairs={{0,1},{2,3},{1,4},{3,6},{4,5},{6,7},{5,8},{7,10},{8,9},{10,11},{9,... | collective-permute-start | bytes 98312 | tf_op jit(solution)/shard_map/ppermute | solution.py:529
  6.7 11.7 %collective-permute-start.2 = (bf16[16,1024]{1,0:T(8,128)(2,1)S(1)}, bf16[16,1024]{1,0:T(8,128)(2,1)S(1)}, u32[]{:S(2)}, u32[]{:S(2)}) collective-permute-start(bf16[16,1024]{1,0:T(8,128)(2,1)S(1)} %get-tuple-element.54), channel_id=1, source_target_pairs={{0,3},{2,1},{1,6},{3,4},{4,7},{6,5},{5,10},{7,8},{8,11},{10,9},{9,... | collective-permute-start | bytes 98312 | tf_op jit(solution)/shard_map/ppermute | solution.py:529
  6.7 10.7 %collective-permute-start.3 = (bf16[64,128]{1,0:T(8,128)(2,1)S(1)}, bf16[64,128]{1,0:T(8,128)(2,1)S(1)}, u32[]{:S(2)}, u32[]{:S(2)}) collective-permute-start(bf16[64,128]{1,0:T(8,128)(2,1)S(1)} %bitcast.9), channel_id=1, source_target_pairs={{0,2},{2,0},{1,3},{3,1},{4,6},{6,4},{5,7},{7,5},{8,10},{10,8},{9,1... | collective-permute-start | bytes 49160 | tf_op jit(solution)/shard_map/ppermute | solution.py:501
  18.5 2.5 %collective-permute-start.15 = (bf16[136,1024]{1,0:T(8,128)(2,1)S(1)}, bf16[136,1024]{1,0:T(8,128)(2,1)S(1)}, u32[]{:S(2)}, u32[]{:S(2)}) collective-permute-start(bf16[136,1024]{1,0:T(8,128)(2,1)S(1)} %get-tuple-element.82.refs_9_), channel_id=1, source_target_pairs={{0,1},{1,0},{2,3},{3,2},{4,5},{5,4},{6,7},{7,6},{8,9},{9,8},{10,11... | collective-permute-start | bytes 835592 | tf_op jit(solution)/shard_map/ppermute | solution.py:565
  19.8 4.0 %collective-permute-start.5 = (bf16[136,1024]{1,0:T(8,128)(2,1)S(1)}, bf16[136,1024]{1,0:T(8,128)(2,1)S(1)}, u32[]{:S(2)}, u32[]{:S(2)}) collective-permute-start(bf16[136,1024]{1,0:T(8,128)(2,1)S(1)} %get-tuple-element.62.refs_9_), channel_id=1, source_target_pairs={{0,1},{1,0},{2,3},{3,2},{4,5},{5,4},{6,7},{7,6},{8,9},{9,8},{10,11... | collective-permute-start | bytes 835592 | tf_op jit(solution)/shard_map/ppermute | solution.py:565
  23.4 5.0 %collective-permute-start.14 = (bf16[136,1024]{1,0:T(8,128)(2,1)S(1)}, bf16[136,1024]{1,0:T(8,128)(2,1)S(1)}, u32[]{:S(2)}, u32[]{:S(2)}) collective-permute-start(bf16[136,1024]{1,0:T(8,128)(2,1)S(1)} %get-tuple-element.89), channel_id=1, source_target_pairs={{0,1},{1,0},{2,3},{3,2},{4,5},{5,4},{6,7},{7,6},{8,9},{9,8},{10,11... | collective-permute-start | bytes 835592 | tf_op jit(solution)/shard_map/ppermute | solution.py:579
  26.2 4.5 %collective-permute-start.4 = (bf16[136,1024]{1,0:T(8,128)(2,1)S(1)}, bf16[136,1024]{1,0:T(8,128)(2,1)S(1)}, u32[]{:S(2)}, u32[]{:S(2)}) collective-permute-start(bf16[136,1024]{1,0:T(8,128)(2,1)S(1)} %get-tuple-element.70), channel_id=1, source_target_pairs={{0,1},{1,0},{2,3},{3,2},{4,5},{5,4},{6,7},{7,6},{8,9},{9,8},{10,11... | collective-permute-start | bytes 835592 | tf_op jit(solution)/shard_map/ppermute | solution.py:579
  26.4 2.8 %collective-permute-start.17 = (bf16[128,512]{1,0:T(8,128)(2,1)S(1)}, bf16[128,512]{1,0:T(8,128)(2,1)S(1)}, u32[]{:S(2)}, u32[]{:S(2)}) collective-permute-start(bf16[128,512]{1,0:T(8,128)(2,1)S(1)} %get-tuple-element.91), channel_id=1, source_target_pairs={{0,4},{1,5},{2,6},{3,7},{16,20},{17,21},{18,22},{19,23}} | collective-permute-start | bytes 393224 | tf_op jit(solution)/shard_map/ppermute | solution.py:587
  27.0 2.9 %collective-permute-start.16 = (bf16[128,512]{1,0:T(8,128)(2,1)S(1)}, bf16[128,512]{1,0:T(8,128)(2,1)S(1)}, u32[]{:S(2)}, u32[]{:S(2)}) collective-permute-start(bf16[128,512]{1,0:T(8,128)(2,1)S(1)} %get-tuple-element.90), channel_id=1, source_target_pairs={{0,4},{1,5},{2,6},{3,7},{16,20},{17,21},{18,22},{19,23}} | collective-permute-start | bytes 393224 | tf_op jit(solution)/shard_map/ppermute | solution.py:587
  27.7 3.0 %collective-permute-start.7 = (bf16[128,512]{1,0:T(8,128)(2,1)S(1)}, bf16[128,512]{1,0:T(8,128)(2,1)S(1)}, u32[]{:S(2)}, u32[]{:S(2)}) collective-permute-start(bf16[128,512]{1,0:T(8,128)(2,1)S(1)} %get-tuple-element.72), channel_id=1, source_target_pairs={{0,4},{1,5},{2,6},{3,7},{16,20},{17,21},{18,22},{19,23}} | collective-permute-start | bytes 393224 | tf_op jit(solution)/shard_map/ppermute | solution.py:587
  28.4 3.1 %collective-permute-start.6 = (bf16[128,512]{1,0:T(8,128)(2,1)S(1)}, bf16[128,512]{1,0:T(8,128)(2,1)S(1)}, u32[]{:S(2)}, u32[]{:S(2)}) collective-permute-start(bf16[128,512]{1,0:T(8,128)(2,1)S(1)} %get-tuple-element.71), channel_id=1, source_target_pairs={{0,4},{1,5},{2,6},{3,7},{16,20},{17,21},{18,22},{19,23}} | collective-permute-start | bytes 393224 | tf_op jit(solution)/shard_map/ppermute | solution.py:587
  29.2 3.0 %collective-permute-start.19 = (bf16[128,512]{1,0:T(8,128)(2,1)S(1)}, bf16[128,512]{1,0:T(8,128)(2,1)S(1)}, u32[]{:S(2)}, u32[]{:S(2)}) collective-permute-start(bf16[128,512]{1,0:T(8,128)(2,1)S(1)} %shard_map.129), channel_id=1, source_target_pairs={{4,8},{5,9},{6,10},{7,11},{20,24},{21,25},{22,26},{23,27}} | collective-permute-start | bytes 393224 | tf_op jit(solution)/shard_map/ppermute | solution.py:587
  30.0 3.6 %collective-permute-start.18 = (bf16[128,512]{1,0:T(8,128)(2,1)S(1)}, bf16[128,512]{1,0:T(8,128)(2,1)S(1)}, u32[]{:S(2)}, u32[]{:S(2)}) collective-permute-start(bf16[128,512]{1,0:T(8,128)(2,1)S(1)} %shard_map.128), channel_id=1, source_target_pairs={{4,8},{5,9},{6,10},{7,11},{20,24},{21,25},{22,26},{23,27}} | collective-permute-start | bytes 393224 | tf_op jit(solution)/shard_map/ppermute | solution.py:587
  30.8 4.1 %collective-permute-start.9 = (bf16[128,512]{1,0:T(8,128)(2,1)S(1)}, bf16[128,512]{1,0:T(8,128)(2,1)S(1)}, u32[]{:S(2)}, u32[]{:S(2)}) collective-permute-start(bf16[128,512]{1,0:T(8,128)(2,1)S(1)} %shard_map.118), channel_id=1, source_target_pairs={{4,8},{5,9},{6,10},{7,11},{20,24},{21,25},{22,26},{23,27}} | collective-permute-start | bytes 393224 | tf_op jit(solution)/shard_map/ppermute | solution.py:587
  31.6 4.8 %collective-permute-start.8 = (bf16[128,512]{1,0:T(8,128)(2,1)S(1)}, bf16[128,512]{1,0:T(8,128)(2,1)S(1)}, u32[]{:S(2)}, u32[]{:S(2)}) collective-permute-start(bf16[128,512]{1,0:T(8,128)(2,1)S(1)} %shard_map.117), channel_id=1, source_target_pairs={{4,8},{5,9},{6,10},{7,11},{20,24},{21,25},{22,26},{23,27}} | collective-permute-start | bytes 393224 | tf_op jit(solution)/shard_map/ppermute | solution.py:587
  32.3 8.3 %collective-permute-start.21 = (bf16[128,512]{1,0:T(8,128)(2,1)S(1)}, bf16[128,512]{1,0:T(8,128)(2,1)S(1)}, u32[]{:S(2)}, u32[]{:S(2)}) collective-permute-start(bf16[128,512]{1,0:T(8,128)(2,1)S(1)} %shard_map.131), channel_id=1, source_target_pairs={{8,12},{9,13},{10,14},{11,15},{24,28},{25,29},{26,30},{27,31}} | collective-permute-start | bytes 393224 | tf_op jit(solution)/shard_map/ppermute | solution.py:587
  33.7 12.0 %collective-permute-start.20 = (bf16[128,512]{1,0:T(8,128)(2,1)S(1)}, bf16[128,512]{1,0:T(8,128)(2,1)S(1)}, u32[]{:S(2)}, u32[]{:S(2)}) collective-permute-start(bf16[128,512]{1,0:T(8,128)(2,1)S(1)} %shard_map.130), channel_id=1, source_target_pairs={{8,12},{9,13},{10,14},{11,15},{24,28},{25,29},{26,30},{27,31}} | collective-permute-start | bytes 393224 | tf_op jit(solution)/shard_map/ppermute | solution.py:587
  35.0 14.6 %collective-permute-start.11 = (bf16[128,512]{1,0:T(8,128)(2,1)S(1)}, bf16[128,512]{1,0:T(8,128)(2,1)S(1)}, u32[]{:S(2)}, u32[]{:S(2)}) collective-permute-start(bf16[128,512]{1,0:T(8,128)(2,1)S(1)} %shard_map.120), channel_id=1, source_target_pairs={{8,12},{9,13},{10,14},{11,15},{24,28},{25,29},{26,30},{27,31}} | collective-permute-start | bytes 393224 | tf_op jit(solution)/shard_map/ppermute | solution.py:587
  36.4 16.1 %collective-permute-start.10 = (bf16[128,512]{1,0:T(8,128)(2,1)S(1)}, bf16[128,512]{1,0:T(8,128)(2,1)S(1)}, u32[]{:S(2)}, u32[]{:S(2)}) collective-permute-start(bf16[128,512]{1,0:T(8,128)(2,1)S(1)} %shard_map.119), channel_id=1, source_target_pairs={{8,12},{9,13},{10,14},{11,15},{24,28},{25,29},{26,30},{27,31}} | collective-permute-start | bytes 393224 | tf_op jit(solution)/shard_map/ppermute | solution.py:587
  46.0 11.9 %collective-permute-start.22 = (bf16[128,1024]{1,0:T(8,128)(2,1)S(1)}, bf16[128,1024]{1,0:T(8,128)(2,1)S(1)}, u32[]{:S(2)}, u32[]{:S(2)}) collective-permute-start(bf16[128,1024]{1,0:T(8,128)(2,1)S(1)} %get-tuple-element.95), channel_id=1, source_target_pairs={{0,1},{1,0},{2,3},{3,2},{4,5},{5,4},{6,7},{7,6},{8,9},{9,8},{10,11... | collective-permute-start | bytes 786440 | tf_op jit(solution)/shard_map/ppermute | solution.py:598
  52.6 7.5 %collective-permute-start.12 = (bf16[128,1024]{1,0:T(8,128)(2,1)S(1)}, bf16[128,1024]{1,0:T(8,128)(2,1)S(1)}, u32[]{:S(2)}, u32[]{:S(2)}) collective-permute-start(bf16[128,1024]{1,0:T(8,128)(2,1)S(1)} %get-tuple-element.76), channel_id=1, source_target_pairs={{0,1},{1,0},{2,3},{3,2},{4,5},{5,4},{6,7},{7,6},{8,9},{9,8},{10,11... | collective-permute-start | bytes 786440 | tf_op jit(solution)/shard_map/ppermute | solution.py:598
